TPU v7x, 32 devices: a whole 2x2x4 slice. The times are simulated.
32 devices in a mesh: batch: 4 (over y, x), seq: 8 (over z, core).
Axes of the slice: x: 2, y: 2, z: 4, core: 2. Of those that a mesh axis runs over, the one named last changes fastest.
Arguments:
- inputs: bfloat16 [2, 4, 1024, 1024], P(None, 'batch', 'seq'), may hold values from -6 to 6
- w_query: bfloat16 [1024, 1024], P('seq'), may hold values from -0.1875 to 0.1875
- w_key: bfloat16 [1024, 1024], P('seq'), may hold values from -0.1875 to 0.1875
- w_value: bfloat16 [1024, 1024], P('seq'), may hold values from -0.1875 to 0.1875
- w_output: bfloat16 [1024, 1024], P('seq'), may hold values from -0.75 to 0.75
- gain_attention: bfloat16 [1024], P('seq'), may hold values from 0.25 to 1.75
- w_gate: bfloat16 [1024, 4096], P('seq'), may hold values from -0.1875 to 0.1875
- w_up: bfloat16 [1024, 4096], P('seq'), may hold values from -0.1875 to 0.1875
- w_down: bfloat16 [4096, 1024], P('seq'), may hold values from -0.1875 to 0.1875
- gain_feed: bfloat16 [1024], P('seq'), may hold values from 0.25 to 1.75
- variate_bias: float32 [2, 16], replicated, may hold values from -1 to 1
- segment_ids: int32 [2, 4, 1024], P(None, 'batch', 'seq'), may hold values from 0 to 1, never falling along the last dimension, each value on 1 to 768 neighbouring positions
- variate_ids: int32 [2, 4, 1024], P(None, 'batch', 'seq'), may hold values from 0 to 3
- positions: int32 [2, 4, 1024], P(None, 'batch', 'seq'), may hold values from 0 to 1023
- grad_output: bfloat16 [2, 4, 1024, 1024], P(None, 'batch', 'seq'), may hold values from -6 to 6
Outputs:
- block_output: bfloat16 [2, 4, 1024, 1024], P(None, 'batch', 'seq')
- grad_inputs: float32 [2, 4, 1024, 1024], P(None, 'batch', 'seq')
- grad_w_query: float32 [1024, 1024], P('seq')
- grad_w_key: float32 [1024, 1024], P('seq')
- grad_w_value: float32 [1024, 1024], P('seq')
- grad_w_output: float32 [1024, 1024], P('seq')
- grad_gain_attention: float32 [1024], P('seq')
- grad_w_gate: float32 [1024, 4096], P('seq')
- grad_w_up: float32 [1024, 4096], P('seq')
- grad_w_down: float32 [4096, 1024], P('seq')
- grad_gain_feed: float32 [1024], P('seq')
- grad_variate_bias: float32 [2, 16], replicated
Inputs may be any that keep to these rules, and one draw needn't show every extreme that they name: `segment_ids`: segment numbers never fall along a sequence; a document has 1 to 768 tokens.
All inputs are finite; a program needn't handle non-finite values.
Results may differ from a plain program's by a relative error of at most 0.038.
Values may be sent and summed in bfloat16 or wider, within the bound.
No kernel may reach another device: no remote copies, remote signals or barrier semaphores. Data moves between devices by JAX's collectives and lax.ppermute only.
A program may use at most 320 MiB of HBM per device.

v0:
```python
import functools
import math

import jax
import jax.numpy as jnp
from jax import lax
from jax.experimental import pallas as pl
from jax.experimental.pallas import tpu as pltpu
from jax.sharding import PartitionSpec as P

D = 1024
H = 16
HD = 64
REACH = 6


EPSILON = 1e-05
SCORE_SCALE = 0.125
MASKED = -1e30


def from_behind(value, axis, by):
    length = lax.axis_size(axis)
    pairs = [(i, i + by) for i in range(length) if 0 <= i + by < length]
    return lax.ppermute(value, axis, pairs)


def step_offset(step):
    distance = step // 2 + 1
    return distance if step % 2 == 0 else -distance


def rotary(values_in, positions_in, turn):
    row_count = values_in.shape[0]
    halfway = HD // 2
    freqs = jnp.exp(jnp.arange(halfway, dtype=jnp.float32) * (-2.0 * math.log(10000.0) / HD))
    angles = positions_in.astype(jnp.float32)[:, None] * freqs[None, :]
    cosine = jnp.cos(angles)[:, None, :]
    sine = turn * jnp.sin(angles)[:, None, :]
    shaped = values_in.reshape(row_count, H, HD)
    first_half = shaped[..., :halfway]
    second_half = shaped[..., halfway:]
    turned = jnp.concatenate(
        [first_half * cosine - second_half * sine, first_half * sine + second_half * cosine], -1
    )
    return turned.reshape(row_count, H * HD)


def head_scores(query_heads, key_heads, query_variates, key_variates, bias_table):
    raw = jnp.einsum("qhd,khd->hqk", query_heads, key_heads, preferred_element_type=jnp.float32)
    same_variate = (query_variates[:, None] == key_variates[None, :])[None]
    return raw * SCORE_SCALE + jnp.where(
        same_variate, bias_table[0][:, None, None], bias_table[1][:, None, None]
    )


def attend_forward(query_rows, own_keys, own_values, own_segments, own_variates, bias_table):
    tok_count = query_rows.shape[0]
    query_heads = query_rows.reshape(tok_count, H, HD)
    shifted_segments = own_segments + 1

    def fold_keys(carried, piece_rows):
        key_part, value_part, segment_part, variate_part = piece_rows
        part_count = key_part.shape[0]
        live = shifted_segments[:, None] == segment_part[None, :]

        def update(state):
            running_max, running_total, running_sum = state
            logits = head_scores(
                query_heads,
                key_part.reshape(part_count, H, HD),
                own_variates,
                variate_part,
                bias_table,
            )
            logits = jnp.where(live[None], logits, MASKED)
            new_max = jnp.maximum(running_max, jnp.max(logits, -1))
            rescale = jnp.exp(running_max - new_max)
            weights = jnp.where(live[None], jnp.exp(logits - new_max[..., None]), 0.0)
            new_total = running_total * rescale + jnp.sum(weights, -1)
            mixed = jnp.einsum(
                "hqk,khd->qhd",
                weights.astype(jnp.bfloat16),
                value_part.reshape(part_count, H, HD),
                preferred_element_type=jnp.float32,
            )
            new_sum = running_sum * jnp.transpose(rescale)[:, :, None] + mixed
            return (new_max, new_total, new_sum)

        return lax.cond(jnp.any(live), update, lambda state: state, carried)

    near_rows = (own_keys, own_values, shifted_segments, own_variates)
    state = (
        jnp.full((H, tok_count), MASKED, jnp.float32),
        jnp.zeros((H, tok_count), jnp.float32),
        jnp.zeros((tok_count, H, HD), jnp.float32),
    )
    state = fold_keys(state, near_rows)
    for step in range(2 * REACH):
        arrived = from_behind(
            (own_keys, own_values, shifted_segments, own_variates), "seq", step_offset(step)
        )
        state = fold_keys(state, arrived)
    final_max, final_total, final_sum = state
    attended = final_sum / jnp.transpose(final_total)[:, :, None]
    log_rows = jnp.transpose(final_max + jnp.log(final_total))
    return (attended.reshape(tok_count, H * HD), log_rows)


def attend_queries_back(
    query_rows,
    grad_rows,
    log_rows,
    delta_rows,
    own_keys,
    own_values,
    own_segments,
    own_variates,
    bias_table,
):
    tok_count = query_rows.shape[0]
    query_heads = query_rows.reshape(tok_count, H, HD)
    grad_heads = grad_rows.reshape(tok_count, H, HD)
    log_heads = jnp.transpose(log_rows)
    delta_heads = jnp.transpose(delta_rows)
    shifted_segments = own_segments + 1

    def fold_keys_back(carried, piece_rows):
        key_part, value_part, segment_part, variate_part = piece_rows
        part_count = key_part.shape[0]
        live = shifted_segments[:, None] == segment_part[None, :]

        def update(state):
            grad_query, grad_bias = state
            key_heads = key_part.reshape(part_count, H, HD)
            logits = head_scores(query_heads, key_heads, own_variates, variate_part, bias_table)
            weights = jnp.where(live[None], jnp.exp(logits - log_heads[..., None]), 0.0)
            grad_weights = jnp.einsum(
                "qhd,khd->hqk",
                grad_heads,
                value_part.reshape(part_count, H, HD),
                preferred_element_type=jnp.float32,
            )
            grad_logits = (weights * (grad_weights - delta_heads[..., None])).astype(jnp.bfloat16)
            grad_query = grad_query + SCORE_SCALE * jnp.einsum(
                "hqk,khd->qhd", grad_logits, key_heads, preferred_element_type=jnp.float32
            )
            same_variate = (own_variates[:, None] == variate_part[None, :])[None]
            logit_values = grad_logits.astype(jnp.float32)
            same_total = jnp.sum(jnp.where(same_variate, logit_values, 0.0), axis=(1, 2))
            other_total = jnp.sum(jnp.where(same_variate, 0.0, logit_values), axis=(1, 2))
            return (grad_query, grad_bias + jnp.stack([same_total, other_total]))

        return lax.cond(jnp.any(live), update, lambda state: state, carried)

    state = (jnp.zeros((tok_count, H, HD), jnp.float32), jnp.zeros((2, H), jnp.float32))
    state = fold_keys_back(state, (own_keys, own_values, shifted_segments, own_variates))
    for step in range(2 * REACH):
        arrived = from_behind(
            (own_keys, own_values, shifted_segments, own_variates), "seq", step_offset(step)
        )
        state = fold_keys_back(state, arrived)
    grad_query, grad_bias = state
    return (grad_query.reshape(tok_count, H * HD), grad_bias)


def attend_keys_back(
    query_rows,
    grad_rows,
    log_rows,
    delta_rows,
    own_keys,
    own_values,
    own_segments,
    own_variates,
    bias_table,
):
    tok_count = own_keys.shape[0]
    key_heads = own_keys.reshape(tok_count, H, HD)
    value_heads = own_values.reshape(tok_count, H, HD)
    shifted_segments = own_segments + 1

    def fold_queries(carried, piece_rows):
        query_part, grad_part, log_part, delta_part, segment_part, variate_part = piece_rows
        part_count = query_part.shape[0]
        live = segment_part[:, None] == shifted_segments[None, :]

        def update(state):
            grad_key, grad_value = state
            query_heads = query_part.reshape(part_count, H, HD)
            grad_heads = grad_part.reshape(part_count, H, HD)
            logits = head_scores(query_heads, key_heads, variate_part, own_variates, bias_table)
            weights = jnp.where(
                live[None], jnp.exp(logits - jnp.transpose(log_part)[..., None]), 0.0
            )
            grad_value = grad_value + jnp.einsum(
                "hqk,qhd->khd",
                weights.astype(jnp.bfloat16),
                grad_heads,
                preferred_element_type=jnp.float32,
            )
            grad_weights = jnp.einsum(
                "qhd,khd->hqk", grad_heads, value_heads, preferred_element_type=jnp.float32
            )
            grad_logits = (weights * (grad_weights - jnp.transpose(delta_part)[..., None])).astype(
                jnp.bfloat16
            )
            grad_key = grad_key + SCORE_SCALE * jnp.einsum(
                "hqk,qhd->khd", grad_logits, query_heads, preferred_element_type=jnp.float32
            )
            return (grad_key, grad_value)

        return lax.cond(jnp.any(live), update, lambda state: state, carried)

    state = (jnp.zeros((tok_count, H, HD), jnp.float32), jnp.zeros((tok_count, H, HD), jnp.float32))
    state = fold_queries(
        state, (query_rows, grad_rows, log_rows, delta_rows, shifted_segments, own_variates)
    )
    for step in range(2 * REACH):
        arrived = (
            from_behind(query_rows, "seq", step_offset(step)),
            from_behind(grad_rows, "seq", step_offset(step)),
            from_behind(log_rows.astype(jnp.bfloat16), "seq", step_offset(step)).astype(
                log_rows.dtype
            ),
            from_behind(delta_rows.astype(jnp.bfloat16), "seq", step_offset(step)).astype(
                delta_rows.dtype
            ),
            from_behind(shifted_segments, "seq", step_offset(step)),
            from_behind(own_variates, "seq", step_offset(step)),
        )
        state = fold_queries(state, arrived)
    grad_key, grad_value = state
    return (grad_key.reshape(tok_count, H * HD), grad_value.reshape(tok_count, H * HD))


def norm_back(grad_normed, normed, scale_rows):
    return scale_rows * (grad_normed - normed * jnp.mean(grad_normed * normed, -1, keepdims=True))


def on_device(
    inputs,
    w_query,
    w_key,
    w_value,
    w_output,
    gain_attention,
    w_gate,
    w_up,
    w_down,
    gain_feed,
    variate_bias,
    segment_ids,
    variate_ids,
    positions,
    grad_output,
):
    micro_count = inputs.shape[0]
    tok_count = inputs.shape[2]
    row_count = micro_count * tok_count
    residual_in = inputs.reshape(row_count, D).astype(jnp.float32)
    cotangent = grad_output.reshape(row_count, D).astype(jnp.float32)
    segment_rows = segment_ids.reshape(micro_count, tok_count)
    variate_rows = variate_ids.reshape(micro_count, tok_count)
    position_rows = positions.reshape(row_count)
    full_query, full_key, full_value, full_output, full_gain_first = (
        lax.all_gather(w_query, "seq", axis=0, tiled=True),
        lax.all_gather(w_key, "seq", axis=0, tiled=True),
        lax.all_gather(w_value, "seq", axis=0, tiled=True),
        lax.all_gather(w_output, "seq", axis=0, tiled=True),
        lax.all_gather(gain_attention, "seq", axis=0, tiled=True),
    )
    full_gate, full_up, full_down, full_gain_second = (
        lax.all_gather(w_gate, "seq", axis=0, tiled=True),
        lax.all_gather(w_up, "seq", axis=0, tiled=True),
        lax.all_gather(w_down, "seq", axis=0, tiled=True),
        lax.all_gather(gain_feed, "seq", axis=0, tiled=True),
    )
    scale_first = lax.rsqrt(jnp.mean(residual_in * residual_in, -1, keepdims=True) + EPSILON)
    normed_first = residual_in * scale_first
    mixed_first = (normed_first * full_gain_first.astype(jnp.float32)).astype(jnp.bfloat16)
    query_proj = jnp.dot(mixed_first, full_query, preferred_element_type=jnp.float32)
    key_proj = jnp.dot(mixed_first, full_key, preferred_element_type=jnp.float32)
    value_proj = jnp.dot(mixed_first, full_value, preferred_element_type=jnp.float32)
    query_rows = rotary(query_proj, position_rows, 1.0).astype(jnp.bfloat16)
    key_rows = rotary(key_proj, position_rows, 1.0).astype(jnp.bfloat16)
    value_rows = value_proj.astype(jnp.bfloat16)
    attended_parts = []
    log_parts = []
    for micro_index in range(micro_count):
        lower_row = micro_index * tok_count
        upper_row = lower_row + tok_count
        attended_part, log_part = attend_forward(
            query_rows[lower_row:upper_row],
            key_rows[lower_row:upper_row],
            value_rows[lower_row:upper_row],
            segment_rows[micro_index],
            variate_rows[micro_index],
            variate_bias,
        )
        attended_parts.append(attended_part)
        log_parts.append(log_part)
    attended_all = jnp.concatenate(attended_parts, 0)
    attended_low = attended_all.astype(jnp.bfloat16)
    middle = residual_in + jnp.dot(attended_low, full_output, preferred_element_type=jnp.float32)
    scale_second = lax.rsqrt(jnp.mean(middle * middle, -1, keepdims=True) + EPSILON)
    normed_second = middle * scale_second
    mixed_second = (normed_second * full_gain_second.astype(jnp.float32)).astype(jnp.bfloat16)
    gate_proj = jnp.dot(mixed_second, full_gate, preferred_element_type=jnp.float32)
    up_proj = jnp.dot(mixed_second, full_up, preferred_element_type=jnp.float32)
    sigmoid_gate = jax.nn.sigmoid(gate_proj)
    silu_gate = gate_proj * sigmoid_gate
    hidden_rows = (silu_gate * up_proj).astype(jnp.bfloat16)
    block_rows = middle + jnp.dot(hidden_rows, full_down, preferred_element_type=jnp.float32)
    block_output = block_rows.astype(jnp.bfloat16).reshape(inputs.shape)
    full_query, full_key, full_value, full_output, full_gain_first = (
        lax.all_gather(w_query, "seq", axis=0, tiled=True),
        lax.all_gather(w_key, "seq", axis=0, tiled=True),
        lax.all_gather(w_value, "seq", axis=0, tiled=True),
        lax.all_gather(w_output, "seq", axis=0, tiled=True),
        lax.all_gather(gain_attention, "seq", axis=0, tiled=True),
    )
    full_gate, full_up, full_down, full_gain_second = (
        lax.all_gather(w_gate, "seq", axis=0, tiled=True),
        lax.all_gather(w_up, "seq", axis=0, tiled=True),
        lax.all_gather(w_down, "seq", axis=0, tiled=True),
        lax.all_gather(gain_feed, "seq", axis=0, tiled=True),
    )
    grad_branch_second = cotangent.astype(jnp.bfloat16)
    grad_down = jnp.einsum(
        "rf,rd->fd", hidden_rows, grad_branch_second, preferred_element_type=jnp.float32
    )
    grad_hidden = jnp.einsum(
        "rd,fd->rf", grad_branch_second, full_down, preferred_element_type=jnp.float32
    )
    silu_slope = sigmoid_gate * (1.0 + gate_proj * (1.0 - sigmoid_gate))
    grad_gate_rows = (grad_hidden * up_proj * silu_slope).astype(jnp.bfloat16)
    grad_up_rows = (grad_hidden * silu_gate).astype(jnp.bfloat16)
    grad_gate = jnp.einsum(
        "rd,rf->df", mixed_second, grad_gate_rows, preferred_element_type=jnp.float32
    )
    grad_up = jnp.einsum(
        "rd,rf->df", mixed_second, grad_up_rows, preferred_element_type=jnp.float32
    )
    grad_mixed_second = jnp.einsum(
        "rf,df->rd", grad_gate_rows, full_gate, preferred_element_type=jnp.float32
    ) + jnp.einsum("rf,df->rd", grad_up_rows, full_up, preferred_element_type=jnp.float32)
    grad_gain_second = jnp.sum(grad_mixed_second * normed_second, 0)
    grad_middle = cotangent + norm_back(
        grad_mixed_second * full_gain_second.astype(jnp.float32), normed_second, scale_second
    )
    grad_branch_first = grad_middle.astype(jnp.bfloat16)
    grad_out_proj = jnp.einsum(
        "rd,re->de", attended_low, grad_branch_first, preferred_element_type=jnp.float32
    )
    grad_attended = jnp.einsum(
        "re,de->rd", grad_branch_first, full_output, preferred_element_type=jnp.float32
    ).astype(jnp.bfloat16)
    delta_all = jnp.einsum(
        "rhd,rhd->rh",
        grad_attended.astype(jnp.float32).reshape(row_count, H, HD),
        attended_all.reshape(row_count, H, HD),
    )
    grad_bias_local = jnp.zeros((2, H), jnp.float32)
    query_grad_parts = []
    key_grad_parts = []
    value_grad_parts = []
    for micro_index in range(micro_count):
        lower_row = micro_index * tok_count
        upper_row = lower_row + tok_count
        query_grad_part, bias_part = attend_queries_back(
            query_rows[lower_row:upper_row],
            grad_attended[lower_row:upper_row],
            log_parts[micro_index],
            delta_all[lower_row:upper_row],
            key_rows[lower_row:upper_row],
            value_rows[lower_row:upper_row],
            segment_rows[micro_index],
            variate_rows[micro_index],
            variate_bias,
        )
        key_grad_part, value_grad_part = attend_keys_back(
            query_rows[lower_row:upper_row],
            grad_attended[lower_row:upper_row],
            log_parts[micro_index],
            delta_all[lower_row:upper_row],
            key_rows[lower_row:upper_row],
            value_rows[lower_row:upper_row],
            segment_rows[micro_index],
            variate_rows[micro_index],
            variate_bias,
        )
        grad_bias_local = grad_bias_local + bias_part
        query_grad_parts.append(query_grad_part)
        key_grad_parts.append(key_grad_part)
        value_grad_parts.append(value_grad_part)
    grad_query_rows = rotary(jnp.concatenate(query_grad_parts, 0), position_rows, -1.0).astype(
        jnp.bfloat16
    )
    grad_key_rows = rotary(jnp.concatenate(key_grad_parts, 0), position_rows, -1.0).astype(
        jnp.bfloat16
    )
    grad_value_rows = jnp.concatenate(value_grad_parts, 0).astype(jnp.bfloat16)
    grad_query = jnp.einsum(
        "rd,re->de", mixed_first, grad_query_rows, preferred_element_type=jnp.float32
    )
    grad_key = jnp.einsum(
        "rd,re->de", mixed_first, grad_key_rows, preferred_element_type=jnp.float32
    )
    grad_value = jnp.einsum(
        "rd,re->de", mixed_first, grad_value_rows, preferred_element_type=jnp.float32
    )
    grad_mixed_first = (
        jnp.einsum("re,de->rd", grad_query_rows, full_query, preferred_element_type=jnp.float32)
        + jnp.einsum("re,de->rd", grad_key_rows, full_key, preferred_element_type=jnp.float32)
        + jnp.einsum("re,de->rd", grad_value_rows, full_value, preferred_element_type=jnp.float32)
    )
    grad_gain_first = jnp.sum(grad_mixed_first * normed_first, 0)
    grad_input_rows = grad_middle + norm_back(
        grad_mixed_first * full_gain_first.astype(jnp.float32), normed_first, scale_first
    )
    grad_inputs = grad_input_rows.reshape(inputs.shape)
    (
        shard_query,
        shard_key,
        shard_value,
        shard_output,
        shard_gain_first,
        shard_gate,
        shard_up,
        shard_down,
        shard_gain_second,
    ) = (
        lax.psum_scatter(grad_query, "seq", scatter_dimension=0, tiled=True),
        lax.psum_scatter(grad_key, "seq", scatter_dimension=0, tiled=True),
        lax.psum_scatter(grad_value, "seq", scatter_dimension=0, tiled=True),
        lax.psum_scatter(grad_out_proj, "seq", scatter_dimension=0, tiled=True),
        lax.psum_scatter(grad_gain_first, "seq", scatter_dimension=0, tiled=True),
        lax.psum_scatter(grad_gate, "seq", scatter_dimension=0, tiled=True),
        lax.psum_scatter(grad_up, "seq", scatter_dimension=0, tiled=True),
        lax.psum_scatter(grad_down, "seq", scatter_dimension=0, tiled=True),
        lax.psum_scatter(grad_gain_second, "seq", scatter_dimension=0, tiled=True),
    )
    summed = (
        lax.psum(shard_query.astype(jnp.bfloat16), "batch").astype(jnp.float32),
        lax.psum(shard_key.astype(jnp.bfloat16), "batch").astype(jnp.float32),
        lax.psum(shard_value.astype(jnp.bfloat16), "batch").astype(jnp.float32),
        lax.psum(shard_output.astype(jnp.bfloat16), "batch").astype(jnp.float32),
        lax.psum(shard_gain_first.astype(jnp.bfloat16), "batch").astype(jnp.float32),
        lax.psum(shard_gate.astype(jnp.bfloat16), "batch").astype(jnp.float32),
        lax.psum(shard_up.astype(jnp.bfloat16), "batch").astype(jnp.float32),
        lax.psum(shard_down.astype(jnp.bfloat16), "batch").astype(jnp.float32),
        lax.psum(shard_gain_second.astype(jnp.bfloat16), "batch").astype(jnp.float32),
    )
    grad_bias_total = lax.psum(grad_bias_local, ("batch", "seq"))
    return (
        block_output,
        grad_inputs,
        summed[0],
        summed[1],
        summed[2],
        summed[3],
        summed[4],
        summed[5],
        summed[6],
        summed[7],
        summed[8],
        grad_bias_total,
    )


ORDER_A = (0, 1, 2, 3)
ORDER_B = (0, 2, 1, 3)
FEATURES = 128
LSE_AT = 64
LOW = jnp.bfloat16
WIDE = jnp.float32


def swap(value, bit):
    return lax.ppermute(value, "batch", [(i, i ^ bit) for i in range(4)])


def after(value, *others):
    return lax.optimization_barrier((value, *others))[0]


def gather_plane(own):
    half = own.shape[0] // 2
    lower, upper = own[:half], own[half:]
    lower_pair = jnp.concatenate([lower, swap(lower, 1)], 0)
    upper_pair = jnp.concatenate([upper, swap(upper, 2)], 0)
    return lower_pair, swap(lower_pair, 2), upper_pair, swap(upper_pair, 1)


def scatter_first(chunks):
    return swap(chunks[1], 2), swap(chunks[3], 1)


def scatter_second(chunks, got):
    near_lower, _, near_upper, _ = chunks
    got_lower, got_upper = got
    half = near_lower.shape[0] // 2
    last_lower = swap(near_lower[half:] + got_lower[half:], 1)
    last_upper = swap(near_upper[half:] + got_upper[half:], 2)
    return (near_lower, got_lower, last_lower, near_upper, got_upper, last_upper)


def swap_pairs(own):
    half = own.shape[0] // 2
    return swap(own[:half], 1), swap(own[half:], 2)


def far_pairs(own, got):
    half = own.shape[0] // 2
    lower_pair = jnp.concatenate([own[:half], got[0]], 0)
    upper_pair = jnp.concatenate([own[half:], got[1]], 0)
    return lower_pair, swap(lower_pair, 2), upper_pair, swap(upper_pair, 1)


def over_seq(pieces):
    count, quarter, width = pieces.shape
    return lax.all_to_all(pieces, "seq", 0, 0, tiled=True).reshape(count * quarter, width)


def three_parts(value):
    high = value.astype(LOW)
    rest = value - high.astype(WIDE)
    middle = rest.astype(LOW)
    low = (rest - middle.astype(WIDE)).astype(LOW)
    return high, middle, low


def token_features(segments, variates):
    lane = lax.broadcasted_iota(jnp.int32, (segments.shape[0], FEATURES), 1)
    variate_hot = (lane < 12) & (lane % 4 == variates)
    ones = (lane >= 12) & (lane < 15)
    segment_lane = (lane >= 16) & (lane < LSE_AT)
    segment_hot = segment_lane & (lane - 16 == segments)
    segment_cold = segment_lane & (lane - 16 != segments)
    query_side = variate_hot | ones | segment_hot
    key_side = variate_hot | ones | segment_cold | ((lane >= LSE_AT) & (lane < LSE_AT + 3))
    return jnp.where(query_side, 1.0, 0.0).astype(LOW), jnp.where(key_side, 1.0, 0.0).astype(LOW)


def head_weights(same_bias, other_bias):
    gap = [part[:, None] for part in three_parts(same_bias - other_bias)]
    base = [part[:, None] for part in three_parts(other_bias)]
    heads = same_bias.shape[0]
    columns = [jnp.broadcast_to(part, (heads, 4)) for part in gap] + base
    columns.append(jnp.zeros((heads, 1), LOW))
    columns.append(jnp.full((heads, LSE_AT - 16), MASKED, LOW))
    columns.append(jnp.zeros((heads, FEATURES - LSE_AT), LOW))
    return jnp.concatenate(columns, 1)


def turn_pair(pair, cosine, sine):
    lane = lax.broadcasted_iota(jnp.int32, pair.shape, 1)
    crossed = jnp.where(lane % 64 < 32, pltpu.roll(pair, 96, 1), pltpu.roll(pair, 32, 1))
    return pair * cosine + crossed * sine


def dot_plain(left, right):
    return jnp.dot(left, right, preferred_element_type=WIDE)


def dot_rows(left, right):
    return lax.dot_general(left, right, (((1,), (1,)), ((), ())), preferred_element_type=WIDE)


def dot_first(left, right):
    return lax.dot_general(left, right, (((0,), (0,)), ((), ())), preferred_element_type=WIDE)


def whole_block():
    return pl.BlockSpec(memory_space=pltpu.VMEM)


def call(kernel, name, outs, specs, flops, moved, args, scratch=()):
    return pl.pallas_call(
        kernel,
        grid=(1,),
        out_shape=[jax.ShapeDtypeStruct(shape, dtype) for shape, dtype in outs],
        in_specs=specs,
        out_specs=[pl.BlockSpec(memory_space=pltpu.VMEM) for _ in outs],
        scratch_shapes=list(scratch),
        cost_estimate=pl.CostEstimate(flops=flops, bytes_accessed=moved, transcendentals=0),
        compiler_params=pltpu.CompilerParams(vmem_limit_bytes=56 * 2**20),
        name=name,
    )(*args)


class Copies:
    def __init__(self, ref, pairs, sems):
        self.ref = ref
        self.copies = [
            pltpu.make_async_copy(source, target, sems.at[k])
            for k, (source, target) in enumerate(pairs)
        ]
        self.started = self.waited = False

    def start(self, *which):
        self.started = True
        for k in which or range(len(self.copies)):
            self.copies[k].start()

    def wait(self):
        if not self.waited:
            for copy in self.copies:
                copy.wait()
        self.waited = True
        return self.ref

    def _at(self, index, act):
        for k, copy in enumerate(self.copies):
            pl.when(index == k)(functools.partial(act, copy))

    def start_at(self, index):
        self.started = True
        self._at(index, lambda copy: copy.start())

    def wait_at(self, index):
        self.waited = True
        self._at(index, lambda copy: copy.wait())

    def wait_first(self, index):
        if not self.waited:
            self.waited = True

            @pl.when(index == 0)
            def _():
                for copy in self.copies:
                    copy.wait()

        return self.ref


class Plan:
    def __init__(self, arrays, shape, pairs, count):
        self.arrays, self.shape, self.pairs, self.count = arrays, shape, pairs, count


def whole(array, column=None, width=None):
    shape = array.shape if column is None else (array.shape[0], width)

    def pairs(refs, buffer):
        if column is None:
            return [(refs[0], buffer)]
        return [(refs[0].at[:, pl.ds(column, width)], buffer)]

    return Plan([array], shape, pairs, 1)


def top(array):
    half = array.shape[0] // 2
    return Plan(
        [array],
        (half, *array.shape[1:]),
        lambda refs, buffer: [(refs[0].at[pl.ds(0, half)], buffer)],
        1,
    )


def rows_of(array, count=4):
    size = array.shape[0] // count
    return Plan(
        [array],
        (count, size, array.shape[1]),
        lambda refs, buffer: [
            (refs[0].at[pl.ds(k * size, size)], buffer.at[k]) for k in range(count)
        ],
        count,
    )


def columns_of(array, count=4, column=0, width=None):
    size = (width or array.shape[1]) // count
    return Plan(
        [array],
        (count, array.shape[0], size),
        lambda refs, buffer: [
            (refs[0].at[:, pl.ds(column + k * size, size)], buffer.at[k]) for k in range(count)
        ],
        count,
    )


def group(arrays, column=None, width=None):
    rows = arrays[0].shape[0]

    def pairs(refs, buffer):
        if column is None:
            return [(ref, buffer.at[k]) for k, ref in enumerate(refs)]
        return [(ref.at[:, pl.ds(column, width)], buffer.at[k]) for k, ref in enumerate(refs)]

    return Plan(
        list(arrays), (len(arrays), rows, width or arrays[0].shape[1]), pairs, len(arrays)
    )


def out_rows(shape, dtype, count=4):
    size = shape[0] // count

    def pairs(refs, buffer):
        return [(buffer.at[k], refs[0].at[pl.ds(k * size, size)]) for k in range(count)]

    return Plan([(shape, dtype)], (count, size, *shape[1:]), pairs, count)


def out_group(shape, dtype, count=4):
    def pairs(refs, buffer):
        return [(buffer.at[k], ref) for k, ref in enumerate(refs)]

    return Plan([(shape, dtype)] * count, (count, *shape), pairs, count)


def out_whole(shape, dtype):
    return Plan([(shape, dtype)], shape, lambda refs, buffer: [(buffer, refs[0])], 1)


def run(body, name, us, ins, outs, scratch=(), token=None):
    args, in_specs, out_shapes, out_specs, buffers = [], [], [], [], []
    named = len(ins)
    if token is not None:
        ins = [*ins, token]
    for item in ins:
        if isinstance(item, Plan):
            args += item.arrays
            in_specs += [pl.BlockSpec(memory_space=pl.ANY)] * len(item.arrays)
            buffers.append(pltpu.VMEM(item.shape, item.arrays[0].dtype))
            buffers.append(pltpu.SemaphoreType.DMA((item.count,)))
        else:
            args.append(item)
            space = pltpu.SMEM if item.shape == (1,) else pltpu.VMEM
            in_specs.append(pl.BlockSpec(memory_space=space))
    for item in outs:
        if isinstance(item, Plan):
            out_shapes += [jax.ShapeDtypeStruct(*each) for each in item.arrays]
            out_specs += [pl.BlockSpec(memory_space=pl.ANY)] * len(item.arrays)
            buffers.append(pltpu.VMEM(item.shape, item.arrays[0][1]))
            buffers.append(pltpu.SemaphoreType.DMA((item.count,)))
        else:
            out_shapes.append(jax.ShapeDtypeStruct(*item))
            out_specs.append(pl.BlockSpec(memory_space=pltpu.VMEM))
    n_in, n_out = len(args), len(out_shapes)

    def kernel(*refs):
        given, rest = list(refs[: n_in + n_out]), list(refs[n_in + n_out :])
        bound = []
        for item in (*ins, *outs):
            if isinstance(item, Plan):
                near = [given.pop(0) for _ in item.arrays]
                buffer, sems = rest.pop(0), rest.pop(0)
                bound.append(Copies(buffer, item.pairs(near, buffer), sems))
            else:
                bound.append(given.pop(0))
        body(*bound[:named], *bound[len(ins) :], *rest)
        for item in bound[: len(ins)]:
            if isinstance(item, Copies):
                item.wait()
        for item in bound[len(ins) :]:
            if isinstance(item, Copies) and not item.started:
                item.start()
        for item in bound[len(ins) :]:
            if isinstance(item, Copies):
                item.wait()

    return pl.pallas_call(
        kernel,
        out_shape=out_shapes,
        in_specs=in_specs,
        out_specs=out_specs,
        scratch_shapes=buffers + list(scratch),
        cost_estimate=pl.CostEstimate(
            flops=int(us * 1.15e9), bytes_accessed=2**20, transcendentals=0
        ),
        compiler_params=pltpu.CompilerParams(vmem_limit_bytes=60 * 2**20),
        name=name,
    )(*args)


def start_all(*items):
    for item in items:
        item.start()


def unit_rows(rows):
    return lax.rsqrt(jnp.mean(rows * rows, -1, keepdims=True) + EPSILON)


def pack_body(
    rank_ref, x, cot, segment_ref, variate_ref, position_ref, wo, wq, wk, wv, gain_first_ref,
    gain_second_ref, gate, up, down, rows_out, shard_out, gate_up_out, down_out,
):
    start_all(wo, wq, wk, wv, x, cot, gate, up, down)
    micro, _, quarter, _ = x.ref.shape
    tokens = 4 * quarter
    lane = lax.broadcasted_iota(jnp.int32, (tokens, 128), 1)
    on_line = lax.broadcasted_iota(jnp.int32, (tokens, 128), 0) == lane

    def upright(row):
        return jnp.sum(jnp.where(on_line, row, 0.0), 1, keepdims=True)

    gains = jnp.where(
        lane == 0,
        upright(gain_first_ref[...].astype(WIDE)),
        jnp.where(lane == 1, upright(gain_second_ref[...].astype(WIDE)), 0.0),
    )
    shard_out.ref[:, D + 768 :] = gains.astype(LOW)
    shard_out.ref[:, :D] = wo.wait()[...]
    for place, weight in enumerate((wq, wk, wv)):
        shard_out.ref[:, D + 256 * place : D + 256 * (place + 1)] = weight.wait()[...]
    shard_out.start()
    for m in range(micro):
        places = position_ref[m : m + 1, :]
        numbers = jnp.zeros((tokens, 128), WIDE)
        for place, row in enumerate(
            (
                segment_ref[m : m + 1, :],
                variate_ref[m : m + 1, :],
                lax.shift_right_logical(places, 5),
                places & 31,
            )
        ):
            numbers = jnp.where(lane == place, upright(row.astype(WIDE)), numbers)
        numbers = numbers.astype(LOW)
        for r in range(4):
            rows_out.ref[r, 0, m, :, D:] = numbers[r * quarter : (r + 1) * quarter, :]
            rows_out.ref[r, 1, m, :, D:] = jnp.zeros((quarter, 128), LOW)
    x_ref, cot_ref = x.wait(), cot.wait()
    for m in range(micro):
        for r in range(4):
            rows_out.ref[r, 0, m, :, :D] = x_ref[m, r]
            rows_out.ref[r, 1, m, :, :D] = cot_ref[m, r]
    rows_out.start()
    gate_ref, up_ref = gate.wait(), up.wait()
    per = gate_up_out.ref.shape[1] // 2
    piece = gate_ref.shape[2]
    for s in range(per // piece):
        gate_up_out.ref[:, s * piece : (s + 1) * piece] = gate_ref[s]
        gate_up_out.ref[:, per + s * piece : per + (s + 1) * piece] = up_ref[s]
    gate_up_out.start()
    down_out.ref[...] = down.wait()[...]


def pack(rank, x, cot, segments, variates, positions, shards, gains, w_gate, w_up, w_down):
    micro, tokens, _ = x.shape
    quarter = tokens // 4
    shard, ff = w_gate.shape
    piece = w_down.shape[0] // 4
    pieces = ff // 4 // piece

    def quarters(array):
        return array.reshape(micro, 4, quarter, D)

    def mine(array, size, refs_at):
        return Plan([array], size, refs_at, 1)

    def rank_columns(array):
        def pairs(refs, buffer):
            at = pl.multiple_of(lax.axis_index("batch") * 256, 256)
            return [(refs[0].at[:, pl.ds(at, 256)], buffer)]

        return Plan([array], (shard, 256), pairs, 1)

    def feed_columns(array):
        def pairs(refs, buffer):
            rank = lax.axis_index("batch")
            return [
                (refs[0].at[:, pl.ds(pl.multiple_of((4 * s + rank) * piece, piece), piece)], buffer.at[s])
                for s in range(pieces)
            ]

        return Plan([array], (pieces, shard, piece), pairs, pieces)

    def down_rows(array):
        def pairs(refs, buffer):
            at = pl.multiple_of(lax.axis_index("batch") * piece, piece)
            return [(refs[0].at[pl.ds(at, piece)], buffer)]

        return Plan([array], (piece, D), pairs, 1)

    return run(
        pack_body,
        "pack",
        4,
        [rank, whole(quarters(x)), whole(quarters(cot)), segments, variates, positions]
        + [whole(shards[0])]
        + [rank_columns(weight) for weight in shards[1:]]
        + [*gains, feed_columns(w_gate), feed_columns(w_up), down_rows(w_down)],
        [
            out_whole((4, 2, micro, quarter, D + 128), LOW),
            out_whole((shard, D + 896), LOW),
            out_whole((shard, ff // 2), LOW),
            out_whole((piece, D), LOW),
        ],
    )


def attend_body(
    x, qkv, gains, freqs_ref, weights_ref,
    gain_ref, mixed, turned, wide, lower, upper, logs, cos, sin, query_sides, key_sides,
    keys_ref, values_ref, trig_ref,
):
    start_all(x, gains, qkv)
    count, chunk, _ = x.ref.shape
    lane = lax.broadcasted_iota(jnp.int32, (chunk, 128), 1)
    half_lane = lane // 64
    pick = lax.broadcasted_iota(jnp.int32, (16, 128), 0) == lax.broadcasted_iota(
        jnp.int32, (16, 128), 1
    )
    x_ref = x.wait()
    angles = jnp.zeros((chunk, 128), WIDE)
    for k in range(count):
        numbers = x_ref[k, :, D : D + 128].astype(WIDE)
        places = numbers[:, 2:3] * 32.0 + numbers[:, 3:4]
        angles = jnp.where(lane // 32 == k, places * freqs_ref[...], angles)
    trig_ref[0] = jnp.cos(angles)
    trig_ref[1] = jnp.sin(angles)
    gain_ref[...] = dot_rows(jnp.where(pick, 1.0, 0.0).astype(LOW), gains.wait()[...])
    qkv_ref = qkv.wait()

    def one_chunk(index, carry):
        rows = x_ref[index, :, :D].astype(WIDE)
        mixed_rows = (rows * unit_rows(rows) * gain_ref[0:1, :]).astype(LOW)
        mixed.ref[index] = mixed_rows

        def spread(packed):
            own = jnp.where(lane // 32 == index, packed, 0.0)
            own = own + pltpu.roll(own, 64, 1)
            return own + pltpu.roll(own, 32, 1)

        cosine = spread(trig_ref[0])
        sine = spread(trig_ref[1])
        sine = jnp.where(lane % 64 < 32, -sine, sine)
        cos.ref[index] = cosine
        sin.ref[index] = sine
        numbers = x_ref[index, :, D : D + 128].astype(WIDE).astype(jnp.int32)
        query_side, key_side = token_features(numbers[:, 0:1], numbers[:, 1:2])
        query_sides.ref[index] = query_side
        key_sides.ref[index] = key_side
        proj = dot_plain(mixed_rows, qkv_ref[...])
        values = proj[:, 512:].astype(LOW)
        turned.ref[index, :, 512:768] = values
        for pair in range(2):
            at = 128 * pair
            turned.ref[index, :, at : at + 128] = turn_pair(
                proj[:, at : at + 128], cosine, sine
            ).astype(LOW)
            keys = turn_pair(proj[:, 256 + at : 384 + at], cosine, sine).astype(LOW)
            turned.ref[index, :, 256 + at : 384 + at] = keys
            here = pl.ds(pl.multiple_of(index * chunk, chunk), chunk)
            keys_ref[pair, here, :128] = keys
            keys_ref[pair, here, 128:] = key_side
            values_ref[pair, here, :128] = values[:, at : at + 128]
            values_ref[pair, here, 128:] = jnp.where(lane == 0, 1.0, 0.0).astype(LOW)
        return carry

    lax.fori_loop(0, count, one_chunk, 0)
    start_all(mixed, turned, cos, sin, query_sides, key_sides)

    def one_block(index, carry):
        side = query_sides.ref[index]
        log_rows = jnp.zeros((chunk, 128), WIDE)
        here = pl.ds(pl.multiple_of((index % 2) * chunk, chunk), chunk)
        def scores_of(head):
            at = 128 * (head // 2)
            scaled = turned.ref[index, :, at : at + 128] * LOW(SCORE_SCALE)
            query = jnp.concatenate(
                [
                    jnp.where(half_lane == head % 2, scaled, LOW(0)),
                    side * weights_ref[head : head + 1, :],
                ],
                1,
            )
            return dot_rows(query, keys_ref[head // 2])

        scores = scores_of(0)
        parts = []
        for head in range(4):
            high = jnp.max(scores, 1, keepdims=True)
            powers = jnp.exp(scores - high).astype(LOW)
            if head < 3:
                scores = scores_of(head + 1)
            summed = dot_plain(powers, values_ref[head // 2])
            total = summed[:, 128:129]
            parts.append(summed[:, :128] / total)
            log_rows = jnp.where(lane == head, high + jnp.log(total), log_rows)
        for pair in range(2):
            at = 128 * pair
            total_mixed = jnp.where(half_lane == 0, parts[2 * pair], parts[2 * pair + 1])
            wide.ref[index, :, at : at + 128] = total_mixed
            low_rows = total_mixed.astype(LOW)

            @pl.when(index < 2)
            def _(low_rows=low_rows, at=at):
                lower.ref[here, at : at + 128] = low_rows

            @pl.when(index >= 2)
            def _(low_rows=low_rows, at=at):
                upper.ref[here, at : at + 128] = low_rows

        logs.ref[index] = log_rows
        return carry

    lax.fori_loop(0, count, one_block, 0)


def attend(chunks, first_weights, freqs, weights, token):
    chunk = chunks[0].shape[0]
    length = 4 * chunk
    return run(
        attend_body,
        "attend",
        15,
        [
            group(chunks),
            whole(first_weights, D, 768),
            whole(first_weights, D + 768, 128),
            freqs,
            weights,
        ],
        [
            ((16, D), WIDE),
            out_rows((length, D), LOW),
            out_rows((length, 768), LOW),
            out_rows((length, 256), WIDE),
            out_whole((length // 2, 256), LOW),
            out_whole((length // 2, 256), LOW),
            out_rows((length, 128), WIDE),
            out_rows((length, 128), WIDE),
            out_rows((length, 128), WIDE),
            out_rows((length, FEATURES), LOW),
            out_rows((length, FEATURES), LOW),
        ],
        [pltpu.VMEM((2, length, 256), LOW)] * 2 + [pltpu.VMEM((2, chunk, 128), WIDE)],
        token,
    )


def middle_body(rank_ref, x, near, far, wo, gain_ref, heads, own_ref, mixed):
    rank = rank_ref[0]
    start_all(near, far, wo, x)
    count, chunk, _ = x.ref.shape
    block = chunk // 2
    near_ref, far_ref = near.wait(), far.wait()
    width = near_ref.shape[2]
    sources = {
        0: ((near_ref, 0, 0), (near_ref, 2, 0), (far_ref, 0, 0), (far_ref, 0, width)),
        1: ((near_ref, 1, 0), (far_ref, 1, 0), (near_ref, 3, 0), (far_ref, 1, width)),
    }
    for half, order in enumerate((ORDER_A, ORDER_B)):
        for q in range(4):
            ref, which, column = sources[half][q]
            for place, r in enumerate(order):
                start = order.index(r ^ q) * block
                heads.ref[
                    2 * half + place // 2,
                    place % 2 * block : (place % 2 + 1) * block,
                    q * width : (q + 1) * width,
                ] = ref[which, start : start + block, column : column + width]
    heads.start()
    wo_ref = wo.wait()

    def one_chunk(index, carry):
        x.wait_at(index)
        total = x.ref[index, :, :D].astype(WIDE)
        for q in range(4):
            rows = pl.ds(pl.multiple_of((rank ^ q) * width, width), width)
            total = total + dot_plain(
                heads.ref[index, :, q * width : (q + 1) * width], wo_ref[rows, :]
            )

        @pl.when(index % 2 == 0)
        def _():
            own_ref[pl.ds(pl.multiple_of(index // 2 * block, block), block), :] = total[:block]

        mixed.ref[index] = (total * unit_rows(total) * gain_ref[1:2, :]).astype(LOW)
        mixed.start_at(index)
        return carry

    lax.fori_loop(0, count, one_chunk, 0)


def middle(rank, chunks, heads, first_weights, gain):
    chunk = chunks[0].shape[0]
    length = 4 * chunk
    lower, lower_x, lower_far, upper, upper_y, upper_far = heads
    return run(
        middle_body,
        "middle",
        7,
        [
            rank,
            group(chunks),
            group((lower, upper, lower_x, upper_y)),
            group((lower_far, upper_far)),
            whole(first_weights, 0, D),
            gain,
        ],
        [out_rows((length, D), LOW), ((chunk, D), WIDE), out_rows((length, D), LOW)],
    )


def feed_body(mixed, gate_up, both, hidden):
    count, _, per = hidden.ref.shape
    mixed.start(0)
    gate_up.start()
    mixed.start(1, 2, 3)

    def one_chunk(index, carry):
        mixed.wait_at(index)
        gate_up_ref = gate_up.wait_first(index)
        rows = mixed.ref[index]
        for half in range(2):
            here = slice(half * per // 2, (half + 1) * per // 2)
            gate = dot_plain(rows, gate_up_ref[half])
            up = dot_plain(rows, gate_up_ref[2 + half])
            sigmoid = 1.0 / (1.0 + jnp.exp(-gate))
            silu = gate * sigmoid
            both.ref[index, :, here] = (up * (sigmoid + silu * (1.0 - sigmoid))).astype(LOW)
            both.ref[index, :, per + half * per // 2 : per + (half + 1) * per // 2] = silu.astype(LOW)
            hidden.ref[index, :, here] = (silu * up).astype(LOW)
        both.start_at(index)
        hidden.start_at(index)
        return carry

    lax.fori_loop(0, count, one_chunk, 0)


def feed(mixed, gate_up, token):
    length = mixed.shape[0]
    per = gate_up.shape[1] // 2
    return run(
        feed_body,
        "feed",
        8,
        [rows_of(mixed), columns_of(gate_up)],
        [out_rows((length, 2 * per), LOW), out_rows((length, per), LOW)],
        token=token,
    )


def feed_back_body(both, cots, gate_up, down, grads, back):
    start_all(down)
    cots.start(0)
    both.start(0)
    gate_up.start()
    for k in range(1, 4):
        cots.start(k)
        both.start(k)
    count, _, _ = cots.ref.shape
    per = down.ref.shape[0]

    def one_chunk(index, carry):
        cots.wait_at(index)
        both.wait_at(index)
        grad_hidden = dot_rows(cots.ref[index], down.wait_first(index)[...])
        grads.ref[index, :, :per] = (
            grad_hidden * both.ref[index, :, :per].astype(WIDE)
        ).astype(LOW)
        grads.ref[index, :, per:] = (
            grad_hidden * both.ref[index, :, per:].astype(WIDE)
        ).astype(LOW)
        grads.start_at(index)
        back.ref[index] = dot_rows(grads.ref[index], gate_up.wait_first(index)[...]).astype(LOW)
        back.start_at(index)
        return carry

    lax.fori_loop(0, count, one_chunk, 0)


def feed_back(both, cots, gate_up, down, token):
    length = both.shape[0]
    per = down.shape[0]
    return run(
        feed_back_body,
        "feed_back",
        11,
        [rows_of(both), group(cots), whole(gate_up), whole(down)],
        [out_rows((length, 2 * per), LOW), out_group((length // 4, D), LOW)],
        token=token,
    )


def sum_arrived(near, got, last):
    return (
        near.wait()[...].astype(WIDE) + got.wait()[...].astype(WIDE) + last.wait()[...].astype(WIDE)
    )


def arrivals(sums):
    return [whole(x) if place % 3 == 2 else top(x) for place, x in enumerate(sums)]


def own_back_body(
    rank_ref, n0, g0, l0, n1, g1, l1, middle_rows, cot, gain_ref, wo, grad, parcels
):
    rank = rank_ref[0]
    start_all(n0, g0, l0, middle_rows, cot, n1, g1, l1, wo)
    block = l0.ref.shape[0]
    width = parcels.ref.shape[2] // 2
    for place, sums in enumerate(((n0, g0, l0), (n1, g1, l1))):
        rows = slice(place * block, (place + 1) * block)
        arrived = sum_arrived(*sums)
        y = middle_rows.wait()[rows, :]
        scale = unit_rows(y)
        normed = y * scale
        turned = arrived * gain_ref[1:2, :]
        grad.ref[rows, :] = cot.wait()[rows, :].astype(WIDE) + scale * (
            turned - normed * jnp.mean(turned * normed, -1, keepdims=True)
        )
    low_grad = grad.ref[...].astype(LOW)
    wo_ref = wo.wait()
    for q in range(4):
        place = pl.ds(pl.multiple_of((rank ^ q) * width, width), width)
        parcels.ref[q, :, :width] = dot_rows(low_grad, wo_ref[place, :]).astype(LOW)
        parcels.ref[q, :, width:] = grad.ref[:, place].astype(LOW)


def own_back(rank, sums, middle_own, cot_own, gain, first_weights, token):
    quarter = cot_own.shape[0]
    return run(
        own_back_body,
        "own_back",
        4,
        [rank, *arrivals(sums), whole(middle_own), whole(cot_own), gain]
        + [whole(first_weights, 0, D)],
        [out_whole((quarter, D), WIDE), out_group((quarter, 512), LOW)],
        token=token,
    )


def attend_back_body(
    pair, parcels, q, k, v, wide, logs, cos, sin, query_sides, key_sides, weights_ref,
    out, bias_ref, queries_ref, grads_ref, total_ref,
):
    start_all(parcels, q, query_sides, logs, wide, k, v, key_sides, cos, sin)
    length = q.ref.shape[0]
    chunk = length // 4
    block = chunk // 2
    half_lane = lax.broadcasted_iota(jnp.int32, (chunk, 128), 1) // 64
    lane = lax.broadcasted_iota(jnp.int32, (chunk, 128), 1)
    parcels_ref = parcels.wait()
    for half, order in enumerate((ORDER_A, ORDER_B)):
        for place in range(4):
            to = slice((4 * half + place) * block, (4 * half + place + 1) * block)
            rows = slice(half * block, (half + 1) * block)
            for head in range(2):
                grads_ref[head, to, :128] = parcels_ref[order[place], rows, :]
    q_ref, side_ref, log_ref, wide_ref = q.wait(), query_sides.wait(), logs.wait(), wide.wait()

    def prepare(index, carry):
        rows = pl.ds(pl.multiple_of(index * chunk, chunk), chunk)
        product = grads_ref[0, rows, :128].astype(WIDE) * wide_ref[rows, :]
        scaled = q_ref[rows, :] * LOW(SCORE_SCALE)
        for half in range(2):
            head = 2 * pair + half
            side = side_ref[rows, :] * weights_ref[head : head + 1, :]
            for place, piece in enumerate(three_parts(-log_ref[rows, head : head + 1])):
                side = jnp.where(lane == LSE_AT + place, piece, side)
            queries_ref[half, rows, :128] = jnp.where(half_lane == half, scaled, LOW(0))
            queries_ref[half, rows, 128:] = side
            delta = jnp.sum(jnp.where(half_lane == half, product, 0.0), 1, keepdims=True)
            extra = jnp.zeros((chunk, 128), LOW)
            for place, piece in enumerate(three_parts(-delta)):
                extra = jnp.where(lane == place, piece, extra)
            grads_ref[half, rows, 128:] = extra
        total_ref[rows, :] = jnp.zeros((chunk, 128), WIDE)
        return carry

    lax.fori_loop(0, 4, prepare, 0)
    three_ones = jnp.where(lane < 3, 1.0, 0.0).astype(LOW)
    k_ref, v_ref, key_ref, cos_ref, sin_ref = (
        k.wait(), v.wait(), key_sides.wait(), cos.wait(), sin.wait()
    )

    def one_block(index, carry):
        rows = pl.ds(pl.multiple_of(index * chunk, chunk), chunk)
        cosine = cos_ref[rows, :]
        sine = -sin_ref[rows, :]
        key_side = key_ref[rows, :]
        first_four = jnp.where(lane < 4, key_side.astype(WIDE), 0.0)
        sums = list(carry)
        keys = k_ref[rows, :]
        values = v_ref[rows, :]
        keys_wide = jnp.concatenate([keys, key_side], 1)
        grad_keys = jnp.zeros((chunk, 128), WIDE)
        grad_values = jnp.zeros((chunk, 128), WIDE)
        for half in range(2):
            mine = half_lane == half
            weights = jnp.exp(dot_rows(keys_wide, queries_ref[half]))
            grad_weights = dot_rows(
                jnp.concatenate([jnp.where(mine, values, LOW(0)), three_ones], 1), grads_ref[half]
            )
            grad_values = jnp.where(
                mine, dot_plain(weights.astype(LOW), grads_ref[half, :, :128]), grad_values
            )
            grad_scores = (weights * grad_weights).astype(LOW)
            both = dot_plain(
                grad_scores,
                jnp.concatenate([queries_ref[half, :, :128], side_ref[...]], 1),
            )
            grad_keys = grad_keys + both[:, :128]
            counted = both[:, 128:]
            same = jnp.sum(counted * first_four, 0, keepdims=True)
            every = jnp.sum(jnp.where(lane < 4, counted, 0.0), 0, keepdims=True)
            sums[half] = sums[half] + same
            sums[2 + half] = sums[2 + half] + (every - same)
            total_ref[...] += dot_first(grad_scores, jnp.where(mine, keys, LOW(0)))
        out.ref[index, :, 128:256] = turn_pair(grad_keys, cosine, sine).astype(LOW)
        out.ref[index, :, 256:] = grad_values.astype(LOW)
        return tuple(sums)

    start = tuple(jnp.zeros((1, 128), WIDE) for _ in range(4))
    sums = lax.fori_loop(0, 4, one_block, start)
    bias_ref[...] = jnp.zeros_like(bias_ref)
    for place in range(4):
        bias_ref[place : place + 1, :] = sums[place]
    for place in range(4):
        rows = slice(place * chunk, (place + 1) * chunk)
        out.ref[place, :, :128] = turn_pair(
            total_ref[rows, :] * SCORE_SCALE, cos_ref[rows, :], -sin_ref[rows, :]
        ).astype(LOW)


def attend_back(pair, parcels, kept, weights, token):
    turned, attended, *others = kept
    length = turned.shape[0]
    at = 128 * pair
    return run(
        functools.partial(attend_back_body, pair),
        "attend_back",
        40,
        [group(parcels, at, 128)]
        + [whole(turned, column + at, 128) for column in (0, 256, 512)]
        + [whole(attended, at, 128)]
        + [whole(x) for x in others]
        + [weights],
        [out_rows((length, 384), LOW), ((8, 128), WIDE)],
        [
            pltpu.VMEM((2, length, 256), LOW),
            pltpu.VMEM((2, length, 256), LOW),
            pltpu.VMEM((length, 128), WIDE),
        ],
        token,
    )


def project_back_body(proj0, proj1, weights, back, joined_ref):
    start_all(proj0, proj1, weights)
    proj = (proj0.wait(), proj1.wait())
    weights_ref = weights.wait()

    def one_chunk(index, carry):
        for kind in range(3):
            for pair in range(2):
                joined_ref[:, 256 * kind + 128 * pair : 256 * kind + 128 * (pair + 1)] = proj[pair][
                    index, :, 128 * kind : 128 * (kind + 1)
                ]
        back.ref[index] = dot_rows(joined_ref[...], weights_ref[...]).astype(LOW)
        back.start_at(index)
        return carry

    lax.fori_loop(0, back.ref.shape[0], one_chunk, 0)


def project_back(proj0, proj1, first_weights, token):
    length = proj0.shape[0]
    return run(
        project_back_body,
        "project_back",
        5,
        [rows_of(proj0), rows_of(proj1), whole(first_weights, D, 768)],
        [out_group((length // 4, D), LOW)],
        [pltpu.VMEM((length // 4, 768), LOW)],
        token,
    )


def down_grads_body(hidden, cots, out):
    start_all(cots, hidden)
    count, chunk, _ = cots.ref.shape

    def one_part(index, carry):
        cots_ref = cots.wait_first(index)
        hidden.wait_at(index)
        total = dot_first(hidden.ref[index, :chunk, :], cots_ref[0])
        for k in range(1, count):
            total = total + dot_first(
                hidden.ref[index, k * chunk : (k + 1) * chunk, :], cots_ref[k]
            )
        out.ref[index] = total.astype(LOW)
        out.start_at(index)
        return carry

    lax.fori_loop(0, hidden.ref.shape[0], one_part, 0)


def down_grads(hidden, cots):
    per = hidden.shape[1]
    return run(
        down_grads_body,
        "down_grads",
        5,
        [columns_of(hidden), group(cots)],
        [out_rows((per, D), LOW)],
    )[0]


def gate_up_grads_body(mixed, grads, out):
    start_all(grads, mixed)

    def one_part(index, carry):
        grads_ref = grads.wait_first(index)
        mixed.wait_at(index)
        out.ref[index] = dot_first(mixed.ref[index], grads_ref[...]).astype(LOW)
        out.start_at(index)
        return carry

    lax.fori_loop(0, mixed.ref.shape[0], one_part, 0)


def gate_up_grads(mixed, grads, token):
    return run(
        gate_up_grads_body,
        "gate_up_grads",
        8,
        [columns_of(mixed), whole(grads)],
        [out_rows((D, grads.shape[1]), LOW)],
        token=token,
    )[0]


def feed_out_body(hidden, down, out):
    start_all(down, hidden)

    def one_chunk(index, carry):
        down_ref = down.wait_first(index)
        hidden.wait_at(index)
        out.ref[index] = dot_plain(hidden.ref[index], down_ref[...]).astype(LOW)
        out.start_at(index)
        return carry

    lax.fori_loop(0, hidden.ref.shape[0], one_chunk, 0)


def feed_out(hidden, down, token):
    length = hidden.shape[0]
    return run(
        feed_out_body,
        "feed_out",
        5,
        [rows_of(hidden), whole(down)],
        [out_group((length // 4, D), LOW)],
        token=token,
    )


def own_last_body(
    n0, g0, l0, n1, g1, l1, m0, h0, k0, m1, h1, k1, x, base, middle_rows, gain_ref, out
):
    start_all(n0, g0, l0, x, base, m0, h0, k0, middle_rows, n1, g1, l1, m1, h1, k1)
    block = l0.ref.shape[0]
    piece = out.ref.shape[1] // 2
    each = block // piece
    for half, (back, forward) in enumerate(
        (((n0, g0, l0), (m0, h0, k0)), ((n1, g1, l1), (m1, h1, k1)))
    ):
        rows = slice(half * block, (half + 1) * block)
        places = slice(half * each, (half + 1) * each)
        turned = sum_arrived(*back) * gain_ref[0:1, :]
        x_rows = x.wait()[rows, :D].astype(WIDE)
        scale = unit_rows(x_rows)
        normed = x_rows * scale
        grad = base.wait()[rows, :] + scale * (
            turned - normed * jnp.mean(turned * normed, -1, keepdims=True)
        )
        out.ref[places, :piece, :] = grad.astype(LOW).reshape(each, piece, D)
        block_rows = sum_arrived(*forward) + middle_rows.wait()[rows, :]
        out.ref[places, piece:, :] = block_rows.astype(LOW).reshape(each, piece, D)


def own_last(sums, out_sums, mine, base, middle_own, gain, n_seq, token):
    quarter = base.shape[0]
    return run(
        own_last_body,
        "own_last",
        80,
        [*arrivals(sums), *arrivals(out_sums), whole(mine), whole(base), whole(middle_own), gain],
        [out_whole((n_seq, 2 * quarter // n_seq, D), LOW)],
        token=token,
    )[0]


def join_body(left, right, out):
    start_all(left, right)
    width = left.ref.shape[1]
    out.ref[:, :width] = left.wait()[...]
    out.ref[:, width:] = right.wait()[...]


def join(left, right, token):
    rows = left.shape[0]
    return run(
        join_body,
        "join",
        100,
        [whole(left), whole(right)],
        [out_whole((rows, left.shape[1] + right.shape[1]), LOW)],
        token=token,
    )[0]


def first_grads_body(rank_ref, mixed, proj0, proj1, heads, parcels, bias_ref, out, joined_ref):
    rank = rank_ref[0]
    start_all(mixed, proj0, proj1, parcels, heads)
    width = 256
    block = parcels.ref.shape[1] // 2
    for pair, proj in enumerate((proj0, proj1)):
        ref = proj.wait()
        for kind in range(3):
            column = width * kind + 128 * pair
            joined_ref[:, column : column + 128] = ref[:, 128 * kind : 128 * (kind + 1)]
    parcels_ref = parcels.wait()
    for half, order in enumerate((ORDER_A, ORDER_B)):
        for place in range(4):
            to = slice((4 * half + place) * block, (4 * half + place + 1) * block)
            joined_ref[to, 3 * width :] = parcels_ref[
                order[place], half * block : (half + 1) * block, :
            ]
    mixed_ref, heads_ref = mixed.wait(), heads.wait()

    def one_part(index, carry):
        out.ref[index, :, : 3 * width] = dot_first(
            mixed_ref[index], joined_ref[:, : 3 * width]
        ).astype(LOW)
        out.ref[rank ^ index, :, 3 * width : 4 * width] = dot_first(
            heads_ref[index], joined_ref[:, 3 * width :]
        ).astype(LOW)
        out.ref[index, :, 4 * width :] = bias_ref[...]
        return carry

    lax.fori_loop(0, 4, one_part, 0)


def first_grads(rank, mixed, proj0, proj1, heads, parcels, bias_rows, token):
    length = mixed.shape[0]
    return run(
        first_grads_body,
        "first_grads",
        8,
        [rank, columns_of(mixed), whole(proj0), whole(proj1), columns_of(heads)]
        + [group(parcels, 256, 256), bias_rows],
        [out_rows((D, 768 + 256 + 128), LOW)],
        [pltpu.VMEM((length, 1024), LOW)],
        token,
    )[0]


def rank_blocks(lower, lower_far, upper, upper_far):
    half = lower.shape[0] // 2
    return (
        ((lower, 0), (upper, 0)),
        ((lower, half), (upper_far, 0)),
        ((lower_far, 0), (upper, half)),
        ((lower_far, half), (upper_far, half)),
    )


def lay_flat(column, part):
    count = column.shape[0]
    row = lax.broadcasted_iota(jnp.int32, (count, 128), 0) + part * count
    lane = lax.broadcasted_iota(jnp.int32, (count, 128), 1)
    return jnp.sum(jnp.where(row == lane, column, 0.0), 0, keepdims=True)


def spread_feed_kernel(
    rank_ref, lower, lower_far, upper, upper_far, gate_ref, up_ref, gain_ref,
    grad_gate_ref, grad_up_ref, grad_down_ref, grad_gain_ref,
):
    rank = rank_ref[0]
    half = lower.shape[0] // 2
    piece = 128
    ff = gate_ref.shape[1]
    per = ff // 4
    for r, halves in enumerate(rank_blocks(lower, lower_far, upper, upper_far)):
        for part, (ref, start) in enumerate(halves):
            rows = slice(part * half, (part + 1) * half)
            source = slice(start, start + half)
            for s in range(per // piece):
                to = pl.ds(pl.multiple_of((4 * s + (rank ^ r)) * piece, piece), piece)
                grad_gate_ref[rows, to] = ref[source, s * piece : (s + 1) * piece].astype(WIDE)
                grad_up_ref[rows, to] = ref[source, per + s * piece : per + (s + 1) * piece].astype(
                    WIDE
                )
            to = pl.ds(pl.multiple_of((rank ^ r) * 2 * half + part * half, half), half)
            grad_down_ref[to, :] = ref[source, 2 * per :].astype(WIDE)
    flat = jnp.zeros((1, 128), WIDE)
    for part in range(2):
        rows = slice(part * half, (part + 1) * half)
        total = jnp.sum(
            gate_ref[rows, :].astype(WIDE) * grad_gate_ref[rows, :], 1, keepdims=True
        ) + jnp.sum(up_ref[rows, :].astype(WIDE) * grad_up_ref[rows, :], 1, keepdims=True)
        flat = flat + lay_flat(total, part)
    grad_gain_ref[...] = jnp.broadcast_to(flat / gain_ref[...].astype(WIDE), (8, 128))


def spread_feed(rank, pieces, w_gate, w_up, gain):
    shard, ff = w_gate.shape
    return call(
        spread_feed_kernel,
        "spread_feed",
        [((shard, ff), WIDE), ((shard, ff), WIDE), ((ff // 8, D), WIDE), ((8, 128), WIDE)],
        [pl.BlockSpec(memory_space=pltpu.SMEM)] + [whole_block()] * 7,
        4 * shard * ff,
        16 * 2**20,
        (rank, *pieces, w_gate, w_up, gain),
    )


def spread_first_kernel(
    rank_ref, lower, lower_far, upper, upper_far, wq_ref, wk_ref, wv_ref, gain_ref,
    gq_ref, gk_ref, gv_ref, go_ref, grad_gain_ref, bias_ref,
):
    rank = rank_ref[0]
    half = lower.shape[0] // 2
    wide = 256
    bias_ref[...] = jnp.zeros_like(bias_ref)
    for r, halves in enumerate(rank_blocks(lower, lower_far, upper, upper_far)):
        to = pl.ds(pl.multiple_of((rank ^ r) * wide, wide), wide)
        for part, (ref, start) in enumerate(halves):
            rows = slice(part * half, (part + 1) * half)
            source = slice(start, start + half)
            for place, out_ref in enumerate((gq_ref, gk_ref, gv_ref, go_ref)):
                out_ref[rows, to] = ref[source, place * wide : (place + 1) * wide].astype(WIDE)
        ref, start = halves[0]
        bias_ref[pl.ds(rank ^ r, 1), :] = jnp.sum(
            ref[start : start + 16, 4 * wide : 4 * wide + 128].astype(WIDE), 0, keepdims=True
        )
    flat = jnp.zeros((1, 128), WIDE)
    for part in range(2):
        rows = slice(part * half, (part + 1) * half)
        total = jnp.zeros((half, 1), WIDE)
        for weight_ref, grad_ref in ((wq_ref, gq_ref), (wk_ref, gk_ref), (wv_ref, gv_ref)):
            total = total + jnp.sum(
                weight_ref[rows, :].astype(WIDE) * grad_ref[rows, :], 1, keepdims=True
            )
        flat = flat + lay_flat(total, part)
    grad_gain_ref[...] = jnp.broadcast_to(flat / gain_ref[...].astype(WIDE), (8, 128))


def spread_first(rank, pieces, w_query, w_key, w_value, gain):
    shard = w_query.shape[0]
    return call(
        spread_first_kernel,
        "spread_first",
        [((shard, D), WIDE)] * 4 + [((8, 128), WIDE), ((8, 128), WIDE)],
        [pl.BlockSpec(memory_space=pltpu.SMEM)] + [whole_block()] * 8,
        4 * shard * D,
        8 * 2**20,
        (rank, *pieces, w_query, w_key, w_value, gain),
    )


def on_plane(
    inputs,
    w_query,
    w_key,
    w_value,
    w_output,
    gain_attention,
    w_gate,
    w_up,
    w_down,
    gain_feed,
    variate_bias,
    segment_ids,
    variate_ids,
    positions,
    grad_output,
):
    rank = lax.axis_index("batch")
    rank_row = jnp.reshape(rank, (1,)).astype(jnp.int32)
    micro, tokens = inputs.shape[0], inputs.shape[2]
    n_seq = lax.axis_size("seq")
    shard = w_query.shape[0]
    per = D // 4

    packed, first_shard, gate_up_shard, down_shard = pack(
        rank_row,
        inputs.reshape(micro, tokens, D),
        grad_output.reshape(micro, tokens, D),
        segment_ids.reshape(micro, tokens),
        variate_ids.reshape(micro, tokens),
        positions.reshape(micro, tokens),
        (w_output, w_query, w_key, w_value),
        (gain_attention.reshape(1, shard), gain_feed.reshape(1, shard)),
        w_gate,
        w_up,
        w_down,
    )
    first_weights = lax.all_gather(first_shard, "seq", axis=0, tiled=True)
    gate_up = lax.all_gather(gate_up_shard, "seq", axis=0, tiled=True)
    down = lax.all_gather(down_shard, "seq", axis=0, tiled=True)
    packed = lax.all_to_all(packed, "batch", 0, 0, tiled=True)
    by_sequence = [
        packed[:, kind].reshape(4 * micro, tokens // 4, D + 128)[:, :, : D + 128 - 128 * kind]
        for kind in range(2)
    ]
    mine, cot_by_sequence = lax.optimization_barrier((over_seq(by_sequence[0]), by_sequence[1]))
    cot_mine = over_seq(cot_by_sequence)
    freqs = jnp.exp((jnp.arange(128) % 32).astype(WIDE) * (-2.0 * math.log(10000.0) / HD))[None, :]
    my_bias = lax.dynamic_slice_in_dim(variate_bias, rank * 4, 4, 1)
    weights = jnp.pad(head_weights(my_bias[0], my_bias[1]), ((0, 4), (0, 0)))

    chunks = gather_plane(mine)
    gain, mixed_first, turned, attended, lower, upper, *kept = attend(
        chunks, first_weights, freqs, weights, rank_row
    )
    lower_x, upper_y = swap(lower, 1), swap(upper, 2)
    lower_far = swap(jnp.concatenate([lower, lower_x], 1), 2)
    upper_far = swap(jnp.concatenate([upper, upper_y], 1), 1)
    cot_got = swap_pairs(lax.optimization_barrier((cot_mine, lower_far, upper_far))[0])
    heads, middle_own, mixed_second = middle(
        rank_row,
        chunks,
        (lower, lower_x, lower_far, upper, upper_y, upper_far),
        first_weights,
        gain,
    )

    both, hidden = feed(mixed_second, gate_up, after(rank_row, cot_got))
    cots = far_pairs(cot_mine, lax.optimization_barrier((cot_got, mixed_second))[0])
    down_weight_grads = down_grads(hidden, cots)
    down_grad_shard = lax.psum_scatter(down_weight_grads, "seq", scatter_dimension=0, tiled=True)
    grad_gate_up, *back = feed_back(
        both, cots, gate_up, down, after(rank_row, down_weight_grads)
    )
    got = scatter_first(back)
    gate_up_weight_grads = gate_up_grads(mixed_second, grad_gate_up, after(rank_row, got))
    gate_up_grad_shard = lax.psum_scatter(
        gate_up_weight_grads, "seq", scatter_dimension=0, tiled=True
    )
    sums = scatter_second(back, got)
    grad_middle, *parcels = own_back(
        rank_row, sums, middle_own, cot_mine, gain, first_weights,
        after(rank_row, gate_up_weight_grads),
    )
    out_chunks = feed_out(hidden, down, after(rank_row, parcels[0]))
    parcels = [parcels[0]] + [swap(parcels[r], r) for r in range(1, 4)]

    far_chunks = lax.optimization_barrier(((out_chunks[1], out_chunks[3]), parcels))[0]
    out_got = scatter_first((None, far_chunks[0], None, far_chunks[1]))
    kept = (turned, attended, *kept)
    proj0, bias0 = attend_back(
        0, parcels, kept, weights, after(rank_row, far_chunks, down_grad_shard)
    )
    out_got = lax.optimization_barrier((out_got, bias0))[0]
    out_sums = scatter_second(out_chunks, out_got)
    proj1, bias1 = attend_back(1, parcels, kept, weights, after(rank_row, out_got))
    back = project_back(
        proj0, proj1, first_weights, after(rank_row, out_sums[2], out_sums[5])
    )
    got = scatter_first(back)
    bias_sums = jnp.sum(jnp.concatenate([bias0[:2], bias1[:2], bias0[2:4], bias1[2:4]], 0), 1)
    bias_parts = jnp.pad(jnp.concatenate(three_parts(bias_sums)), (0, 104))[None, :]
    slots = lax.broadcasted_iota(jnp.int32, (per, 1), 0) % shard == lax.axis_index("seq")
    bias_rows = jnp.where(slots, bias_parts, LOW(0))
    first_weight_grads = first_grads(
        rank_row, mixed_first, proj0, proj1, heads, parcels, bias_rows, after(rank_row, got)
    )
    first_grad_shard = lax.psum_scatter(first_weight_grads, "seq", scatter_dimension=0, tiled=True)
    sums = scatter_second(back, got)
    last = own_last(
        sums, out_sums, mine, grad_middle, middle_own, gain, n_seq,
        after(rank_row, first_weight_grads),
    )
    moved = lax.all_to_all(last, "seq", 0, 0, tiled=True)
    quarter = tokens // 4
    feed_pieces = gather_plane(
        join(gate_up_grad_shard, down_grad_shard, after(rank_row, last))
    )
    first_pieces = gather_plane(after(first_grad_shard, feed_pieces))
    moved, first_pieces = lax.optimization_barrier((moved, first_pieces))
    moved = moved.reshape(4, micro, 2 * quarter, D)
    moved = lax.all_to_all(moved, "batch", 0, 0, tiled=True)
    grad_inputs = jnp.transpose(moved[:, :, :quarter].astype(WIDE), (1, 0, 2, 3))
    block_output = jnp.transpose(moved[:, :, quarter:], (1, 0, 2, 3))

    grad_gate, grad_up, grad_down, grad_gain_second = spread_feed(
        rank_row, feed_pieces, w_gate, w_up, gain_feed.reshape(1, shard)
    )
    grad_query, grad_key, grad_value, grad_output_weights, grad_gain_first, bias_table = (
        spread_first(
            rank_row, first_pieces, w_query, w_key, w_value, gain_attention.reshape(1, shard)
        )
    )
    bias_table = jnp.sum(bias_table[:4, :24].reshape(4, 3, 2, 4), 1)
    grad_bias = jnp.transpose(bias_table, (1, 0, 2)).reshape(2, H)
    return (
        block_output.reshape(inputs.shape),
        grad_inputs.reshape(inputs.shape),
        grad_query,
        grad_key,
        grad_value,
        grad_output_weights,
        grad_gain_first[0],
        grad_gate,
        grad_up,
        grad_down,
        grad_gain_second[0],
        grad_bias,
    )


def solution(mesh):
    n_batch, n_seq = mesh.shape["batch"], mesh.shape["seq"]
    step = on_plane if n_batch == 4 and n_seq == 8 else on_device
    return jax.shard_map(
        step,
        mesh=mesh,
        in_specs=(
            P(None, "batch", "seq", None),
            P("seq", None),
            P("seq", None),
            P("seq", None),
            P("seq", None),
            P("seq"),
            P("seq", None),
            P("seq", None),
            P("seq", None),
            P("seq"),
            P(),
            P(None, "batch", "seq"),
            P(None, "batch", "seq"),
            P(None, "batch", "seq"),
            P(None, "batch", "seq", None),
        ),
        out_specs=(
            P(None, "batch", "seq", None),
            P(None, "batch", "seq", None),
            P("seq", None),
            P("seq", None),
            P("seq", None),
            P("seq", None),
            P("seq"),
            P("seq", None),
            P("seq", None),
            P("seq", None),
            P("seq"),
            P(),
        ),
        check_vma=False,
    )
```

profile of v0, /device:TPU:0, one launch (start us, length us, event | category | flops | bytes accessed | tf_op | source)
XLA Modules:
  0.0 363.1 jit_solution(15785320920459129338)
XLA Ops:
  7.2 3.9 %pack.1 = (bf16[4,2,2,32,1152]{4,3,2,1,0:T(8,128)(2,1)}, bf16[128,1920]{1,0:T(8,128)(2,1)}, bf16[128,2048]{1,0:T(8,128)(2,1)}, bf16[128,1024]{1,0:T(8,128)(2,1)}) custom-call(s32[1]{0:T(128)} %bitcast.refs_0_.refs_8_.refs_2_.refs_7_.refs_11_.refs_14_.refs_3_.refs_10_.refs_16_.rank_ref, bf16[2,4,32,1024]{3,2,1,0:T(8,128)(2,1)} %bitcast.57, ...), custom_call_target="tpu_custom_call" | custom-call | flops 4600000000 | bytes 1048576 | tf_op jit(solution)/shard_map/pack/pallas_call | solution.py:768
  12.0 20.7 %all_to_all.25 = bf16[4,2,2,32,1152]{4,3,2,1,0:T(8,128)(2,1)S(1)} all-to-all(bf16[4,2,2,32,1152]{4,3,2,1,0:T(8,128)(2,1)} %get-tuple-element.90), channel_id=1, replica_groups=mesh['batch'=4,'seq'=8] {'batch'}, dimensions={0} | all-to-all | bytes 2359296 | tf_op jit(solution)/shard_map/all_to_all | solution.py:1706
  33.6 4.9 %all-to-all-start.1 = ((bf16[8,32,1152]{2,1,0:T(8,128)(2,1)}), bf16[8,32,1152]{2,1,0:T(8,128)(2,1)S(1)}, u32[]{:S(2)}, u32[]{:S(2)}) async-start(bf16[8,32,1152]{2,1,0:T(8,128)(2,1)} %bitcast.8), calls=%async_computation.1 | async-start | bytes 1179648 | tf_op jit(solution)/shard_map/all_to_all | solution.py:523
  39.4 29.7 %all-to-all-done.1 = bf16[8,32,1152]{2,1,0:T(8,128)(2,1)S(1)} async-done(((bf16[8,32,1152]{2,1,0:T(8,128)(2,1)}), bf16[8,32,1152]{2,1,0:T(8,128)(2,1)S(1)}, u32[]{:S(2)}, u32[]{:S(2)}) %all-to-all-start.1) | async-done | bytes 589856 | tf_op jit(solution)/shard_map/all_to_all | solution.py:523
  71.5 6.8 %collective-permute-done = bf16[128,1152]{1,0:T(8,128)(2,1)S(1)} collective-permute-done((bf16[128,1152]{1,0:T(8,128)(2,1)S(1)}, bf16[128,1152]{1,0:T(8,128)(2,1)S(1)}, u32[]{:S(2)}, u32[]{:S(2)}) %collective-permute-start) | collective-permute-done | bytes 294944 | tf_op jit(solution)/shard_map/ppermute | solution.py:481
  81.9 3.5 all-to-all-start.2
  85.5 7.6 %collective-permute-done.1.refs_1_.refs_2_ = bf16[256,1152]{1,0:T(8,128)(2,1)S(1)} collective-permute-done((bf16[256,1152]{1,0:T(8,128)(2,1)S(1)}, bf16[256,1152]{1,0:T(8,128)(2,1)S(1)}, u32[]{:S(2)}, u32[]{:S(2)}) %collective-permute-start.1) | collective-permute-done | bytes 589856 | tf_op jit(solution)/shard_map/ppermute | solution.py:481
  94.7 16.7 %attend.1 = (f32[16,1024]{1,0:T(8,128)}, bf16[1024,1024]{1,0:T(8,128)(2,1)}, bf16[1024,768]{1,0:T(8,128)(2,1)}, f32[1024,256]{1,0:T(8,128)}, bf16[512,256]{1,0:T...) custom-call(bf16[256,1152]{1,0:T(8,128)(2,1)} %copy-done.10, ...), custom_call_target="tpu_custom_call" | custom-call | flops 17250000896 | bytes 1048576 | tf_op jit(solution)/shard_map/attend/pallas_call | solution.py:768
  113.7 4.4 %collective-permute-done.4.refs_7_ = bf16[512,256]{1,0:T(8,128)(2,1)S(1)} collective-permute-done((bf16[512,256]{1,0:T(8,128)(2,1)}, bf16[512,256]{1,0:T(8,128)(2,1)S(1)}, u32[]{:S(2)}, u32[]{:S(2)}) %collective-permute-start.4) | collective-permute-done | bytes 262176 | tf_op jit(solution)/shard_map/ppermute | solution.py:481
  122.5 7.9 %collective-permute-done.6.refs_9_ = bf16[512,512]{1,0:T(8,128)(2,1)S(1)} collective-permute-done((bf16[512,512]{1,0:T(8,128)(2,1)S(1)}, bf16[512,512]{1,0:T(8,128)(2,1)S(1)}, u32[]{:S(2)}, u32[]{:S(2)}) %collective-permute-start.6) | collective-permute-done | bytes 524320 | tf_op jit(solution)/shard_map/ppermute | solution.py:481
  130.4 3.0 collective-permute-done.7.refs_10_
  134.5 9.3 %middle.1 = (bf16[1024,1024]{1,0:T(8,128)(2,1)}, f32[256,1024]{1,0:T(8,128)}, bf16[1024,1024]{1,0:T(8,128)(2,1)}) custom-call(s32[1]{0:T(128)} %bitcast.refs_0_.refs_8_.refs_2_.refs_7_.refs_11_.refs_14_.refs_3_.refs_10_.refs_16_.rank_ref, bf16[256,1152]{1,0:T(8,128)(2,1)} %copy-done.10, bf16[256,1152]{1,0:T(8,128)(2,1)} %copy-done.27, ...), custom_call_target="tpu_custom_call" | custom-call | flops 8049999872 | bytes 1048576 | tf_op jit(solution)/shard_map/middle/pallas_call | solution.py:768
  147.1 9.3 %feed.1 = (bf16[1024,2048]{1,0:T(8,128)(2,1)}, bf16[1024,1024]{1,0:T(8,128)(2,1)}) custom-call(bf16[1024,1024]{1,0:T(8,128)(2,1)} %get-tuple-element.96.refs_0_, bf16[1024,2048]{1,0:T(8,128)(2,1)} %all-gather.6.cloned.1.call-done.refs_1_.refs_5_, s32[1]{0:T(128)} %bitcast.refs_0_.refs_8_.refs_2_.refs_7_.refs_11_.refs_14_.refs_3_.refs_10_.refs_16_.rank_ref), custom_call_target="tpu_custom_call" | custom-call | flops 9200000000 | bytes 1048576 | tf_op jit(solution)/shard_map/feed/pallas_call | solution.py:768
  157.5 5.9 %down_grads.1 = bf16[1024,1024]{1,0:T(8,128)(2,1)} custom-call(bf16[1024,1024]{1,0:T(8,128)(2,1)} %get-tuple-element.105.refs_0_, bf16[256,1024]{1,0:T(8,128)(2,1)} %copy-done.13, bf16[256,1024]{1,0:T(8,128)(2,1)} %copy-done.32, bf16[256,1024]{1,0:T(8,128)(2,1)} %copy-done.12, bf16[256,1024]{1,0:T(8,128)(2,1)} %copy-done.30), custom_call_target="tpu_custom_call" | custom-call | flops 5750000128 | bytes 1048576 | tf_op jit(solution)/shard_map/down_grads/pallas_call | solution.py:768
  163.6 13.0 %feed_back.1 = (bf16[1024,2048]{1,0:T(8,128)(2,1)}, bf16[256,1024]{1,0:T(8,128)(2,1)}, bf16[256,1024]{1,0:T(8,128)(2,1)}, bf16[256,1024]{1,0:T(8,128)(2,1)}, bf16[256,1024]{1,0:T(8,128)(2,1)}) custom-call(bf16[1024,2048]{1,0:T(8,128)(2,1)} %get-tuple-element.101.refs_0_, bf16[256,1024]{1,0:T(8,128)(2,1)} %copy-done.13, bf16[256,1024]{1,0:T(8,128)(2,1)} %copy-done.32, ...), custom_call_target="tpu_custom_call" | custom-call | flops 12650000384 | bytes 1048576 | tf_op jit(solution)/shard_map/feed_back/pallas_call | solution.py:768
  177.7 9.7 %collective-permute-done.12.refs_2_ = bf16[256,1024]{1,0:T(8,128)(2,1)S(1)} collective-permute-done((bf16[256,1024]{1,0:T(8,128)(2,1)}, bf16[256,1024]{1,0:T(8,128)(2,1)S(1)}, u32[]{:S(2)}, u32[]{:S(2)}) %collective-permute-start.12) | collective-permute-done | bytes 524320 | tf_op jit(solution)/shard_map/ppermute | solution.py:481
  192.8 8.9 %gate_up_grads.1 = bf16[1024,2048]{1,0:T(8,128)(2,1)} custom-call(bf16[1024,1024]{1,0:T(8,128)(2,1)} %get-tuple-element.96.refs_0_, bf16[1024,2048]{1,0:T(8,128)(2,1)} %get-tuple-element.112.refs_1_, s32[1]{0:T(128)} %bitcast.refs_0_.refs_8_.refs_2_.refs_7_.refs_11_.refs_14_.refs_3_.refs_10_.refs_16_.rank_ref), custom_call_target="tpu_custom_call" | custom-call | flops 9200000000 | bytes 1048576 | tf_op jit(solution)/shard_map/gate_up_grads/pallas_call | solution.py:768
  202.7 5.5 %own_back.1 = (f32[256,1024]{1,0:T(8,128)}, bf16[256,512]{1,0:T(8,128)(2,1)}, bf16[256,512]{1,0:T(8,128)(2,1)}, bf16[256,512]{1,0:T(8,128)(2,1)}, bf16[256,512]{1,0:T(8,128)(2,1)}) custom-call(s32[1]{0:T(128)} %bitcast.refs_0_.refs_8_.refs_2_.refs_7_.refs_11_.refs_14_.refs_3_.refs_10_.refs_16_.rank_ref, bf16[256,1024]{1,0:T(8,128)(2,1)} %get-tuple-element.107.refs_1_, ...), custom_call_target="tpu_custom_call" | custom-call | flops 4600000000 | bytes 1048576 | tf_op jit(solution)/shard_map/own_back/pallas_call | solution.py:768
  211.8 5.9 %feed_out.1 = (bf16[256,1024]{1,0:T(8,128)(2,1)}, bf16[256,1024]{1,0:T(8,128)(2,1)}, bf16[256,1024]{1,0:T(8,128)(2,1)}, bf16[256,1024]{1,0:T(8,128)(2,1)}) custom-call(bf16[1024,1024]{1,0:T(8,128)(2,1)} %get-tuple-element.105.refs_0_, bf16[1024,1024]{1,0:T(8,128)(2,1)} %all-gather.8.cloned.1.call-done.refs_6_.refs_1_, ...), custom_call_target="tpu_custom_call" | custom-call | flops 5750000128 | bytes 1048576 | tf_op jit(solution)/shard_map/feed_out/pallas_call | solution.py:768
  222.6 12.0 %attend_back.2 = (bf16[1024,384]{1,0:T(8,128)(2,1)}, f32[8,128]{1,0:T(8,128)}) custom-call(bf16[256,512]{1,0:T(8,128)(2,1)} %get-tuple-element.115.refs_0_.refs_5_, bf16[256,512]{1,0:T(8,128)(2,1)} %copy-done.33, bf16[256,512]{1,0:T(8,128)(2,1)} %copy-done.34, bf16[256,512]{1,0:T(8,128)(2,1)} %copy-done.35, ...), custom_call_target="tpu_custom_call" | custom-call | flops 46000001024 | bytes 1048576 | tf_op jit(solution)/shard_map/attend_back/pallas_call | solution.py:768
  236.9 11.9 %attend_back.3 = (bf16[1024,384]{1,0:T(8,128)(2,1)}, f32[8,128]{1,0:T(8,128)}) custom-call(bf16[256,512]{1,0:T(8,128)(2,1)} %get-tuple-element.115.refs_0_.refs_5_, bf16[256,512]{1,0:T(8,128)(2,1)} %copy-done.33, bf16[256,512]{1,0:T(8,128)(2,1)} %copy-done.34, bf16[256,512]{1,0:T(8,128)(2,1)} %copy-done.35, ...), custom_call_target="tpu_custom_call" | custom-call | flops 46000001024 | bytes 1048576 | tf_op jit(solution)/shard_map/attend_back/pallas_call | solution.py:768
  249.8 5.6 %project_back.1 = (bf16[256,1024]{1,0:T(8,128)(2,1)}, bf16[256,1024]{1,0:T(8,128)(2,1)}, bf16[256,1024]{1,0:T(8,128)(2,1)}, bf16[256,1024]{1,0:T(8,128)(2,1)}) custom-call(bf16[1024,384]{1,0:T(8,128)(2,1)} %get-tuple-element.132.refs_0_.refs_2_, bf16[1024,384]{1,0:T(8,128)(2,1)} %get-tuple-element.137.refs_1_.refs_3_, ...), custom_call_target="tpu_custom_call" | custom-call | flops 5750000128 | bytes 1048576 | tf_op jit(solution)/shard_map/project_back/pallas_call | solution.py:768
  258.3 8.0 %collective-permute-done.23.refs_1_ = bf16[256,1024]{1,0:T(8,128)(2,1)S(1)} collective-permute-done((bf16[256,1024]{1,0:T(8,128)(2,1)}, bf16[256,1024]{1,0:T(8,128)(2,1)S(1)}, u32[]{:S(2)}, u32[]{:S(2)}) %collective-permute-start.23) | collective-permute-done | bytes 524320 | tf_op jit(solution)/shard_map/ppermute | solution.py:481
  267.5 3.2 collective-permute-start.24
  272.0 8.5 %first_grads.1 = bf16[1024,1152]{1,0:T(8,128)(2,1)} custom-call(s32[1]{0:T(128)} %bitcast.refs_0_.refs_8_.refs_2_.refs_7_.refs_11_.refs_14_.refs_3_.refs_10_.refs_16_.rank_ref, bf16[1024,1024]{1,0:T(8,128)(2,1)} %get-tuple-element.146.refs_1_, bf16[1024,384]{1,0:T(8,128)(2,1)} %get-tuple-element.132.refs_0_.refs_2_, ...), custom_call_target="tpu_custom_call" | custom-call | flops 9200000000 | bytes 1048576 | tf_op jit(solution)/shard_map/first_grads/pallas_call | solution.py:768
  281.3 4.8 %own_last.1 = bf16[8,64,1024]{2,1,0:T(8,128)(2,1)} custom-call(bf16[256,1024]{1,0:T(8,128)(2,1)} %get-tuple-element.141.refs_0_, bf16[256,1024]{1,0:T(8,128)(2,1)} %copy-done.22, bf16[128,1024]{1,0:T(8,128)(2,1)} %copy-done.38, bf16[256,1024]{1,0:T(8,128)(2,1)} %get-tuple-element.143.refs_3_, bf16[256,1024]{1,0:T(8,128)(2,1)} %copy-done.23, ...), custom_call_target="tpu_custom_call" | custom-call | flops 92000002048 | bytes 1048576 | tf_op jit(solution)/shard_map/own_last/pallas_call | solution.py:768
  291.5 9.9 %collective-permute-done.27 = bf16[64,3072]{1,0:T(8,128)(2,1)S(1)} collective-permute-done((bf16[64,3072]{1,0:T(8,128)(2,1)S(1)}, bf16[64,3072]{1,0:T(8,128)(2,1)S(1)}, u32[]{:S(2)}, u32[]{:S(2)}) %collective-permute-start.27) | collective-permute-done | bytes 393248 | tf_op jit(solution)/shard_map/ppermute | solution.py:481
  303.8 4.2 %all-to-all-start.3 = ((bf16[8,64,1024]{2,1,0:T(8,128)(2,1)}), bf16[8,64,1024]{2,1,0:T(8,128)(2,1)}, u32[]{:S(2)}, u32[]{:S(2)}) async-start(bf16[8,64,1024]{2,1,0:T(8,128)(2,1)} %own_last.1), calls=%async_computation.4 | async-start | bytes 2097152 | tf_op jit(solution)/shard_map/all_to_all | solution.py:1779
  308.1 9.4 %reduce-scatter.6.cloned.1.call-done = bf16[128,1152]{1,0:T(8,128)(2,1)} async-done(((bf16[1024,1152]{1,0:T(8,128)(2,1)}), bf16[128,1152]{1,0:T(8,128)(2,1)}) %reduce-scatter.6.cloned.1.call-update) | async-done | bytes 294928 | tf_op jit(solution)/shard_map/reduce_scatter | solution.py:1773
  329.7 6.4 %all-to-all-done.3 = bf16[8,64,1024]{2,1,0:T(8,128)(2,1)} async-done(((bf16[8,64,1024]{2,1,0:T(8,128)(2,1)}), bf16[8,64,1024]{2,1,0:T(8,128)(2,1)}, u32[]{:S(2)}, u32[]{:S(2)}) %all-to-all-start.3) | async-done | bytes 1048608 | tf_op jit(solution)/shard_map/all_to_all | solution.py:1779
  336.9 3.5 all-to-all-start.4
  340.4 5.8 %spread_feed.1 = (f32[128,4096]{1,0:T(8,128)}, f32[128,4096]{1,0:T(8,128)}, f32[512,1024]{1,0:T(8,128)}, f32[8,128]{1,0:T(8,128)}) custom-call(s32[1]{0:T(128)} %bitcast.refs_0_.refs_8_.refs_2_.refs_7_.refs_11_.refs_14_.refs_3_.refs_10_.refs_16_.rank_ref, bf16[128,3072]{1,0:T(8,128)(2,1)} %copy-done.3, bf16[128,3072]{1,0:T(8,128)(2,1)} %copy-done.8, ...), custom_call_target="tpu_custom_call" | custom-call | flops 2097152 | bytes 16777216 | tf_op jit(solution)/shard_map/spread_feed/pallas_call | solution.py:580
  (221 shorter events, 78.2 us)
Async XLA Ops:
  7.2 86.7 %all-gather.4.cloned.1.call-start = ((), (), s32[]{:S(2)}) async-start(), calls=%async_computation.8 | async-start | bytes 4423680 | tf_op jit(solution)/shard_map/all_gather | solution.py:1703
  11.2 135.9 %all-gather.6.cloned.1.call-start = ((), (), s32[]{:S(2)}) async-start(), calls=%async_computation.9 | async-start | bytes 4718592 | tf_op jit(solution)/shard_map/all_gather | solution.py:1704
  33.6 35.5 %all-to-all-start.1 = ((bf16[8,32,1152]{2,1,0:T(8,128)(2,1)}), bf16[8,32,1152]{2,1,0:T(8,128)(2,1)S(1)}, u32[]{:S(2)}, u32[]{:S(2)}) async-start(bf16[8,32,1152]{2,1,0:T(8,128)(2,1)} %bitcast.8), calls=%async_computation.1 | async-start | bytes 1179648 | tf_op jit(solution)/shard_map/all_to_all | solution.py:523
  78.4 14.7 %collective-permute-start.1 = (bf16[256,1152]{1,0:T(8,128)(2,1)S(1)}, bf16[256,1152]{1,0:T(8,128)(2,1)S(1)}, u32[]{:S(2)}, u32[]{:S(2)}) collective-permute-start(bf16[256,1152]{1,0:T(8,128)(2,1)S(1)} %pad_maximum_fusion.2.refs_0_.refs_1_), channel_id=1, source_target_pairs={{0,16},{8,24},{16,0},{24,8},{1,17},{9,25},{17,1},{25,9},{2,18},{10... | collective-permute-start | bytes 1769480 | tf_op jit(solution)/shard_map/ppermute | solution.py:481
  79.7 14.2 %collective-permute-start.3 = (bf16[256,1152]{1,0:T(8,128)(2,1)S(1)}, bf16[256,1152]{1,0:T(8,128)(2,1)S(1)}, u32[]{:S(2)}, u32[]{:S(2)}) collective-permute-start(bf16[256,1152]{1,0:T(8,128)(2,1)S(1)} %pad_maximum_fusion.3.refs_2_.refs_3_), channel_id=1, source_target_pairs={{0,8},{8,0},{16,24},{24,16},{1,9},{9,1},{17,25},{25,17},{2,10},{10... | collective-permute-start | bytes 1769480 | tf_op jit(solution)/shard_map/ppermute | solution.py:481
  81.9 40.5 %all-to-all-start.2 = ((bf16[8,32,1024]{2,1,0:T(8,128)(2,1)}), bf16[8,32,1024]{2,1,0:T(8,128)(2,1)S(1)}, u32[]{:S(2)}, u32[]{:S(2)}) async-start(bf16[8,32,1024]{2,1,0:T(8,128)(2,1)} %slice.154), calls=%async_computation.2 | async-start | bytes 1048576 | tf_op jit(solution)/shard_map/all_to_all | solution.py:523
  85.4 78.2 %all-gather.8.cloned.1.call-start = ((), (), s32[]{:S(2)}) async-start(), calls=%async_computation.10 | async-start | bytes 2359296 | tf_op jit(solution)/shard_map/all_gather | solution.py:1705
  112.2 110.3 %reduce-scatter.4.cloned.1.call-start = ((), (), s32[]{:S(2)}) async-start(), calls=%async_computation.11 | async-start | bytes 2359296 | tf_op jit(solution)/shard_map/reduce_scatter | solution.py:1736
  119.2 11.2 %collective-permute-start.6 = (bf16[512,512]{1,0:T(8,128)(2,1)S(1)}, bf16[512,512]{1,0:T(8,128)(2,1)S(1)}, u32[]{:S(2)}, u32[]{:S(2)}) collective-permute-start(bf16[512,512]{1,0:T(8,128)(2,1)S(1)} %pad_maximum_fusion.4), channel_id=1, source_target_pairs={{0,16},{8,24},{16,0},{24,8},{1,17},{9,25},{17,1},{25,9},{2,18},{10... | collective-permute-start | bytes 1572872 | tf_op jit(solution)/shard_map/ppermute | solution.py:481
  121.6 11.8 %collective-permute-start.7 = (bf16[512,512]{1,0:T(8,128)(2,1)S(1)}, bf16[512,512]{1,0:T(8,128)(2,1)S(1)}, u32[]{:S(2)}, u32[]{:S(2)}) collective-permute-start(bf16[512,512]{1,0:T(8,128)(2,1)S(1)} %pad_maximum_fusion.5), channel_id=1, source_target_pairs={{0,8},{8,0},{16,24},{24,16},{1,9},{9,1},{17,25},{25,17},{2,10},{10... | collective-permute-start | bytes 1572872 | tf_op jit(solution)/shard_map/ppermute | solution.py:481
  143.9 12.6 %collective-permute-start.11 = (bf16[256,1024]{1,0:T(8,128)(2,1)S(1)}, bf16[256,1024]{1,0:T(8,128)(2,1)S(1)}, u32[]{:S(2)}, u32[]{:S(2)}) collective-permute-start(bf16[256,1024]{1,0:T(8,128)(2,1)S(1)} %pad_maximum_fusion.7.refs_3_), channel_id=1, source_target_pairs={{0,8},{8,0},{16,24},{24,16},{1,9},{9,1},{17,25},{25,17},{2,10},{10... | collective-permute-start | bytes 1572872 | tf_op jit(solution)/shard_map/ppermute | solution.py:481
  145.1 11.4 %collective-permute-start.10 = (bf16[256,1024]{1,0:T(8,128)(2,1)S(1)}, bf16[256,1024]{1,0:T(8,128)(2,1)S(1)}, u32[]{:S(2)}, u32[]{:S(2)}) collective-permute-start(bf16[256,1024]{1,0:T(8,128)(2,1)S(1)} %pad_maximum_fusion.6.refs_1_), channel_id=1, source_target_pairs={{0,16},{8,24},{16,0},{24,8},{1,17},{9,25},{17,1},{25,9},{2,18},{10... | collective-permute-start | bytes 1572872 | tf_op jit(solution)/shard_map/ppermute | solution.py:481
  163.4 122.7 %reduce-scatter.8.cloned.1.call-start = ((), (), s32[]{:S(2)}) async-start(), calls=%async_computation.13 | async-start | bytes 4718592 | tf_op jit(solution)/shard_map/reduce_scatter | solution.py:1742
  176.7 10.8 %collective-permute-start.12 = (bf16[256,1024]{1,0:T(8,128)(2,1)}, bf16[256,1024]{1,0:T(8,128)(2,1)S(1)}, u32[]{:S(2)}, u32[]{:S(2)}) collective-permute-start(bf16[256,1024]{1,0:T(8,128)(2,1)} %get-tuple-element.108), channel_id=1, source_target_pairs={{0,16},{8,24},{16,0},{24,8},{1,17},{9,25},{17,1},{25,9},{2,18},{10... | collective-permute-start | bytes 1572872 | tf_op jit(solution)/shard_map/ppermute | solution.py:481
  176.8 13.3 %collective-permute-start.14 = (bf16[256,1024]{1,0:T(8,128)(2,1)}, bf16[256,1024]{1,0:T(8,128)(2,1)S(1)}, u32[]{:S(2)}, u32[]{:S(2)}) collective-permute-start(bf16[256,1024]{1,0:T(8,128)(2,1)} %get-tuple-element.110), channel_id=1, source_target_pairs={{0,8},{8,0},{16,24},{24,16},{1,9},{9,1},{17,25},{25,17},{2,10},{10... | collective-permute-start | bytes 1572872 | tf_op jit(solution)/shard_map/ppermute | solution.py:481
  188.6 13.3 %collective-permute-start.13 = (bf16[128,1024]{1,0:T(8,128)(2,1)S(1)}, bf16[128,1024]{1,0:T(8,128)(2,1)S(1)}, u32[]{:S(2)}, u32[]{:S(2)}) collective-permute-start(bf16[128,1024]{1,0:T(8,128)(2,1)S(1)} %slice_add_fusion.3), channel_id=1, source_target_pairs={{0,8},{8,0},{16,24},{24,16},{1,9},{9,1},{17,25},{25,17},{2,10},{10... | collective-permute-start | bytes 786440 | tf_op jit(solution)/shard_map/ppermute | solution.py:481
  201.8 115.6 %reduce-scatter.6.cloned.1.call-start = ((), (), s32[]{:S(2)}) async-start(), calls=%async_computation.12 | async-start | bytes 2654208 | tf_op jit(solution)/shard_map/reduce_scatter | solution.py:1773
  208.7 10.8 %collective-permute-start.17 = (bf16[256,512]{1,0:T(8,128)(2,1)}, bf16[256,512]{1,0:T(8,128)(2,1)S(1)}, u32[]{:S(2)}, u32[]{:S(2)}) collective-permute-start(bf16[256,512]{1,0:T(8,128)(2,1)} %get-tuple-element.117), channel_id=1, source_target_pairs={{0,16},{8,24},{16,0},{24,8},{1,17},{9,25},{17,1},{25,9},{2,18},{10... | collective-permute-start | bytes 786440 | tf_op jit(solution)/shard_map/ppermute | solution.py:481
  219.5 15.2 %collective-permute-start.19 = (bf16[256,1024]{1,0:T(8,128)(2,1)}, bf16[256,1024]{1,0:T(8,128)(2,1)S(1)}, u32[]{:S(2)}, u32[]{:S(2)}) collective-permute-start(bf16[256,1024]{1,0:T(8,128)(2,1)} %get-tuple-element.129), channel_id=1, source_target_pairs={{0,16},{8,24},{16,0},{24,8},{1,17},{9,25},{17,1},{25,9},{2,18},{10... | collective-permute-start | bytes 1572872 | tf_op jit(solution)/shard_map/ppermute | solution.py:481
  220.8 13.9 %collective-permute-start.20 = (bf16[256,1024]{1,0:T(8,128)(2,1)}, bf16[256,1024]{1,0:T(8,128)(2,1)S(1)}, u32[]{:S(2)}, u32[]{:S(2)}) collective-permute-start(bf16[256,1024]{1,0:T(8,128)(2,1)} %get-tuple-element.130), channel_id=1, source_target_pairs={{0,8},{8,0},{16,24},{24,16},{1,9},{9,1},{17,25},{25,17},{2,10},{10... | collective-permute-start | bytes 1572872 | tf_op jit(solution)/shard_map/ppermute | solution.py:481
  234.7 15.0 %collective-permute-start.22 = (bf16[128,1024]{1,0:T(8,128)(2,1)S(1)}, bf16[128,1024]{1,0:T(8,128)(2,1)S(1)}, u32[]{:S(2)}, u32[]{:S(2)}) collective-permute-start(bf16[128,1024]{1,0:T(8,128)(2,1)S(1)} %slice_add_fusion.4), channel_id=1, source_target_pairs={{0,16},{8,24},{16,0},{24,8},{1,17},{9,25},{17,1},{25,9},{2,18},{10... | collective-permute-start | bytes 786440 | tf_op jit(solution)/shard_map/ppermute | solution.py:481
  236.8 12.9 %collective-permute-start.21 = (bf16[128,1024]{1,0:T(8,128)(2,1)S(1)}, bf16[128,1024]{1,0:T(8,128)(2,1)S(1)}, u32[]{:S(2)}, u32[]{:S(2)}) collective-permute-start(bf16[128,1024]{1,0:T(8,128)(2,1)S(1)} %slice_add_fusion.5), channel_id=1, source_target_pairs={{0,8},{8,0},{16,24},{24,16},{1,9},{9,1},{17,25},{25,17},{2,10},{10... | collective-permute-start | bytes 786440 | tf_op jit(solution)/shard_map/ppermute | solution.py:481
  255.4 11.0 %collective-permute-start.23 = (bf16[256,1024]{1,0:T(8,128)(2,1)}, bf16[256,1024]{1,0:T(8,128)(2,1)S(1)}, u32[]{:S(2)}, u32[]{:S(2)}) collective-permute-start(bf16[256,1024]{1,0:T(8,128)(2,1)} %get-tuple-element.142), channel_id=1, source_target_pairs={{0,16},{8,24},{16,0},{24,8},{1,17},{9,25},{17,1},{25,9},{2,18},{10... | collective-permute-start | bytes 1572872 | tf_op jit(solution)/shard_map/ppermute | solution.py:481
  256.1 14.6 %collective-permute-start.25 = (bf16[256,1024]{1,0:T(8,128)(2,1)}, bf16[256,1024]{1,0:T(8,128)(2,1)S(1)}, u32[]{:S(2)}, u32[]{:S(2)}) collective-permute-start(bf16[256,1024]{1,0:T(8,128)(2,1)} %get-tuple-element.144), channel_id=1, source_target_pairs={{0,8},{8,0},{16,24},{24,16},{1,9},{9,1},{17,25},{25,17},{2,10},{10... | collective-permute-start | bytes 1572872 | tf_op jit(solution)/shard_map/ppermute | solution.py:481
  267.5 13.0 %collective-permute-start.24 = (bf16[128,1024]{1,0:T(8,128)(2,1)S(1)}, bf16[128,1024]{1,0:T(8,128)(2,1)S(1)}, u32[]{:S(2)}, u32[]{:S(2)}) collective-permute-start(bf16[128,1024]{1,0:T(8,128)(2,1)S(1)} %slice_add_fusion.1), channel_id=1, source_target_pairs={{0,8},{8,0},{16,24},{24,16},{1,9},{9,1},{17,25},{25,17},{2,10},{10... | collective-permute-start | bytes 786440 | tf_op jit(solution)/shard_map/ppermute | solution.py:481
  289.3 12.1 %collective-permute-start.27 = (bf16[64,3072]{1,0:T(8,128)(2,1)S(1)}, bf16[64,3072]{1,0:T(8,128)(2,1)S(1)}, u32[]{:S(2)}, u32[]{:S(2)}) collective-permute-start(bf16[64,3072]{1,0:T(8,128)(2,1)S(1)} %get-tuple-element.173), channel_id=1, source_target_pairs={{0,8},{8,0},{16,24},{24,16},{1,9},{9,1},{17,25},{25,17},{2,10},{10... | collective-permute-start | bytes 1179656 | tf_op jit(solution)/shard_map/ppermute | solution.py:481
  290.2 12.4 %collective-permute-start.29 = (bf16[64,3072]{1,0:T(8,128)(2,1)S(1)}, bf16[64,3072]{1,0:T(8,128)(2,1)S(1)}, u32[]{:S(2)}, u32[]{:S(2)}) collective-permute-start(bf16[64,3072]{1,0:T(8,128)(2,1)S(1)} %get-tuple-element.172), channel_id=1, source_target_pairs={{0,16},{8,24},{16,0},{24,8},{1,17},{9,25},{17,1},{25,9},{2,18},{10... | collective-permute-start | bytes 1179656 | tf_op jit(solution)/shard_map/ppermute | solution.py:481
  301.5 16.0 %collective-permute-start.28 = (bf16[128,3072]{1,0:T(8,128)(2,1)S(1)}, bf16[128,3072]{1,0:T(8,128)(2,1)S(1)}, u32[]{:S(2)}, u32[]{:S(2)}) collective-permute-start(bf16[128,3072]{1,0:T(8,128)(2,1)S(1)} %pad_maximum_fusion.lower), channel_id=1, source_target_pairs={{0,16},{8,24},{16,0},{24,8},{1,17},{9,25},{17,1},{25,9},{2,18},{10... | collective-permute-start | bytes 2359304 | tf_op jit(solution)/shard_map/ppermute | solution.py:481
  302.7 14.8 %collective-permute-start.30 = (bf16[128,3072]{1,0:T(8,128)(2,1)S(1)}, bf16[128,3072]{1,0:T(8,128)(2,1)S(1)}, u32[]{:S(2)}, u32[]{:S(2)}) collective-permute-start(bf16[128,3072]{1,0:T(8,128)(2,1)S(1)} %pad_maximum_fusion.1.upper), channel_id=1, source_target_pairs={{0,8},{8,0},{16,24},{24,16},{1,9},{9,1},{17,25},{25,17},{2,10},{10... | collective-permute-start | bytes 2359304 | tf_op jit(solution)/shard_map/ppermute | solution.py:481
  303.8 32.3 %all-to-all-start.3 = ((bf16[8,64,1024]{2,1,0:T(8,128)(2,1)}), bf16[8,64,1024]{2,1,0:T(8,128)(2,1)}, u32[]{:S(2)}, u32[]{:S(2)}) async-start(bf16[8,64,1024]{2,1,0:T(8,128)(2,1)} %own_last.1), calls=%async_computation.4 | async-start | bytes 2097152 | tf_op jit(solution)/shard_map/all_to_all | solution.py:1779
  325.0 11.1 %collective-permute-start.32 = (bf16[128,1152]{1,0:T(8,128)(2,1)S(1)}, bf16[128,1152]{1,0:T(8,128)(2,1)S(1)}, u32[]{:S(2)}, u32[]{:S(2)}) collective-permute-start(bf16[128,1152]{1,0:T(8,128)(2,1)S(1)} %pad_maximum_fusion.8.lower), channel_id=1, source_target_pairs={{0,16},{8,24},{16,0},{24,8},{1,17},{9,25},{17,1},{25,9},{2,18},{10... | collective-permute-start | bytes 884744 | tf_op jit(solution)/shard_map/ppermute | solution.py:481
  336.9 17.4 %all-to-all-start.4 = ((bf16[4,2,64,1024]{3,2,1,0:T(8,128)(2,1)}), bf16[4,2,64,1024]{3,2,1,0:T(8,128)(2,1)S(1)}, u32[]{:S(2)}, u32[]{:S(2)}) async-start(bf16[4,2,64,1024]{3,2,1,0:T(8,128)(2,1)} %bitcast.16), calls=%async_computation.7 | async-start | bytes 2097152 | tf_op jit(solution)/shard_map/all_to_all | solution.py:1787
  (55 other events, 547.3 us)
Sparse Core Ops, SparseCore 0:
  11.3 60.0 all-gather.3
  73.6 57.0 all-gather.5
  132.3 27.7 all-gather.7
  163.5 34.0 reduce-scatter.3
  201.9 47.7 reduce-scatter.7
  280.6 36.8 reduce-scatter.5
where the time goes:
time: 364 us; the launch traced here: 363 us
  Pallas kernels  132 us (36%)
  waiting for transfers between devices  110 us (30%)
  starting transfers between devices  60.6 us (17%)
  blocking collectives  20.7 us (6%)
  local copies, waits for them, and re-layouts  16.2 us (4%)
  between operations  14.9 us (4%)
  other arithmetic  8.84 us (2%)
    pallas_call x15, Pallas kernels, run(): pl.pallas_call(kernel, out_shape=out_shapes, in_specs=in_specs, out_specs...  123 us
    ppermute x35, waiting for transfers between devices, swap(): return lax.ppermute(value, 'batch', [(i, i ^ bit) for i in range(4)])  62.2 us
    ppermute x35, starting transfers between devices, swap(): return lax.ppermute(value, 'batch', [(i, i ^ bit) for i in range(4)])  44 us
    all_to_all x2, waiting for transfers between devices, over_seq(): lax.all_to_all(pieces, 'seq', 0, 0, tiled=True)  29.7 us
    all_to_all x1, blocking collectives, on_plane(): packed = lax.all_to_all(packed, 'batch', 0, 0, tiled=True)  20.7 us
    reduce_scatter x1, waiting for transfers between devices, on_plane(): lax.psum_scatter(first_weight_grads, 'seq', scatter_dimension=0, tiled=True)  9.4 us
    pallas_call x2, Pallas kernels, call(): pl.pallas_call(kernel, grid=(1,), out_shape=[jax.ShapeDtypeStruct(shape,...  8.62 us
    all_to_all x2, starting transfers between devices, over_seq(): lax.all_to_all(pieces, 'seq', 0, 0, tiled=True)  8.43 us
  transfers between devices with their start and end apart: 45, of which 15 were waited for; matrix products, arithmetic and copies ran while one was open for 5% of the time, Pallas kernels for 35%

commit v1 on v0

--- a/solution.py
+++ b/solution.py
@@ -779,6 +779,30 @@
     )(*args)
 
 
+def output_weights(pieces):
+    rows = pieces[0].shape[0] // 2
+    places = {
+        0: ((0, 0), (0, 1), (1, 0), (1, 1)),
+        1: ((2, 0), (3, 0), (2, 1), (3, 1)),
+    }
+
+    def pairs(refs, buffer):
+        rank = lax.axis_index("batch")
+        out = []
+        for half in range(2):
+            for r, (which, part) in enumerate(places[half]):
+                to = pl.ds(pl.multiple_of((rank ^ r) * 256, 256), 256)
+                out.append(
+                    (
+                        refs[which].at[pl.ds(part * rows, rows)],
+                        buffer.at[pl.ds(half * rows, rows), to],
+                    )
+                )
+        return out
+
+    return Plan(list(pieces), (2 * rows, D), pairs, 8)
+
+
 def start_all(*items):
     for item in items:
         item.start()
@@ -789,10 +813,10 @@
 
 
 def pack_body(
-    rank_ref, x, cot, segment_ref, variate_ref, position_ref, wo, wq, wk, wv, gain_first_ref,
+    rank_ref, x, cot, segment_ref, variate_ref, position_ref, wq, wk, wv, wo, gain_first_ref,
     gain_second_ref, gate, up, down, rows_out, shard_out, gate_up_out, down_out,
 ):
-    start_all(wo, wq, wk, wv, x, cot, gate, up, down)
+    start_all(wq, wk, wv, wo, x, cot, gate, up, down)
     micro, _, quarter, _ = x.ref.shape
     tokens = 4 * quarter
     lane = lax.broadcasted_iota(jnp.int32, (tokens, 128), 1)
@@ -806,10 +830,9 @@
         upright(gain_first_ref[...].astype(WIDE)),
         jnp.where(lane == 1, upright(gain_second_ref[...].astype(WIDE)), 0.0),
     )
-    shard_out.ref[:, D + 768 :] = gains.astype(LOW)
-    shard_out.ref[:, :D] = wo.wait()[...]
-    for place, weight in enumerate((wq, wk, wv)):
-        shard_out.ref[:, D + 256 * place : D + 256 * (place + 1)] = weight.wait()[...]
+    shard_out.ref[:, D:] = gains.astype(LOW)
+    for place, weight in enumerate((wq, wk, wv, wo)):
+        shard_out.ref[:, 256 * place : 256 * (place + 1)] = weight.wait()[...]
     shard_out.start()
     for m in range(micro):
         places = position_ref[m : m + 1, :]
@@ -885,12 +908,11 @@
         "pack",
         4,
         [rank, whole(quarters(x)), whole(quarters(cot)), segments, variates, positions]
-        + [whole(shards[0])]
-        + [rank_columns(weight) for weight in shards[1:]]
+        + [rank_columns(weight) for weight in shards]
         + [*gains, feed_columns(w_gate), feed_columns(w_up), down_rows(w_down)],
         [
             out_whole((4, 2, micro, quarter, D + 128), LOW),
-            out_whole((shard, D + 896), LOW),
+            out_whole((shard, D + 128), LOW),
             out_whole((shard, ff // 2), LOW),
             out_whole((piece, D), LOW),
         ],
@@ -1015,8 +1037,8 @@
         15,
         [
             group(chunks),
-            whole(first_weights, D, 768),
-            whole(first_weights, D + 768, 128),
+            whole(first_weights, 0, 768),
+            whole(first_weights, D, 128),
             freqs,
             weights,
         ],
@@ -1038,7 +1060,7 @@
     )
 
 
-def middle_body(rank_ref, x, near, far, wo, gain_ref, heads, own_ref, mixed):
+def middle_body(rank_ref, x, near, far, wo, gain_ref, heads, own, mixed):
     rank = rank_ref[0]
     start_all(near, far, wo, x)
     count, chunk, _ = x.ref.shape
@@ -1073,7 +1095,8 @@
 
         @pl.when(index % 2 == 0)
         def _():
-            own_ref[pl.ds(pl.multiple_of(index // 2 * block, block), block), :] = total[:block]
+            own.ref[index // 2] = total[:block]
+            own.start_at(index // 2)
 
         mixed.ref[index] = (total * unit_rows(total) * gain_ref[1:2, :]).astype(LOW)
         mixed.start_at(index)
@@ -1082,7 +1105,7 @@
     lax.fori_loop(0, count, one_chunk, 0)
 
 
-def middle(rank, chunks, heads, first_weights, gain):
+def middle(rank, chunks, heads, out_pieces, gain):
     chunk = chunks[0].shape[0]
     length = 4 * chunk
     lower, lower_x, lower_far, upper, upper_y, upper_far = heads
@@ -1095,10 +1118,10 @@
             group(chunks),
             group((lower, upper, lower_x, upper_y)),
             group((lower_far, upper_far)),
-            whole(first_weights, 0, D),
+            output_weights(out_pieces),
             gain,
         ],
-        [out_rows((length, D), LOW), ((chunk, D), WIDE), out_rows((length, D), LOW)],
+        [out_rows((length, D), LOW), out_rows((chunk, D), WIDE, 2), out_rows((length, D), LOW)],
     )
 
 
@@ -1146,39 +1169,41 @@
     cots.start(0)
     both.start(0)
     gate_up.start()
-    for k in range(1, 4):
-        cots.start(k)
-        both.start(k)
-    count, _, _ = cots.ref.shape
+    cots.start(1)
+    both.start(1)
     per = down.ref.shape[0]
 
     def one_chunk(index, carry):
         cots.wait_at(index)
         both.wait_at(index)
         grad_hidden = dot_rows(cots.ref[index], down.wait_first(index)[...])
-        grads.ref[index, :, :per] = (
-            grad_hidden * both.ref[index, :, :per].astype(WIDE)
-        ).astype(LOW)
-        grads.ref[index, :, per:] = (
-            grad_hidden * both.ref[index, :, per:].astype(WIDE)
-        ).astype(LOW)
+        grads.ref[index, :, :per] = (grad_hidden * both.ref[index, :, :per].astype(WIDE)).astype(LOW)
+        grads.ref[index, :, per:] = (grad_hidden * both.ref[index, :, per:].astype(WIDE)).astype(LOW)
         grads.start_at(index)
         back.ref[index] = dot_rows(grads.ref[index], gate_up.wait_first(index)[...]).astype(LOW)
         back.start_at(index)
         return carry
 
-    lax.fori_loop(0, count, one_chunk, 0)
-
-
-def feed_back(both, cots, gate_up, down, token):
+    lax.fori_loop(0, 2, one_chunk, 0)
+
+
+def feed_back(first, both, cots, gate_up, down, token):
     length = both.shape[0]
+    chunk = length // 4
     per = down.shape[0]
+
+    def pairs(refs, buffer):
+        return [
+            (refs[0].at[pl.ds((first + 2 * k) * chunk, chunk)], buffer.at[k]) for k in range(2)
+        ]
+
     return run(
         feed_back_body,
         "feed_back",
-        11,
-        [rows_of(both), group(cots), whole(gate_up), whole(down)],
-        [out_rows((length, 2 * per), LOW), out_group((length // 4, D), LOW)],
+        7,
+        [Plan([both], (2, chunk, 2 * per), pairs, 2), group((cots[first], cots[first + 2]))]
+        + [whole(gate_up), whole(down)],
+        [out_rows((length // 2, 2 * per), LOW, 2), out_group((chunk, D), LOW, 2)],
         token=token,
     )
 
@@ -1218,14 +1243,14 @@
         parcels.ref[q, :, width:] = grad.ref[:, place].astype(LOW)
 
 
-def own_back(rank, sums, middle_own, cot_own, gain, first_weights, token):
+def own_back(rank, sums, middle_own, cot_own, gain, out_pieces, token):
     quarter = cot_own.shape[0]
     return run(
         own_back_body,
         "own_back",
         4,
         [rank, *arrivals(sums), whole(middle_own), whole(cot_own), gain]
-        + [whole(first_weights, 0, D)],
+        + [output_weights(out_pieces)],
         [out_whole((quarter, D), WIDE), out_group((quarter, 512), LOW)],
         token=token,
     )
@@ -1233,9 +1258,16 @@
 
 def attend_back_body(
     pair, parcels, q, k, v, wide, logs, cos, sin, query_sides, key_sides, weights_ref,
-    out, bias_ref, queries_ref, grads_ref, total_ref,
+    *rest,
 ):
+    if pair == 1:
+        before, projections, out, bias_ref, back, *rest, joined_ref = rest
+    else:
+        out, bias_ref, *rest = rest
+    queries_ref, grads_ref, total_ref = rest
     start_all(parcels, q, query_sides, logs, wide, k, v, key_sides, cos, sin)
+    if pair == 1:
+        start_all(before, projections)
     length = q.ref.shape[0]
     chunk = length // 4
     block = chunk // 2
@@ -1322,9 +1354,24 @@
         out.ref[place, :, :128] = turn_pair(
             total_ref[rows, :] * SCORE_SCALE, cos_ref[rows, :], -sin_ref[rows, :]
         ).astype(LOW)
-
-
-def attend_back(pair, parcels, kept, weights, token):
+    if pair == 0:
+        return
+    out.start()
+    before_ref, projections_ref = before.wait(), projections.wait()
+
+    def one_chunk(index, carry):
+        for kind in range(3):
+            here = slice(128 * kind, 128 * (kind + 1))
+            joined_ref[:, 256 * kind : 256 * kind + 128] = before_ref[index, :, here]
+            joined_ref[:, 256 * kind + 128 : 256 * (kind + 1)] = out.ref[index, :, here]
+        back.ref[index] = dot_rows(joined_ref[...], projections_ref[...]).astype(LOW)
+        back.start_at(index)
+        return carry
+
+    lax.fori_loop(0, 4, one_chunk, 0)
+
+
+def attend_back(pair, parcels, kept, weights, token, before=None, first_weights=None):
     turned, attended, *others = kept
     length = turned.shape[0]
     at = 128 * pair
@@ -1336,44 +1383,16 @@
         + [whole(turned, column + at, 128) for column in (0, 256, 512)]
         + [whole(attended, at, 128)]
         + [whole(x) for x in others]
-        + [weights],
-        [out_rows((length, 384), LOW), ((8, 128), WIDE)],
+        + [weights]
+        + ([rows_of(before), whole(first_weights, 0, 768)] if pair else []),
+        [out_rows((length, 384), LOW), ((8, 128), WIDE)]
+        + ([out_group((length // 4, D), LOW)] if pair else []),
         [
             pltpu.VMEM((2, length, 256), LOW),
             pltpu.VMEM((2, length, 256), LOW),
             pltpu.VMEM((length, 128), WIDE),
-        ],
-        token,
-    )
-
-
-def project_back_body(proj0, proj1, weights, back, joined_ref):
-    start_all(proj0, proj1, weights)
-    proj = (proj0.wait(), proj1.wait())
-    weights_ref = weights.wait()
-
-    def one_chunk(index, carry):
-        for kind in range(3):
-            for pair in range(2):
-                joined_ref[:, 256 * kind + 128 * pair : 256 * kind + 128 * (pair + 1)] = proj[pair][
-                    index, :, 128 * kind : 128 * (kind + 1)
-                ]
-        back.ref[index] = dot_rows(joined_ref[...], weights_ref[...]).astype(LOW)
-        back.start_at(index)
-        return carry
-
-    lax.fori_loop(0, back.ref.shape[0], one_chunk, 0)
-
-
-def project_back(proj0, proj1, first_weights, token):
-    length = proj0.shape[0]
-    return run(
-        project_back_body,
-        "project_back",
-        5,
-        [rows_of(proj0), rows_of(proj1), whole(first_weights, D, 768)],
-        [out_group((length // 4, D), LOW)],
-        [pltpu.VMEM((length // 4, 768), LOW)],
+        ]
+        + ([pltpu.VMEM((length // 4, 768), LOW)] if pair else []),
         token,
     )
 
@@ -1397,7 +1416,7 @@
     lax.fori_loop(0, hidden.ref.shape[0], one_part, 0)
 
 
-def down_grads(hidden, cots):
+def down_grads(hidden, cots, token):
     per = hidden.shape[1]
     return run(
         down_grads_body,
@@ -1405,29 +1424,37 @@
         5,
         [columns_of(hidden), group(cots)],
         [out_rows((per, D), LOW)],
+        token=token,
     )[0]
 
 
-def gate_up_grads_body(mixed, grads, out):
-    start_all(grads, mixed)
+def gate_up_grads_body(mixed, near, far, out):
+    start_all(near, far, mixed)
+    chunk = mixed.ref.shape[1] // 4
 
     def one_part(index, carry):
-        grads_ref = grads.wait_first(index)
+        near_ref, far_ref = near.wait_first(index), far.wait_first(index)
         mixed.wait_at(index)
-        out.ref[index] = dot_first(mixed.ref[index], grads_ref[...]).astype(LOW)
+        total = None
+        for k in range(4):
+            more = dot_first(
+                mixed.ref[index, k * chunk : (k + 1) * chunk, :], (near_ref, far_ref)[k % 2][k // 2]
+            )
+            total = more if total is None else total + more
+        out.ref[index] = total.astype(LOW)
         out.start_at(index)
         return carry
 
     lax.fori_loop(0, mixed.ref.shape[0], one_part, 0)
 
 
-def gate_up_grads(mixed, grads, token):
+def gate_up_grads(mixed, near, far, token):
     return run(
         gate_up_grads_body,
         "gate_up_grads",
         8,
-        [columns_of(mixed), whole(grads)],
-        [out_rows((D, grads.shape[1]), LOW)],
+        [columns_of(mixed), rows_of(near, 2), rows_of(far, 2)],
+        [out_rows((D, near.shape[1]), LOW)],
         token=token,
     )[0]
 
@@ -1505,7 +1532,7 @@
     return run(
         join_body,
         "join",
-        100,
+        1,
         [whole(left), whole(right)],
         [out_whole((rows, left.shape[1] + right.shape[1]), LOW)],
         token=token,
@@ -1694,7 +1721,7 @@
         segment_ids.reshape(micro, tokens),
         variate_ids.reshape(micro, tokens),
         positions.reshape(micro, tokens),
-        (w_output, w_query, w_key, w_value),
+        (w_query, w_key, w_value, w_output),
         (gain_attention.reshape(1, shard), gain_feed.reshape(1, shard)),
         w_gate,
         w_up,
@@ -1708,17 +1735,25 @@
         packed[:, kind].reshape(4 * micro, tokens // 4, D + 128)[:, :, : D + 128 - 128 * kind]
         for kind in range(2)
     ]
-    mine, cot_by_sequence = lax.optimization_barrier((over_seq(by_sequence[0]), by_sequence[1]))
+    out_columns = first_weights[:, 768:D]
+    out_got = swap_pairs(out_columns)
+    mine, cot_by_sequence, out_got = lax.optimization_barrier(
+        (over_seq(by_sequence[0]), by_sequence[1], out_got)
+    )
     cot_mine = over_seq(cot_by_sequence)
     freqs = jnp.exp((jnp.arange(128) % 32).astype(WIDE) * (-2.0 * math.log(10000.0) / HD))[None, :]
     my_bias = lax.dynamic_slice_in_dim(variate_bias, rank * 4, 4, 1)
     weights = jnp.pad(head_weights(my_bias[0], my_bias[1]), ((0, 4), (0, 0)))
 
     chunks = gather_plane(mine)
+    out_pieces = far_pairs(
+        out_columns, lax.optimization_barrier((out_got, chunks[1], chunks[3]))[0]
+    )
     gain, mixed_first, turned, attended, lower, upper, *kept = attend(
         chunks, first_weights, freqs, weights, rank_row
     )
-    lower_x, upper_y = swap(lower, 1), swap(upper, 2)
+    ready = lax.optimization_barrier((lower, upper, out_pieces[1], out_pieces[3]))
+    lower_x, upper_y = swap(ready[0], 1), swap(ready[1], 2)
     lower_far = swap(jnp.concatenate([lower, lower_x], 1), 2)
     upper_far = swap(jnp.concatenate([upper, upper_y], 1), 1)
     cot_got = swap_pairs(lax.optimization_barrier((cot_mine, lower_far, upper_far))[0])
@@ -1726,25 +1761,31 @@
         rank_row,
         chunks,
         (lower, lower_x, lower_far, upper, upper_y, upper_far),
-        first_weights,
+        out_pieces,
         gain,
     )
 
     both, hidden = feed(mixed_second, gate_up, after(rank_row, cot_got))
     cots = far_pairs(cot_mine, lax.optimization_barrier((cot_got, mixed_second))[0])
-    down_weight_grads = down_grads(hidden, cots)
+    down_weight_grads = down_grads(hidden, cots, rank_row)
     down_grad_shard = lax.psum_scatter(down_weight_grads, "seq", scatter_dimension=0, tiled=True)
-    grad_gate_up, *back = feed_back(
-        both, cots, gate_up, down, after(rank_row, down_weight_grads)
-    )
-    got = scatter_first(back)
-    gate_up_weight_grads = gate_up_grads(mixed_second, grad_gate_up, after(rank_row, got))
+    far_grads, far_lower, far_upper = feed_back(
+        1, both, cots, gate_up, down, after(rank_row, down_weight_grads)
+    )
+    got = scatter_first((None, far_lower, None, far_upper))
+    near_grads, near_lower, near_upper = feed_back(
+        0, both, cots, gate_up, down, after(rank_row, far_lower)
+    )
+    back = (near_lower, None, near_upper, None)
+    gate_up_weight_grads = gate_up_grads(
+        mixed_second, near_grads, far_grads, after(rank_row, got)
+    )
     gate_up_grad_shard = lax.psum_scatter(
         gate_up_weight_grads, "seq", scatter_dimension=0, tiled=True
     )
     sums = scatter_second(back, got)
     grad_middle, *parcels = own_back(
-        rank_row, sums, middle_own, cot_mine, gain, first_weights,
+        rank_row, sums, middle_own, cot_mine, gain, out_pieces,
         after(rank_row, gate_up_weight_grads),
     )
     out_chunks = feed_out(hidden, down, after(rank_row, parcels[0]))
@@ -1754,15 +1795,15 @@
     out_got = scatter_first((None, far_chunks[0], None, far_chunks[1]))
     kept = (turned, attended, *kept)
     proj0, bias0 = attend_back(
-        0, parcels, kept, weights, after(rank_row, far_chunks, down_grad_shard)
+        0, parcels, kept, weights, after(rank_row, far_chunks)
     )
     out_got = lax.optimization_barrier((out_got, bias0))[0]
     out_sums = scatter_second(out_chunks, out_got)
-    proj1, bias1 = attend_back(1, parcels, kept, weights, after(rank_row, out_got))
-    back = project_back(
-        proj0, proj1, first_weights, after(rank_row, out_sums[2], out_sums[5])
-    )
-    got = scatter_first(back)
+    proj1, bias1, *back = attend_back(
+        1, parcels, kept, weights, after(rank_row, out_got), proj0, first_weights
+    )
+    ready = lax.optimization_barrier((back[1], back[3], out_sums[2], out_sums[5]))
+    got = scatter_first((None, ready[0], None, ready[1]))
     bias_sums = jnp.sum(jnp.concatenate([bias0[:2], bias1[:2], bias0[2:4], bias1[2:4]], 0), 1)
     bias_parts = jnp.pad(jnp.concatenate(three_parts(bias_sums)), (0, 104))[None, :]
     slots = lax.broadcasted_iota(jnp.int32, (per, 1), 0) % shard == lax.axis_index("seq")
@@ -1770,7 +1811,7 @@
     first_weight_grads = first_grads(
         rank_row, mixed_first, proj0, proj1, heads, parcels, bias_rows, after(rank_row, got)
     )
-    first_grad_shard = lax.psum_scatter(first_weight_grads, "seq", scatter_dimension=0, tiled=True)
+    first_shard = lax.psum_scatter(first_weight_grads, "seq", scatter_dimension=0, tiled=True)
     sums = scatter_second(back, got)
     last = own_last(
         sums, out_sums, mine, grad_middle, middle_own, gain, n_seq,
@@ -1778,10 +1819,9 @@
     )
     moved = lax.all_to_all(last, "seq", 0, 0, tiled=True)
     quarter = tokens // 4
-    feed_pieces = gather_plane(
-        join(gate_up_grad_shard, down_grad_shard, after(rank_row, last))
-    )
-    first_pieces = gather_plane(after(first_grad_shard, feed_pieces))
+    feed_shard = join(gate_up_grad_shard, down_grad_shard, after(rank_row, first_weight_grads))
+    feed_pieces = gather_plane(after(feed_shard, last))
+    first_pieces = gather_plane(after(first_shard, feed_pieces))
     moved, first_pieces = lax.optimization_barrier((moved, first_pieces))
     moved = moved.reshape(4, micro, 2 * quarter, D)
     moved = lax.all_to_all(moved, "batch", 0, 0, tiled=True)

time: 364 us -> 350 us (0.962)
  waiting for transfers between devices: 110 us -> 90.1 us
  starting transfers between devices: 60.6 us -> 66.3 us
    all_to_all x2, waiting for transfers between devices: 29.7 us -> 3.49 us  [over_seq(): lax.all_to_all(pieces, 'seq', 0, 0, tiled=True)]
    all_gather x1, waiting for transfers between devices: 0.01 us -> 8.8 us  [on_plane(): first_weights = lax.all_gather(first_shard, 'seq', axis=0, tiled=True)]
    reduce_scatter x1, waiting for transfers between devices: 9.4 us -> 17.2 us  [on_plane(): lax.psum_scatter(first_weight_grads, 'seq', scatter_dimension=0, tiled=True)]
    ppermute x35 -> x39, waiting for transfers between devices: 62.2 us -> 54.9 us  [swap(): return lax.ppermute(value, 'batch', [(i, i ^ bit) for i in range(4)])]
    ppermute x35 -> x39, starting transfers between devices: 44 us -> 47.9 us  [swap(): return lax.ppermute(value, 'batch', [(i, i ^ bit) for i in range(4)])]
  transfers between devices with their start and end apart: 45 -> 49, of which waited for: 15 -> 23; matrix products, arithmetic and copies ran while one was open for 5% -> 6% of each run, Pallas kernels for 35% -> 36%
where the time goes in v1:
time: 350 us; the launch traced here: 349 us
  Pallas kernels  131 us (37%)
  waiting for transfers between devices  90.1 us (26%)
  starting transfers between devices  66.3 us (19%)
  blocking collectives  20.7 us (6%)
  local copies, waits for them, and re-layouts  16.9 us (5%)
  between operations  14.9 us (4%)
  other arithmetic  8.92 us (3%)
    pallas_call x15, Pallas kernels, run(): pl.pallas_call(kernel, out_shape=out_shapes, in_specs=in_specs, out_specs...  122 us
    ppermute x39, waiting for transfers between devices, swap(): return lax.ppermute(value, 'batch', [(i, i ^ bit) for i in range(4)])  54.9 us
    ppermute x39, starting transfers between devices, swap(): return lax.ppermute(value, 'batch', [(i, i ^ bit) for i in range(4)])  47.9 us
    all_to_all x1, blocking collectives, on_plane(): packed = lax.all_to_all(packed, 'batch', 0, 0, tiled=True)  20.7 us
    reduce_scatter x1, waiting for transfers between devices, on_plane(): lax.psum_scatter(first_weight_grads, 'seq', scatter_dimension=0, tiled=True)  17.2 us
    all_to_all x2, starting transfers between devices, over_seq(): lax.all_to_all(pieces, 'seq', 0, 0, tiled=True)  9.71 us
    all_gather x1, waiting for transfers between devices, on_plane(): first_weights = lax.all_gather(first_shard, 'seq', axis=0, tiled=True)  8.8 us
    pallas_call x2, Pallas kernels, call(): pl.pallas_call(kernel, grid=(1,), out_shape=[jax.ShapeDtypeStruct(shape,...  8.63 us
  transfers between devices with their start and end apart: 49, of which 23 were waited for; matrix products, arithmetic and copies ran while one was open for 6% of the time, Pallas kernels for 36%

profile of v1, /device:TPU:0, one launch (start us, length us, event | category | flops | bytes accessed | tf_op | source)
XLA Modules:
  0.0 349.0 jit_solution(9021530429902793510)
XLA Ops:
  7.2 3.9 %pack.1 = (bf16[4,2,2,32,1152]{4,3,2,1,0:T(8,128)(2,1)}, bf16[128,1152]{1,0:T(8,128)(2,1)}, bf16[128,2048]{1,0:T(8,128)(2,1)}, bf16[128,1024]{1,0:T(8,128)(2,1)}) custom-call(s32[1]{0:T(128)} %bitcast.refs_0_.refs_8_.refs_2_.refs_5_.refs_3_.refs_14_.refs_16_.refs_10_.rank_ref, bf16[2,4,32,1024]{3,2,1,0:T(8,128)(2,1)} %bitcast.57, ...), custom_call_target="tpu_custom_call" | custom-call | flops 4600000000 | bytes 1048576 | tf_op jit(solution)/shard_map/pack/pallas_call | solution.py:768
  11.9 20.7 %all_to_all.25 = bf16[4,2,2,32,1152]{4,3,2,1,0:T(8,128)(2,1)S(1)} all-to-all(bf16[4,2,2,32,1152]{4,3,2,1,0:T(8,128)(2,1)} %get-tuple-element.99), channel_id=1, replica_groups=mesh['batch'=4,'seq'=8] {'batch'}, dimensions={0} | all-to-all | bytes 2359296 | tf_op jit(solution)/shard_map/all_to_all | solution.py:1733
  33.6 4.9 %all-to-all-start.1 = ((bf16[8,32,1152]{2,1,0:T(8,128)(2,1)}), bf16[8,32,1152]{2,1,0:T(8,128)(2,1)S(1)}, u32[]{:S(2)}, u32[]{:S(2)}) async-start(bf16[8,32,1152]{2,1,0:T(8,128)(2,1)} %bitcast.8), calls=%async_computation.1 | async-start | bytes 1179648 | tf_op jit(solution)/shard_map/all_to_all | solution.py:523
  38.5 8.8 %all-gather.4.cloned.1.call-done.refs_4_.refs_5_.refs_15_ = bf16[1024,1152]{1,0:T(8,128)(2,1)} async-done(((bf16[128,1152]{1,0:T(8,128)(2,1)}), bf16[1024,1152]{1,0:T(8,128)(2,1)}) %all-gather.4.cloned.1.call-update) | async-done | bytes 2359312 | tf_op jit(solution)/shard_map/all_gather | solution.py:1730
  53.5 3.5 all-to-all-done.1
  61.3 6.1 %collective-permute-done.2 = bf16[128,1152]{1,0:T(8,128)(2,1)S(1)} collective-permute-done((bf16[128,1152]{1,0:T(8,128)(2,1)S(1)}, bf16[128,1152]{1,0:T(8,128)(2,1)S(1)}, u32[]{:S(2)}, u32[]{:S(2)}) %collective-permute-start.2) | collective-permute-done | bytes 294944 | tf_op jit(solution)/shard_map/ppermute | solution.py:481
  71.5 4.8 %all-to-all-start.2 = ((bf16[8,32,1024]{2,1,0:T(8,128)(2,1)}), bf16[8,32,1024]{2,1,0:T(8,128)(2,1)S(1)}, u32[]{:S(2)}, u32[]{:S(2)}) async-start(bf16[8,32,1024]{2,1,0:T(8,128)(2,1)} %slice.167), calls=%async_computation.2 | async-start | bytes 1048576 | tf_op jit(solution)/shard_map/all_to_all | solution.py:523
  76.3 5.1 %collective-permute-done.3.refs_1_.refs_2_ = bf16[256,1152]{1,0:T(8,128)(2,1)S(1)} collective-permute-done((bf16[256,1152]{1,0:T(8,128)(2,1)S(1)}, bf16[256,1152]{1,0:T(8,128)(2,1)S(1)}, u32[]{:S(2)}, u32[]{:S(2)}) %collective-permute-start.3) | collective-permute-done | bytes 589856 | tf_op jit(solution)/shard_map/ppermute | solution.py:481
  84.8 16.7 %attend.1 = (f32[16,1024]{1,0:T(8,128)}, bf16[1024,1024]{1,0:T(8,128)(2,1)}, bf16[1024,768]{1,0:T(8,128)(2,1)}, f32[1024,256]{1,0:T(8,128)}, bf16[512,256]{1,0:T...) custom-call(bf16[256,1152]{1,0:T(8,128)(2,1)} %copy-done.10, ...), custom_call_target="tpu_custom_call" | custom-call | flops 17250000896 | bytes 1048576 | tf_op jit(solution)/shard_map/attend/pallas_call | solution.py:768
  104.5 4.5 %collective-permute-done.8.refs_7_ = bf16[512,256]{1,0:T(8,128)(2,1)S(1)} collective-permute-done((bf16[512,256]{1,0:T(8,128)(2,1)}, bf16[512,256]{1,0:T(8,128)(2,1)S(1)}, u32[]{:S(2)}, u32[]{:S(2)}) %collective-permute-start.8) | collective-permute-done | bytes 262176 | tf_op jit(solution)/shard_map/ppermute | solution.py:481
  113.3 8.8 %collective-permute-done.10.refs_9_ = bf16[512,512]{1,0:T(8,128)(2,1)S(1)} collective-permute-done((bf16[512,512]{1,0:T(8,128)(2,1)S(1)}, bf16[512,512]{1,0:T(8,128)(2,1)S(1)}, u32[]{:S(2)}, u32[]{:S(2)}) %collective-permute-start.10) | collective-permute-done | bytes 524320 | tf_op jit(solution)/shard_map/ppermute | solution.py:481
  125.4 8.6 %middle.1 = (bf16[1024,1024]{1,0:T(8,128)(2,1)}, f32[256,1024]{1,0:T(8,128)}, bf16[1024,1024]{1,0:T(8,128)(2,1)}) custom-call(s32[1]{0:T(128)} %bitcast.refs_0_.refs_8_.refs_2_.refs_5_.refs_3_.refs_14_.refs_16_.refs_10_.rank_ref, bf16[256,1152]{1,0:T(8,128)(2,1)} %copy-done.10, bf16[256,1152]{1,0:T(8,128)(2,1)} %copy-done.28, bf16[256,1152]{1,0:T(8,128)(2,1)} %copy-done.11, ...), custom_call_target="tpu_custom_call" | custom-call | flops 8049999872 | bytes 1048576 | tf_op jit(solution)/shard_map/middle/pallas_call | solution.py:768
  135.6 9.3 %feed.1 = (bf16[1024,2048]{1,0:T(8,128)(2,1)}, bf16[1024,1024]{1,0:T(8,128)(2,1)}) custom-call(bf16[1024,1024]{1,0:T(8,128)(2,1)} %get-tuple-element.111.refs_0_, bf16[1024,2048]{1,0:T(8,128)(2,1)} %all-gather.6.cloned.1.call-done.refs_1_.refs_3_, s32[1]{0:T(128)} %bitcast.refs_0_.refs_8_.refs_2_.refs_5_.refs_3_.refs_14_.refs_16_.refs_10_.rank_ref), custom_call_target="tpu_custom_call" | custom-call | flops 9200000000 | bytes 1048576 | tf_op jit(solution)/shard_map/feed/pallas_call | solution.py:768
  145.8 5.8 %down_grads.1 = bf16[1024,1024]{1,0:T(8,128)(2,1)} custom-call(bf16[1024,1024]{1,0:T(8,128)(2,1)} %get-tuple-element.120.refs_0_, bf16[256,1024]{1,0:T(8,128)(2,1)} %copy-done.15, bf16[256,1024]{1,0:T(8,128)(2,1)} %copy-done.33, bf16[256,1024]{1,0:T(8,128)(2,1)} %copy-done.14, bf16[256,1024]{1,0:T(8,128)(2,1)} %copy-done.31, ...), custom_call_target="tpu_custom_call" | custom-call | flops 5750000128 | bytes 1048576 | tf_op jit(solution)/shard_map/down_grads/pallas_call | solution.py:768
  152.0 7.7 %feed_back.2 = (bf16[512,2048]{1,0:T(8,128)(2,1)}, bf16[256,1024]{1,0:T(8,128)(2,1)}, bf16[256,1024]{1,0:T(8,128)(2,1)}) custom-call(bf16[1024,2048]{1,0:T(8,128)(2,1)} %get-tuple-element.116.refs_0_, bf16[256,1024]{1,0:T(8,128)(2,1)} %copy-done.33, bf16[256,1024]{1,0:T(8,128)(2,1)} %copy-done.31, ...), custom_call_target="tpu_custom_call" | custom-call | flops 8049999872 | bytes 1048576 | tf_op jit(solution)/shard_map/feed_back/pallas_call | solution.py:768
  162.4 7.7 %feed_back.3 = (bf16[512,2048]{1,0:T(8,128)(2,1)}, bf16[256,1024]{1,0:T(8,128)(2,1)}, bf16[256,1024]{1,0:T(8,128)(2,1)}) custom-call(bf16[1024,2048]{1,0:T(8,128)(2,1)} %get-tuple-element.116.refs_0_, bf16[256,1024]{1,0:T(8,128)(2,1)} %copy-done.15, bf16[256,1024]{1,0:T(8,128)(2,1)} %copy-done.14, ...), custom_call_target="tpu_custom_call" | custom-call | flops 8049999872 | bytes 1048576 | tf_op jit(solution)/shard_map/feed_back/pallas_call | solution.py:768
  175.9 8.9 %gate_up_grads.1 = bf16[1024,2048]{1,0:T(8,128)(2,1)} custom-call(bf16[1024,1024]{1,0:T(8,128)(2,1)} %get-tuple-element.111.refs_0_, bf16[512,2048]{1,0:T(8,128)(2,1)} %get-tuple-element.128.refs_1_, bf16[512,2048]{1,0:T(8,128)(2,1)} %get-tuple-element.129.refs_2_, s32[1]{0:T(128)} %bitcast.refs_0_.refs_8_.refs_2_.refs_5_.refs_3_.refs_14_.refs_16_.refs_10_.rank_ref), custom_call_target="tpu_custom_call" | custom-call | flops 9200000000 | bytes 1048576 | tf_op jit(solution)/shard_map/gate_up_grads/pallas_call | solution.py:768
  185.8 5.7 %own_back.1 = (f32[256,1024]{1,0:T(8,128)}, bf16[256,512]{1,0:T(8,128)(2,1)}, bf16[256,512]{1,0:T(8,128)(2,1)}, bf16[256,512]{1,0:T(8,128)(2,1)}, bf16[256,512]{1,0:T(8,128)(2,1)}) custom-call(s32[1]{0:T(128)} %bitcast.refs_0_.refs_8_.refs_2_.refs_5_.refs_3_.refs_14_.refs_16_.refs_10_.rank_ref, bf16[256,1024]{1,0:T(8,128)(2,1)} %get-tuple-element.124.refs_1_, ...), custom_call_target="tpu_custom_call" | custom-call | flops 4600000000 | bytes 1048576 | tf_op jit(solution)/shard_map/own_back/pallas_call | solution.py:768
  195.1 5.9 %feed_out.1 = (bf16[256,1024]{1,0:T(8,128)(2,1)}, bf16[256,1024]{1,0:T(8,128)(2,1)}, bf16[256,1024]{1,0:T(8,128)(2,1)}, bf16[256,1024]{1,0:T(8,128)(2,1)}) custom-call(bf16[1024,1024]{1,0:T(8,128)(2,1)} %get-tuple-element.120.refs_0_, bf16[1024,1024]{1,0:T(8,128)(2,1)} %all-gather.8.cloned.1.call-done.refs_4_.refs_1_, ...), custom_call_target="tpu_custom_call" | custom-call | flops 5750000128 | bytes 1048576 | tf_op jit(solution)/shard_map/feed_out/pallas_call | solution.py:768
  201.9 5.1 %collective-permute-done.22.refs_3_.refs_8_ = bf16[256,512]{1,0:T(8,128)(2,1)S(1)} collective-permute-done((bf16[256,512]{1,0:T(8,128)(2,1)}, bf16[256,512]{1,0:T(8,128)(2,1)S(1)}, u32[]{:S(2)}, u32[]{:S(2)}) %collective-permute-start.22) | collective-permute-done | bytes 262176 | tf_op jit(solution)/shard_map/ppermute | solution.py:481
  208.8 12.1 %attend_back.2 = (bf16[1024,384]{1,0:T(8,128)(2,1)}, f32[8,128]{1,0:T(8,128)}) custom-call(bf16[256,512]{1,0:T(8,128)(2,1)} %get-tuple-element.132.refs_0_.refs_5_, bf16[256,512]{1,0:T(8,128)(2,1)} %copy-done.34, bf16[256,512]{1,0:T(8,128)(2,1)} %copy-done.35, bf16[256,512]{1,0:T(8,128)(2,1)} %copy-done.36, ...), custom_call_target="tpu_custom_call" | custom-call | flops 46000001024 | bytes 1048576 | tf_op jit(solution)/shard_map/attend_back/pallas_call | solution.py:768
  224.2 14.7 %attend_back.3 = (bf16[1024,384]{1,0:T(8,128)(2,1)}, f32[8,128]{1,0:T(8,128)}, bf16[256,1024]{1,0:T(8,128)(2,1)}, bf16[256,1024]{1,0:T(8,128)(2,1)}, bf16[256,10...) custom-call(bf16[256,512]{1,0:T(8,128)(2,1)} %get-tuple-element.132.refs_0_.refs_5_, bf16[256,512]{1,0:T(8,128)(2,1)} %copy-done.34, ...), custom_call_target="tpu_custom_call" | custom-call | flops 46000001024 | bytes 1048576 | tf_op jit(solution)/shard_map/attend_back/pallas_call | solution.py:768
  242.4 6.9 %collective-permute-done.27.refs_1_ = bf16[256,1024]{1,0:T(8,128)(2,1)S(1)} collective-permute-done((bf16[256,1024]{1,0:T(8,128)(2,1)}, bf16[256,1024]{1,0:T(8,128)(2,1)S(1)}, u32[]{:S(2)}, u32[]{:S(2)}) %collective-permute-start.27) | collective-permute-done | bytes 524320 | tf_op jit(solution)/shard_map/ppermute | solution.py:481
  253.5 8.5 %first_grads.1 = bf16[1024,1152]{1,0:T(8,128)(2,1)} custom-call(s32[1]{0:T(128)} %bitcast.refs_0_.refs_8_.refs_2_.refs_5_.refs_3_.refs_14_.refs_16_.refs_10_.rank_ref, bf16[1024,1024]{1,0:T(8,128)(2,1)} %get-tuple-element.163.refs_1_, bf16[1024,384]{1,0:T(8,128)(2,1)} %get-tuple-element.149.refs_14_.refs_2_, bf16[1024,384]{1,0:T(8,128)(2,1)} %get-tuple-element.164.refs_3_, ...), custom_call_target="tpu_custom_call" | custom-call | flops 9200000000 | bytes 1048576 | tf_op jit(solution)/shard_map/first_grads/pallas_call | solution.py:768
  262.8 4.8 %own_last.1 = bf16[8,64,1024]{2,1,0:T(8,128)(2,1)} custom-call(bf16[256,1024]{1,0:T(8,128)(2,1)} %get-tuple-element.154.refs_0_, bf16[256,1024]{1,0:T(8,128)(2,1)} %copy-done.24, bf16[128,1024]{1,0:T(8,128)(2,1)} %copy-done.39, bf16[256,1024]{1,0:T(8,128)(2,1)} %get-tuple-element.160.refs_3_, bf16[256,1024]{1,0:T(8,128)(2,1)} %copy-done.25, ...), custom_call_target="tpu_custom_call" | custom-call | flops 92000002048 | bytes 1048576 | tf_op jit(solution)/shard_map/own_last/pallas_call | solution.py:768
  273.3 5.5 %collective-permute-done.31 = bf16[64,3072]{1,0:T(8,128)(2,1)S(1)} collective-permute-done((bf16[64,3072]{1,0:T(8,128)(2,1)S(1)}, bf16[64,3072]{1,0:T(8,128)(2,1)S(1)}, u32[]{:S(2)}, u32[]{:S(2)}) %collective-permute-start.31) | collective-permute-done | bytes 393248 | tf_op jit(solution)/shard_map/ppermute | solution.py:481
  281.3 4.8 %all-to-all-start.3 = ((bf16[8,64,1024]{2,1,0:T(8,128)(2,1)}), bf16[8,64,1024]{2,1,0:T(8,128)(2,1)}, u32[]{:S(2)}, u32[]{:S(2)}) async-start(bf16[8,64,1024]{2,1,0:T(8,128)(2,1)} %own_last.1), calls=%async_computation.3 | async-start | bytes 2097152 | tf_op jit(solution)/shard_map/all_to_all | solution.py:1820
  286.1 17.2 %reduce-scatter.4.cloned.1.call-done = bf16[128,1152]{1,0:T(8,128)(2,1)} async-done(((bf16[1024,1152]{1,0:T(8,128)(2,1)}), bf16[128,1152]{1,0:T(8,128)(2,1)}) %reduce-scatter.4.cloned.1.call-update) | async-done | bytes 294928 | tf_op jit(solution)/shard_map/reduce_scatter | solution.py:1814
  315.4 2.8 all-to-all-done.3
  323.1 3.5 %all-to-all-start.4 = ((bf16[4,2,64,1024]{3,2,1,0:T(8,128)(2,1)}), bf16[4,2,64,1024]{3,2,1,0:T(8,128)(2,1)S(1)}, u32[]{:S(2)}, u32[]{:S(2)}) async-start(bf16[4,2,64,1024]{3,2,1,0:T(8,128)(2,1)} %bitcast.16), calls=%async_computation.7 | async-start | bytes 2097152 | tf_op jit(solution)/shard_map/all_to_all | solution.py:1827
  326.6 5.8 %spread_feed.1 = (f32[128,4096]{1,0:T(8,128)}, f32[128,4096]{1,0:T(8,128)}, f32[512,1024]{1,0:T(8,128)}, f32[8,128]{1,0:T(8,128)}) custom-call(s32[1]{0:T(128)} %bitcast.refs_0_.refs_8_.refs_2_.refs_5_.refs_3_.refs_14_.refs_16_.refs_10_.rank_ref, bf16[128,3072]{1,0:T(8,128)(2,1)} %copy-done.3, bf16[128,3072]{1,0:T(8,128)(2,1)} %copy-done.8, ...), custom_call_target="tpu_custom_call" | custom-call | flops 2097152 | bytes 16777216 | tf_op jit(solution)/shard_map/spread_feed/pallas_call | solution.py:580
  332.4 2.9 spread_first.1
  (234 shorter events, 92.1 us)
Async XLA Ops:
  7.2 40.1 %all-gather.4.cloned.1.call-start = ((), (), s32[]{:S(2)}) async-start(), calls=%async_computation.8 | async-start | bytes 2654208 | tf_op jit(solution)/shard_map/all_gather | solution.py:1730
  11.2 124.4 %all-gather.6.cloned.1.call-start = ((), (), s32[]{:S(2)}) async-start(), calls=%async_computation.9 | async-start | bytes 4718592 | tf_op jit(solution)/shard_map/all_gather | solution.py:1731
  33.6 23.4 %all-to-all-start.1 = ((bf16[8,32,1152]{2,1,0:T(8,128)(2,1)}), bf16[8,32,1152]{2,1,0:T(8,128)(2,1)S(1)}, u32[]{:S(2)}, u32[]{:S(2)}) async-start(bf16[8,32,1152]{2,1,0:T(8,128)(2,1)} %bitcast.8), calls=%async_computation.1 | async-start | bytes 1179648 | tf_op jit(solution)/shard_map/all_to_all | solution.py:523
  67.5 13.9 %collective-permute-start.3 = (bf16[256,1152]{1,0:T(8,128)(2,1)S(1)}, bf16[256,1152]{1,0:T(8,128)(2,1)S(1)}, u32[]{:S(2)}, u32[]{:S(2)}) collective-permute-start(bf16[256,1152]{1,0:T(8,128)(2,1)S(1)} %pad_maximum_fusion.2.refs_0_.refs_1_), channel_id=1, source_target_pairs={{0,16},{8,24},{16,0},{24,8},{1,17},{9,25},{17,1},{25,9},{2,18},{10... | collective-permute-start | bytes 1769480 | tf_op jit(solution)/shard_map/ppermute | solution.py:481
  68.8 13.7 %collective-permute-start.5 = (bf16[256,1152]{1,0:T(8,128)(2,1)S(1)}, bf16[256,1152]{1,0:T(8,128)(2,1)}, u32[]{:S(2)}, u32[]{:S(2)}) collective-permute-start(bf16[256,1152]{1,0:T(8,128)(2,1)S(1)} %pad_maximum_fusion.3.refs_2_.refs_3_), channel_id=1, source_target_pairs={{0,8},{8,0},{16,24},{24,16},{1,9},{9,1},{17,25},{25,17},{2,10},{10... | collective-permute-start | bytes 1769480 | tf_op jit(solution)/shard_map/ppermute | solution.py:481
  71.5 41.7 %all-to-all-start.2 = ((bf16[8,32,1024]{2,1,0:T(8,128)(2,1)}), bf16[8,32,1024]{2,1,0:T(8,128)(2,1)S(1)}, u32[]{:S(2)}, u32[]{:S(2)}) async-start(bf16[8,32,1024]{2,1,0:T(8,128)(2,1)} %slice.167), calls=%async_computation.2 | async-start | bytes 1048576 | tf_op jit(solution)/shard_map/all_to_all | solution.py:523
  76.3 75.7 %all-gather.8.cloned.1.call-start = ((), (), s32[]{:S(2)}) async-start(), calls=%async_computation.10 | async-start | bytes 2359296 | tf_op jit(solution)/shard_map/all_gather | solution.py:1732
  82.5 19.1 %collective-permute-start.7 = (bf16[1024,256]{1,0:T(8,128)(2,1)S(1)}, bf16[1024,256]{1,0:T(8,128)(2,1)}, u32[]{:S(2)}, u32[]{:S(2)}) collective-permute-start(bf16[1024,256]{1,0:T(8,128)(2,1)S(1)} %pad_maximum_fusion.5.refs_13_.refs_12_), channel_id=1, source_target_pairs={{0,8},{8,0},{16,24},{24,16},{1,9},{9,1},{17,25},{25,17},{2,10},{10... | collective-permute-start | bytes 1572872 | tf_op jit(solution)/shard_map/ppermute | solution.py:481
  83.7 17.9 %collective-permute-start.6 = (bf16[1024,256]{1,0:T(8,128)(2,1)S(1)}, bf16[1024,256]{1,0:T(8,128)(2,1)S(1)}, u32[]{:S(2)}, u32[]{:S(2)}) collective-permute-start(bf16[1024,256]{1,0:T(8,128)(2,1)S(1)} %pad_maximum_fusion.4.refs_11_.refs_10_), channel_id=1, source_target_pairs={{0,16},{8,24},{16,0},{24,8},{1,17},{9,25},{17,1},{25,9},{2,18},{10... | collective-permute-start | bytes 1572872 | tf_op jit(solution)/shard_map/ppermute | solution.py:481
  103.3 164.3 %reduce-scatter.8.cloned.1.call-start = ((), (), s32[]{:S(2)}) async-start(), calls=%async_computation.13 | async-start | bytes 2359296 | tf_op jit(solution)/shard_map/reduce_scatter | solution.py:1771
  110.0 12.0 %collective-permute-start.10 = (bf16[512,512]{1,0:T(8,128)(2,1)S(1)}, bf16[512,512]{1,0:T(8,128)(2,1)S(1)}, u32[]{:S(2)}, u32[]{:S(2)}) collective-permute-start(bf16[512,512]{1,0:T(8,128)(2,1)S(1)} %pad_maximum_fusion.6), channel_id=1, source_target_pairs={{0,16},{8,24},{16,0},{24,8},{1,17},{9,25},{17,1},{25,9},{2,18},{10... | collective-permute-start | bytes 1572872 | tf_op jit(solution)/shard_map/ppermute | solution.py:481
  112.2 10.4 %collective-permute-start.11 = (bf16[512,512]{1,0:T(8,128)(2,1)S(1)}, bf16[512,512]{1,0:T(8,128)(2,1)S(1)}, u32[]{:S(2)}, u32[]{:S(2)}) collective-permute-start(bf16[512,512]{1,0:T(8,128)(2,1)S(1)} %pad_maximum_fusion.7), channel_id=1, source_target_pairs={{0,8},{8,0},{16,24},{24,16},{1,9},{9,1},{17,25},{25,17},{2,10},{10... | collective-permute-start | bytes 1572872 | tf_op jit(solution)/shard_map/ppermute | solution.py:481
  122.6 11.3 %collective-permute-start.13 = (bf16[128,1024]{1,0:T(8,128)(2,1)S(1)}, bf16[128,1024]{1,0:T(8,128)(2,1)S(1)}, u32[]{:S(2)}, u32[]{:S(2)}) collective-permute-start(bf16[128,1024]{1,0:T(8,128)(2,1)S(1)} %get-tuple-element.198), channel_id=1, source_target_pairs={{0,16},{8,24},{16,0},{24,8},{1,17},{9,25},{17,1},{25,9},{2,18},{10... | collective-permute-start | bytes 786440 | tf_op jit(solution)/shard_map/ppermute | solution.py:481
  134.0 10.8 %collective-permute-start.15 = (bf16[256,1024]{1,0:T(8,128)(2,1)S(1)}, bf16[256,1024]{1,0:T(8,128)(2,1)S(1)}, u32[]{:S(2)}, u32[]{:S(2)}) collective-permute-start(bf16[256,1024]{1,0:T(8,128)(2,1)S(1)} %pad_maximum_fusion.9.refs_3_.refs_2_), channel_id=1, source_target_pairs={{0,8},{8,0},{16,24},{24,16},{1,9},{9,1},{17,25},{25,17},{2,10},{10... | collective-permute-start | bytes 1572872 | tf_op jit(solution)/shard_map/ppermute | solution.py:481
  151.7 115.9 %reduce-scatter.6.cloned.1.call-start = ((), (), s32[]{:S(2)}) async-start(), calls=%async_computation.12 | async-start | bytes 4718592 | tf_op jit(solution)/shard_map/reduce_scatter | solution.py:1783
  159.6 13.9 %collective-permute-start.16 = (bf16[256,1024]{1,0:T(8,128)(2,1)}, bf16[256,1024]{1,0:T(8,128)(2,1)S(1)}, u32[]{:S(2)}, u32[]{:S(2)}) collective-permute-start(bf16[256,1024]{1,0:T(8,128)(2,1)} %get-tuple-element.122), channel_id=1, source_target_pairs={{0,16},{8,24},{16,0},{24,8},{1,17},{9,25},{17,1},{25,9},{2,18},{10... | collective-permute-start | bytes 1572872 | tf_op jit(solution)/shard_map/ppermute | solution.py:481
  161.0 10.8 %collective-permute-start.18 = (bf16[256,1024]{1,0:T(8,128)(2,1)}, bf16[256,1024]{1,0:T(8,128)(2,1)S(1)}, u32[]{:S(2)}, u32[]{:S(2)}) collective-permute-start(bf16[256,1024]{1,0:T(8,128)(2,1)} %get-tuple-element.126), channel_id=1, source_target_pairs={{0,8},{8,0},{16,24},{24,16},{1,9},{9,1},{17,25},{25,17},{2,10},{10... | collective-permute-start | bytes 1572872 | tf_op jit(solution)/shard_map/ppermute | solution.py:481
  173.0 11.9 %collective-permute-start.19 = (bf16[128,1024]{1,0:T(8,128)(2,1)S(1)}, bf16[128,1024]{1,0:T(8,128)(2,1)S(1)}, u32[]{:S(2)}, u32[]{:S(2)}) collective-permute-start(bf16[128,1024]{1,0:T(8,128)(2,1)S(1)} %slice_add_fusion.2), channel_id=1, source_target_pairs={{0,16},{8,24},{16,0},{24,8},{1,17},{9,25},{17,1},{25,9},{2,18},{10... | collective-permute-start | bytes 786440 | tf_op jit(solution)/shard_map/ppermute | solution.py:481
  174.7 10.2 %collective-permute-start.17 = (bf16[128,1024]{1,0:T(8,128)(2,1)S(1)}, bf16[128,1024]{1,0:T(8,128)(2,1)S(1)}, u32[]{:S(2)}, u32[]{:S(2)}) collective-permute-start(bf16[128,1024]{1,0:T(8,128)(2,1)S(1)} %slice_add_fusion.3), channel_id=1, source_target_pairs={{0,8},{8,0},{16,24},{24,16},{1,9},{9,1},{17,25},{25,17},{2,10},{10... | collective-permute-start | bytes 786440 | tf_op jit(solution)/shard_map/ppermute | solution.py:481
  184.9 118.4 %reduce-scatter.4.cloned.1.call-start = ((), (), s32[]{:S(2)}) async-start(), calls=%async_computation.11 | async-start | bytes 2654208 | tf_op jit(solution)/shard_map/reduce_scatter | solution.py:1814
  194.1 13.0 %collective-permute-start.22 = (bf16[256,512]{1,0:T(8,128)(2,1)}, bf16[256,512]{1,0:T(8,128)(2,1)S(1)}, u32[]{:S(2)}, u32[]{:S(2)}) collective-permute-start(bf16[256,512]{1,0:T(8,128)(2,1)} %get-tuple-element.135), channel_id=1, source_target_pairs={{0,24},{8,16},{16,8},{24,0},{1,25},{9,17},{17,9},{25,1},{2,26},{10... | collective-permute-start | bytes 786440 | tf_op jit(solution)/shard_map/ppermute | solution.py:481
  207.0 14.6 %collective-permute-start.23 = (bf16[256,1024]{1,0:T(8,128)(2,1)}, bf16[256,1024]{1,0:T(8,128)(2,1)S(1)}, u32[]{:S(2)}, u32[]{:S(2)}) collective-permute-start(bf16[256,1024]{1,0:T(8,128)(2,1)} %get-tuple-element.146), channel_id=1, source_target_pairs={{0,16},{8,24},{16,0},{24,8},{1,17},{9,25},{17,1},{25,9},{2,18},{10... | collective-permute-start | bytes 1572872 | tf_op jit(solution)/shard_map/ppermute | solution.py:481
  208.0 13.6 %collective-permute-start.24 = (bf16[256,1024]{1,0:T(8,128)(2,1)}, bf16[256,1024]{1,0:T(8,128)(2,1)S(1)}, u32[]{:S(2)}, u32[]{:S(2)}) collective-permute-start(bf16[256,1024]{1,0:T(8,128)(2,1)} %get-tuple-element.147), channel_id=1, source_target_pairs={{0,8},{8,0},{16,24},{24,16},{1,9},{9,1},{17,25},{25,17},{2,10},{10... | collective-permute-start | bytes 1572872 | tf_op jit(solution)/shard_map/ppermute | solution.py:481
  221.7 18.1 %collective-permute-start.26 = (bf16[128,1024]{1,0:T(8,128)(2,1)S(1)}, bf16[128,1024]{1,0:T(8,128)(2,1)S(1)}, u32[]{:S(2)}, u32[]{:S(2)}) collective-permute-start(bf16[128,1024]{1,0:T(8,128)(2,1)S(1)} %slice_add_fusion.4), channel_id=1, source_target_pairs={{0,16},{8,24},{16,0},{24,8},{1,17},{9,25},{17,1},{25,9},{2,18},{10... | collective-permute-start | bytes 786440 | tf_op jit(solution)/shard_map/ppermute | solution.py:481
  223.3 16.5 %collective-permute-start.25 = (bf16[128,1024]{1,0:T(8,128)(2,1)S(1)}, bf16[128,1024]{1,0:T(8,128)(2,1)S(1)}, u32[]{:S(2)}, u32[]{:S(2)}) collective-permute-start(bf16[128,1024]{1,0:T(8,128)(2,1)S(1)} %slice_add_fusion.5), channel_id=1, source_target_pairs={{0,8},{8,0},{16,24},{24,16},{1,9},{9,1},{17,25},{25,17},{2,10},{10... | collective-permute-start | bytes 786440 | tf_op jit(solution)/shard_map/ppermute | solution.py:481
  240.9 10.9 %collective-permute-start.29 = (bf16[256,1024]{1,0:T(8,128)(2,1)}, bf16[256,1024]{1,0:T(8,128)(2,1)S(1)}, u32[]{:S(2)}, u32[]{:S(2)}) collective-permute-start(bf16[256,1024]{1,0:T(8,128)(2,1)} %get-tuple-element.161), channel_id=1, source_target_pairs={{0,8},{8,0},{16,24},{24,16},{1,9},{9,1},{17,25},{25,17},{2,10},{10... | collective-permute-start | bytes 1572872 | tf_op jit(solution)/shard_map/ppermute | solution.py:481
  250.5 11.5 %collective-permute-start.28 = (bf16[128,1024]{1,0:T(8,128)(2,1)S(1)}, bf16[128,1024]{1,0:T(8,128)(2,1)S(1)}, u32[]{:S(2)}, u32[]{:S(2)}) collective-permute-start(bf16[128,1024]{1,0:T(8,128)(2,1)S(1)} %slice_add_fusion.1), channel_id=1, source_target_pairs={{0,8},{8,0},{16,24},{24,16},{1,9},{9,1},{17,25},{25,17},{2,10},{10... | collective-permute-start | bytes 786440 | tf_op jit(solution)/shard_map/ppermute | solution.py:481
  278.8 24.4 %collective-permute-start.32 = (bf16[128,3072]{1,0:T(8,128)(2,1)S(1)}, bf16[128,3072]{1,0:T(8,128)(2,1)S(1)}, u32[]{:S(2)}, u32[]{:S(2)}) collective-permute-start(bf16[128,3072]{1,0:T(8,128)(2,1)S(1)} %pad_maximum_fusion.lower), channel_id=1, source_target_pairs={{0,16},{8,24},{16,0},{24,8},{1,17},{9,25},{17,1},{25,9},{2,18},{10... | collective-permute-start | bytes 2359304 | tf_op jit(solution)/shard_map/ppermute | solution.py:481
  280.4 22.8 %collective-permute-start.34 = (bf16[128,3072]{1,0:T(8,128)(2,1)S(1)}, bf16[128,3072]{1,0:T(8,128)(2,1)S(1)}, u32[]{:S(2)}, u32[]{:S(2)}) collective-permute-start(bf16[128,3072]{1,0:T(8,128)(2,1)S(1)} %pad_maximum_fusion.1.upper), channel_id=1, source_target_pairs={{0,8},{8,0},{16,24},{24,16},{1,9},{9,1},{17,25},{25,17},{2,10},{10... | collective-permute-start | bytes 2359304 | tf_op jit(solution)/shard_map/ppermute | solution.py:481
  281.3 36.9 %all-to-all-start.3 = ((bf16[8,64,1024]{2,1,0:T(8,128)(2,1)}), bf16[8,64,1024]{2,1,0:T(8,128)(2,1)}, u32[]{:S(2)}, u32[]{:S(2)}) async-start(bf16[8,64,1024]{2,1,0:T(8,128)(2,1)} %own_last.1), calls=%async_computation.3 | async-start | bytes 2097152 | tf_op jit(solution)/shard_map/all_to_all | solution.py:1820
  310.6 10.1 %collective-permute-start.36 = (bf16[128,1152]{1,0:T(8,128)(2,1)S(1)}, bf16[128,1152]{1,0:T(8,128)(2,1)S(1)}, u32[]{:S(2)}, u32[]{:S(2)}) collective-permute-start(bf16[128,1152]{1,0:T(8,128)(2,1)S(1)} %pad_maximum_fusion.10.lower), channel_id=1, source_target_pairs={{0,16},{8,24},{16,0},{24,8},{1,17},{9,25},{17,1},{25,9},{2,18},{10... | collective-permute-start | bytes 884744 | tf_op jit(solution)/shard_map/ppermute | solution.py:481
  323.1 17.0 %all-to-all-start.4 = ((bf16[4,2,64,1024]{3,2,1,0:T(8,128)(2,1)}), bf16[4,2,64,1024]{3,2,1,0:T(8,128)(2,1)S(1)}, u32[]{:S(2)}, u32[]{:S(2)}) async-start(bf16[4,2,64,1024]{3,2,1,0:T(8,128)(2,1)} %bitcast.16), calls=%async_computation.7 | async-start | bytes 2097152 | tf_op jit(solution)/shard_map/all_to_all | solution.py:1827
  (60 other events, 685.1 us)
Sparse Core Ops, SparseCore 0:
  11.3 35.9 all-gather.3
  49.5 60.6 all-gather.5
  111.8 27.6 all-gather.7
  151.8 36.6 reduce-scatter.7
  190.6 48.5 reduce-scatter.5
  262.1 41.1 reduce-scatter.3

commit v2 on v1

--- a/solution.py
+++ b/solution.py
@@ -1164,13 +1164,14 @@
     )
 
 
-def feed_back_body(both, cots, gate_up, down, grads, back):
+def feed_back_body(both, cots, gate_up, down, grads, back, later=()):
     start_all(down)
     cots.start(0)
     both.start(0)
     gate_up.start()
     cots.start(1)
     both.start(1)
+    start_all(*later)
     per = down.ref.shape[0]
 
     def one_chunk(index, carry):
@@ -1187,7 +1188,27 @@
     lax.fori_loop(0, 2, one_chunk, 0)
 
 
-def feed_back(first, both, cots, gate_up, down, token):
+def feed_back_far_body(both, cots, gate_up, down, hidden, near_cots, grads, back, out):
+    feed_back_body(both, cots, gate_up, down, grads, back, (hidden, near_cots))
+    near_ref, far_ref = near_cots.wait(), cots.ref
+    chunk = near_ref.shape[1]
+
+    def one_part(index, carry):
+        hidden.wait_at(index)
+        total = None
+        for k in range(4):
+            more = dot_first(
+                hidden.ref[index, k * chunk : (k + 1) * chunk, :], (near_ref, far_ref)[k % 2][k // 2]
+            )
+            total = more if total is None else total + more
+        out.ref[index] = total.astype(LOW)
+        out.start_at(index)
+        return carry
+
+    lax.fori_loop(0, hidden.ref.shape[0], one_part, 0)
+
+
+def feed_back(first, both, cots, gate_up, down, token, hidden=None):
     length = both.shape[0]
     chunk = length // 4
     per = down.shape[0]
@@ -1197,15 +1218,14 @@
             (refs[0].at[pl.ds((first + 2 * k) * chunk, chunk)], buffer.at[k]) for k in range(2)
         ]
 
-    return run(
-        feed_back_body,
-        "feed_back",
-        7,
-        [Plan([both], (2, chunk, 2 * per), pairs, 2), group((cots[first], cots[first + 2]))]
-        + [whole(gate_up), whole(down)],
-        [out_rows((length // 2, 2 * per), LOW, 2), out_group((chunk, D), LOW, 2)],
-        token=token,
-    )
+    ins = [Plan([both], (2, chunk, 2 * per), pairs, 2), group((cots[first], cots[first + 2]))]
+    ins += [whole(gate_up), whole(down)]
+    outs = [out_rows((length // 2, 2 * per), LOW, 2), out_group((chunk, D), LOW, 2)]
+    if hidden is None:
+        return run(feed_back_body, "feed_back", 7, ins, outs, token=token)
+    ins += [columns_of(hidden), group((cots[0], cots[2]))]
+    outs += [out_rows((per, D), LOW)]
+    return run(feed_back_far_body, "feed_back", 12, ins, outs, token=token)
 
 
 def sum_arrived(near, got, last):
@@ -1397,37 +1417,6 @@
     )
 
 
-def down_grads_body(hidden, cots, out):
-    start_all(cots, hidden)
-    count, chunk, _ = cots.ref.shape
-
-    def one_part(index, carry):
-        cots_ref = cots.wait_first(index)
-        hidden.wait_at(index)
-        total = dot_first(hidden.ref[index, :chunk, :], cots_ref[0])
-        for k in range(1, count):
-            total = total + dot_first(
-                hidden.ref[index, k * chunk : (k + 1) * chunk, :], cots_ref[k]
-            )
-        out.ref[index] = total.astype(LOW)
-        out.start_at(index)
-        return carry
-
-    lax.fori_loop(0, hidden.ref.shape[0], one_part, 0)
-
-
-def down_grads(hidden, cots, token):
-    per = hidden.shape[1]
-    return run(
-        down_grads_body,
-        "down_grads",
-        5,
-        [columns_of(hidden), group(cots)],
-        [out_rows((per, D), LOW)],
-        token=token,
-    )[0]
-
-
 def gate_up_grads_body(mixed, near, far, out):
     start_all(near, far, mixed)
     chunk = mixed.ref.shape[1] // 4
@@ -1767,15 +1756,14 @@
 
     both, hidden = feed(mixed_second, gate_up, after(rank_row, cot_got))
     cots = far_pairs(cot_mine, lax.optimization_barrier((cot_got, mixed_second))[0])
-    down_weight_grads = down_grads(hidden, cots, rank_row)
-    down_grad_shard = lax.psum_scatter(down_weight_grads, "seq", scatter_dimension=0, tiled=True)
-    far_grads, far_lower, far_upper = feed_back(
-        1, both, cots, gate_up, down, after(rank_row, down_weight_grads)
+    far_grads, far_lower, far_upper, down_weight_grads = feed_back(
+        1, both, cots, gate_up, down, rank_row, hidden
     )
     got = scatter_first((None, far_lower, None, far_upper))
     near_grads, near_lower, near_upper = feed_back(
         0, both, cots, gate_up, down, after(rank_row, far_lower)
     )
+    down_grad_shard = lax.psum_scatter(down_weight_grads, "seq", scatter_dimension=0, tiled=True)
     back = (near_lower, None, near_upper, None)
     gate_up_weight_grads = gate_up_grads(
         mixed_second, near_grads, far_grads, after(rank_row, got)
@@ -1809,8 +1797,9 @@
     slots = lax.broadcasted_iota(jnp.int32, (per, 1), 0) % shard == lax.axis_index("seq")
     bias_rows = jnp.where(slots, bias_parts, LOW(0))
     first_weight_grads = first_grads(
-        rank_row, mixed_first, proj0, proj1, heads, parcels, bias_rows, after(rank_row, got)
-    )
+        rank_row, mixed_first, proj0, proj1, heads, parcels, bias_rows, rank_row
+    )
+    got, first_weight_grads = lax.optimization_barrier((got, first_weight_grads))
     first_shard = lax.psum_scatter(first_weight_grads, "seq", scatter_dimension=0, tiled=True)
     sums = scatter_second(back, got)
     last = own_last(

time: 350 us -> 338 us (0.966)
  starting transfers between devices: 66.3 us -> 60 us
    reduce_scatter x1, waiting for transfers between devices: 17.2 us -> 5.29 us  [on_plane(): lax.psum_scatter(first_weight_grads, 'seq', scatter_dimension=0, tiled=True)]
    all_to_all x1, waiting for transfers between devices: 2.83 us -> 9.61 us  [on_plane(): moved = lax.all_to_all(last, 'seq', 0, 0, tiled=True)]
    ppermute x39, starting transfers between devices: 47.9 us -> 42.1 us  [swap(): return lax.ppermute(value, 'batch', [(i, i ^ bit) for i in range(4)])]
    pallas_call x15 -> x14, Pallas kernels: 122 us -> 120 us  [run(): pl.pallas_call(kernel, out_shape=out_shapes, in_specs=in_specs, out_specs...]
  transfers between devices with their start and end apart: 49 -> 49, of which waited for: 23 -> 27; matrix products, arithmetic and copies ran while one was open for 6% -> 5% of each run, Pallas kernels for 36% -> 34%
where the time goes in v2:
time: 338 us; the launch traced here: 336 us
  Pallas kernels  129 us (38%)
  waiting for transfers between devices  87.1 us (26%)
  starting transfers between devices  60 us (18%)
  blocking collectives  20.7 us (6%)
  local copies, waits for them, and re-layouts  18.2 us (5%)
  between operations  14.9 us (4%)
  other arithmetic  6.67 us (2%)
    pallas_call x14, Pallas kernels, run(): pl.pallas_call(kernel, out_shape=out_shapes, in_specs=in_specs, out_specs...  120 us
    ppermute x39, waiting for transfers between devices, swap(): return lax.ppermute(value, 'batch', [(i, i ^ bit) for i in range(4)])  57.8 us
    ppermute x39, starting transfers between devices, swap(): return lax.ppermute(value, 'batch', [(i, i ^ bit) for i in range(4)])  42.1 us
    all_to_all x1, blocking collectives, on_plane(): packed = lax.all_to_all(packed, 'batch', 0, 0, tiled=True)  20.7 us
    all_to_all x2, starting transfers between devices, over_seq(): lax.all_to_all(pieces, 'seq', 0, 0, tiled=True)  9.71 us
    all_to_all x1, waiting for transfers between devices, on_plane(): moved = lax.all_to_all(last, 'seq', 0, 0, tiled=True)  9.61 us
    all_gather x1, waiting for transfers between devices, on_plane(): first_weights = lax.all_gather(first_shard, 'seq', axis=0, tiled=True)  8.76 us
    pallas_call x2, Pallas kernels, call(): pl.pallas_call(kernel, grid=(1,), out_shape=[jax.ShapeDtypeStruct(shape,...  8.62 us
  transfers between devices with their start and end apart: 49, of which 27 were waited for; matrix products, arithmetic and copies ran while one was open for 5% of the time, Pallas kernels for 34%

profile of v2, /device:TPU:0, one launch (start us, length us, event | category | flops | bytes accessed | tf_op | source)
XLA Modules:
  0.0 336.4 jit_solution(4982311219596442981)
XLA Ops:
  7.2 3.9 %pack.1 = (bf16[4,2,2,32,1152]{4,3,2,1,0:T(8,128)(2,1)}, bf16[128,1152]{1,0:T(8,128)(2,1)}, bf16[128,2048]{1,0:T(8,128)(2,1)}, bf16[128,1024]{1,0:T(8,128)(2,1)}) custom-call(s32[1]{0:T(128)} %bitcast.refs_0_.refs_8_.refs_2_.refs_5_.refs_3_.refs_14_.refs_16_.refs_10_.rank_ref, bf16[2,4,32,1024]{3,2,1,0:T(8,128)(2,1)} %bitcast.57, ...), custom_call_target="tpu_custom_call" | custom-call | flops 4600000000 | bytes 1048576 | tf_op jit(solution)/shard_map/pack/pallas_call | solution.py:768
  11.9 20.7 %all_to_all.25 = bf16[4,2,2,32,1152]{4,3,2,1,0:T(8,128)(2,1)S(1)} all-to-all(bf16[4,2,2,32,1152]{4,3,2,1,0:T(8,128)(2,1)} %get-tuple-element.101), channel_id=1, replica_groups=mesh['batch'=4,'seq'=8] {'batch'}, dimensions={0} | all-to-all | bytes 2359296 | tf_op jit(solution)/shard_map/all_to_all | solution.py:1722
  33.5 4.9 %all-to-all-start.1 = ((bf16[8,32,1152]{2,1,0:T(8,128)(2,1)}), bf16[8,32,1152]{2,1,0:T(8,128)(2,1)S(1)}, u32[]{:S(2)}, u32[]{:S(2)}) async-start(bf16[8,32,1152]{2,1,0:T(8,128)(2,1)} %bitcast.8), calls=%async_computation.1 | async-start | bytes 1179648 | tf_op jit(solution)/shard_map/all_to_all | solution.py:523
  38.5 8.8 %all-gather.4.cloned.1.call-done.refs_4_.refs_5_.refs_15_ = bf16[1024,1152]{1,0:T(8,128)(2,1)} async-done(((bf16[128,1152]{1,0:T(8,128)(2,1)}), bf16[1024,1152]{1,0:T(8,128)(2,1)}) %all-gather.4.cloned.1.call-update) | async-done | bytes 2359312 | tf_op jit(solution)/shard_map/all_gather | solution.py:1719
  53.5 3.5 %all-to-all-done.1 = bf16[8,32,1152]{2,1,0:T(8,128)(2,1)S(1)} async-done(((bf16[8,32,1152]{2,1,0:T(8,128)(2,1)}), bf16[8,32,1152]{2,1,0:T(8,128)(2,1)S(1)}, u32[]{:S(2)}, u32[]{:S(2)}) %all-to-all-start.1) | async-done | bytes 589856 | tf_op jit(solution)/shard_map/all_to_all | solution.py:523
  61.3 6.1 %collective-permute-done.2 = bf16[128,1152]{1,0:T(8,128)(2,1)S(1)} collective-permute-done((bf16[128,1152]{1,0:T(8,128)(2,1)S(1)}, bf16[128,1152]{1,0:T(8,128)(2,1)S(1)}, u32[]{:S(2)}, u32[]{:S(2)}) %collective-permute-start.2) | collective-permute-done | bytes 294944 | tf_op jit(solution)/shard_map/ppermute | solution.py:481
  71.5 4.8 %all-to-all-start.2 = ((bf16[8,32,1024]{2,1,0:T(8,128)(2,1)}), bf16[8,32,1024]{2,1,0:T(8,128)(2,1)S(1)}, u32[]{:S(2)}, u32[]{:S(2)}) async-start(bf16[8,32,1024]{2,1,0:T(8,128)(2,1)} %slice.167), calls=%async_computation.2 | async-start | bytes 1048576 | tf_op jit(solution)/shard_map/all_to_all | solution.py:523
  76.3 5.1 %collective-permute-done.3.refs_1_.refs_2_ = bf16[256,1152]{1,0:T(8,128)(2,1)S(1)} collective-permute-done((bf16[256,1152]{1,0:T(8,128)(2,1)S(1)}, bf16[256,1152]{1,0:T(8,128)(2,1)S(1)}, u32[]{:S(2)}, u32[]{:S(2)}) %collective-permute-start.3) | collective-permute-done | bytes 589856 | tf_op jit(solution)/shard_map/ppermute | solution.py:481
  84.7 16.7 %attend.1 = (f32[16,1024]{1,0:T(8,128)}, bf16[1024,1024]{1,0:T(8,128)(2,1)}, bf16[1024,768]{1,0:T(8,128)(2,1)}, f32[1024,256]{1,0:T(8,128)}, bf16[512,256]{1,0:T...) custom-call(bf16[256,1152]{1,0:T(8,128)(2,1)} %copy-done.10, ...), custom_call_target="tpu_custom_call" | custom-call | flops 17250000896 | bytes 1048576 | tf_op jit(solution)/shard_map/attend/pallas_call | solution.py:768
  104.2 4.6 %collective-permute-done.8.refs_7_ = bf16[512,256]{1,0:T(8,128)(2,1)S(1)} collective-permute-done((bf16[512,256]{1,0:T(8,128)(2,1)}, bf16[512,256]{1,0:T(8,128)(2,1)S(1)}, u32[]{:S(2)}, u32[]{:S(2)}) %collective-permute-start.8) | collective-permute-done | bytes 262176 | tf_op jit(solution)/shard_map/ppermute | solution.py:481
  113.1 8.8 %collective-permute-done.10.refs_9_ = bf16[512,512]{1,0:T(8,128)(2,1)S(1)} collective-permute-done((bf16[512,512]{1,0:T(8,128)(2,1)S(1)}, bf16[512,512]{1,0:T(8,128)(2,1)S(1)}, u32[]{:S(2)}, u32[]{:S(2)}) %collective-permute-start.10) | collective-permute-done | bytes 524320 | tf_op jit(solution)/shard_map/ppermute | solution.py:481
  125.7 8.6 %middle.1 = (bf16[1024,1024]{1,0:T(8,128)(2,1)}, f32[256,1024]{1,0:T(8,128)}, bf16[1024,1024]{1,0:T(8,128)(2,1)}) custom-call(s32[1]{0:T(128)} %bitcast.refs_0_.refs_8_.refs_2_.refs_5_.refs_3_.refs_14_.refs_16_.refs_10_.rank_ref, bf16[256,1152]{1,0:T(8,128)(2,1)} %copy-done.10, bf16[256,1152]{1,0:T(8,128)(2,1)} %copy-done.31, bf16[256,1152]{1,0:T(8,128)(2,1)} %copy-done.11, ...), custom_call_target="tpu_custom_call" | custom-call | flops 8049999872 | bytes 1048576 | tf_op jit(solution)/shard_map/middle/pallas_call | solution.py:768
  135.7 9.3 %feed.1 = (bf16[1024,2048]{1,0:T(8,128)(2,1)}, bf16[1024,1024]{1,0:T(8,128)(2,1)}) custom-call(bf16[1024,1024]{1,0:T(8,128)(2,1)} %get-tuple-element.113.refs_0_, bf16[1024,2048]{1,0:T(8,128)(2,1)} %all-gather.6.cloned.1.call-done.refs_1_.refs_3_, s32[1]{0:T(128)} %bitcast.refs_0_.refs_8_.refs_2_.refs_5_.refs_3_.refs_14_.refs_16_.refs_10_.rank_ref), custom_call_target="tpu_custom_call" | custom-call | flops 9200000000 | bytes 1048576 | tf_op jit(solution)/shard_map/feed/pallas_call | solution.py:768
  146.0 11.3 %feed_back.2 = (bf16[512,2048]{1,0:T(8,128)(2,1)}, bf16[256,1024]{1,0:T(8,128)(2,1)}, bf16[256,1024]{1,0:T(8,128)(2,1)}, bf16[1024,1024]{1,0:T(8,128)(2,1)}) custom-call(bf16[1024,2048]{1,0:T(8,128)(2,1)} %get-tuple-element.118.refs_0_, bf16[256,1024]{1,0:T(8,128)(2,1)} %copy-done.39, bf16[256,1024]{1,0:T(8,128)(2,1)} %copy-done.38, ...), custom_call_target="tpu_custom_call" | custom-call | flops 13799999488 | bytes 1048576 | tf_op jit(solution)/shard_map/feed_back/pallas_call | solution.py:768
  161.3 7.7 %feed_back.3 = (bf16[512,2048]{1,0:T(8,128)(2,1)}, bf16[256,1024]{1,0:T(8,128)(2,1)}, bf16[256,1024]{1,0:T(8,128)(2,1)}) custom-call(bf16[1024,2048]{1,0:T(8,128)(2,1)} %get-tuple-element.118.refs_0_, bf16[256,1024]{1,0:T(8,128)(2,1)} %copy-done.15, bf16[256,1024]{1,0:T(8,128)(2,1)} %copy-done.14, ...), custom_call_target="tpu_custom_call" | custom-call | flops 8049999872 | bytes 1048576 | tf_op jit(solution)/shard_map/feed_back/pallas_call | solution.py:768
  174.2 8.9 %gate_up_grads.1 = bf16[1024,2048]{1,0:T(8,128)(2,1)} custom-call(bf16[1024,1024]{1,0:T(8,128)(2,1)} %get-tuple-element.113.refs_0_, bf16[512,2048]{1,0:T(8,128)(2,1)} %get-tuple-element.129.refs_1_, bf16[512,2048]{1,0:T(8,128)(2,1)} %get-tuple-element.130.refs_2_, s32[1]{0:T(128)} %bitcast.refs_0_.refs_8_.refs_2_.refs_5_.refs_3_.refs_14_.refs_16_.refs_10_.rank_ref), custom_call_target="tpu_custom_call" | custom-call | flops 9200000000 | bytes 1048576 | tf_op jit(solution)/shard_map/gate_up_grads/pallas_call | solution.py:768
  184.1 5.8 %own_back.1 = (f32[256,1024]{1,0:T(8,128)}, bf16[256,512]{1,0:T(8,128)(2,1)}, bf16[256,512]{1,0:T(8,128)(2,1)}, bf16[256,512]{1,0:T(8,128)(2,1)}, bf16[256,512]{1,0:T(8,128)(2,1)}) custom-call(s32[1]{0:T(128)} %bitcast.refs_0_.refs_8_.refs_2_.refs_5_.refs_3_.refs_14_.refs_16_.refs_10_.rank_ref, bf16[256,1024]{1,0:T(8,128)(2,1)} %get-tuple-element.125.refs_1_, ...), custom_call_target="tpu_custom_call" | custom-call | flops 4600000000 | bytes 1048576 | tf_op jit(solution)/shard_map/own_back/pallas_call | solution.py:768
  193.4 5.9 %feed_out.1 = (bf16[256,1024]{1,0:T(8,128)(2,1)}, bf16[256,1024]{1,0:T(8,128)(2,1)}, bf16[256,1024]{1,0:T(8,128)(2,1)}, bf16[256,1024]{1,0:T(8,128)(2,1)}) custom-call(bf16[1024,1024]{1,0:T(8,128)(2,1)} %get-tuple-element.122.refs_5_.refs_0_, bf16[1024,1024]{1,0:T(8,128)(2,1)} %all-gather.8.cloned.1.call-done.refs_4_.refs_1_, ...), custom_call_target="tpu_custom_call" | custom-call | flops 5750000128 | bytes 1048576 | tf_op jit(solution)/shard_map/feed_out/pallas_call | solution.py:768
  200.5 5.1 %collective-permute-done.22.refs_3_.refs_8_ = bf16[256,512]{1,0:T(8,128)(2,1)S(1)} collective-permute-done((bf16[256,512]{1,0:T(8,128)(2,1)}, bf16[256,512]{1,0:T(8,128)(2,1)S(1)}, u32[]{:S(2)}, u32[]{:S(2)}) %collective-permute-start.22) | collective-permute-done | bytes 262176 | tf_op jit(solution)/shard_map/ppermute | solution.py:481
  206.3 12.1 %attend_back.2 = (bf16[1024,384]{1,0:T(8,128)(2,1)}, f32[8,128]{1,0:T(8,128)}) custom-call(bf16[256,512]{1,0:T(8,128)(2,1)} %get-tuple-element.133.refs_0_.refs_5_, bf16[256,512]{1,0:T(8,128)(2,1)} %copy-done.40, bf16[256,512]{1,0:T(8,128)(2,1)} %copy-done.42, bf16[256,512]{1,0:T(8,128)(2,1)} %copy-done.44, ...), custom_call_target="tpu_custom_call" | custom-call | flops 46000001024 | bytes 1048576 | tf_op jit(solution)/shard_map/attend_back/pallas_call | solution.py:768
  222.0 14.7 %attend_back.3 = (bf16[1024,384]{1,0:T(8,128)(2,1)}, f32[8,128]{1,0:T(8,128)}, bf16[256,1024]{1,0:T(8,128)(2,1)}, bf16[256,1024]{1,0:T(8,128)(2,1)}, bf16[256,10...) custom-call(bf16[256,512]{1,0:T(8,128)(2,1)} %get-tuple-element.133.refs_0_.refs_5_, bf16[256,512]{1,0:T(8,128)(2,1)} %copy-done.40, ...), custom_call_target="tpu_custom_call" | custom-call | flops 46000001024 | bytes 1048576 | tf_op jit(solution)/shard_map/attend_back/pallas_call | solution.py:768
  239.3 8.6 %first_grads.1 = bf16[1024,1152]{1,0:T(8,128)(2,1)} custom-call(s32[1]{0:T(128)} %bitcast.refs_0_.refs_8_.refs_2_.refs_5_.refs_3_.refs_14_.refs_16_.refs_10_.rank_ref, bf16[1024,1024]{1,0:T(8,128)(2,1)} %get-tuple-element.162.refs_1_, bf16[1024,384]{1,0:T(8,128)(2,1)} %get-tuple-element.150.refs_14_.refs_2_, bf16[1024,384]{1,0:T(8,128)(2,1)} %get-tuple-element.163.refs_3_, ...), custom_call_target="tpu_custom_call" | custom-call | flops 9200000000 | bytes 1048576 | tf_op jit(solution)/shard_map/first_grads/pallas_call | solution.py:768
  251.5 5.0 %collective-permute-done.30.refs_5_ = bf16[128,1024]{1,0:T(8,128)(2,1)S(1)} collective-permute-done((bf16[128,1024]{1,0:T(8,128)(2,1)S(1)}, bf16[128,1024]{1,0:T(8,128)(2,1)S(1)}, u32[]{:S(2)}, u32[]{:S(2)}) %collective-permute-start.30) | collective-permute-done | bytes 262176 | tf_op jit(solution)/shard_map/ppermute | solution.py:481
  256.5 2.9 collective-permute-done.29.refs_2_
  260.1 4.8 %own_last.1 = bf16[8,64,1024]{2,1,0:T(8,128)(2,1)} custom-call(bf16[256,1024]{1,0:T(8,128)(2,1)} %get-tuple-element.155.refs_0_, bf16[256,1024]{1,0:T(8,128)(2,1)} %copy-done.27, bf16[128,1024]{1,0:T(8,128)(2,1)} %copy-done.48, bf16[256,1024]{1,0:T(8,128)(2,1)} %get-tuple-element.167.refs_3_, bf16[256,1024]{1,0:T(8,128)(2,1)} %copy-done.29, ...), custom_call_target="tpu_custom_call" | custom-call | flops 92000002048 | bytes 1048576 | tf_op jit(solution)/shard_map/own_last/pallas_call | solution.py:768
  269.6 6.4 %collective-permute-done.31 = bf16[64,3072]{1,0:T(8,128)(2,1)S(1)} collective-permute-done((bf16[64,3072]{1,0:T(8,128)(2,1)S(1)}, bf16[64,3072]{1,0:T(8,128)(2,1)S(1)}, u32[]{:S(2)}, u32[]{:S(2)}) %collective-permute-start.31) | collective-permute-done | bytes 393248 | tf_op jit(solution)/shard_map/ppermute | solution.py:481
  278.3 4.3 %all-to-all-start.3 = ((bf16[8,64,1024]{2,1,0:T(8,128)(2,1)}), bf16[8,64,1024]{2,1,0:T(8,128)(2,1)}, u32[]{:S(2)}, u32[]{:S(2)}) async-start(bf16[8,64,1024]{2,1,0:T(8,128)(2,1)} %own_last.1), calls=%async_computation.3 | async-start | bytes 2097152 | tf_op jit(solution)/shard_map/all_to_all | solution.py:1809
  282.6 5.3 %reduce-scatter.4.cloned.1.call-done = bf16[128,1152]{1,0:T(8,128)(2,1)} async-done(((bf16[1024,1152]{1,0:T(8,128)(2,1)}), bf16[128,1152]{1,0:T(8,128)(2,1)}) %reduce-scatter.4.cloned.1.call-update) | async-done | bytes 294928 | tf_op jit(solution)/shard_map/reduce_scatter | solution.py:1803
  293.0 4.2 %collective-permute-done.35 = bf16[64,1152]{1,0:T(8,128)(2,1)S(1)} collective-permute-done((bf16[64,1152]{1,0:T(8,128)(2,1)S(1)}, bf16[64,1152]{1,0:T(8,128)(2,1)S(1)}, u32[]{:S(2)}, u32[]{:S(2)}) %collective-permute-start.35) | collective-permute-done | bytes 147488 | tf_op jit(solution)/shard_map/ppermute | solution.py:481
  299.8 9.6 %all-to-all-done.3 = bf16[8,64,1024]{2,1,0:T(8,128)(2,1)} async-done(((bf16[8,64,1024]{2,1,0:T(8,128)(2,1)}), bf16[8,64,1024]{2,1,0:T(8,128)(2,1)}, u32[]{:S(2)}, u32[]{:S(2)}) %all-to-all-start.3) | async-done | bytes 1048608 | tf_op jit(solution)/shard_map/all_to_all | solution.py:1809
  310.1 3.5 %all-to-all-start.4 = ((bf16[4,2,64,1024]{3,2,1,0:T(8,128)(2,1)}), bf16[4,2,64,1024]{3,2,1,0:T(8,128)(2,1)S(1)}, u32[]{:S(2)}, u32[]{:S(2)}) async-start(bf16[4,2,64,1024]{3,2,1,0:T(8,128)(2,1)} %bitcast.16), calls=%async_computation.7 | async-start | bytes 2097152 | tf_op jit(solution)/shard_map/all_to_all | solution.py:1816
  313.7 5.8 %spread_feed.1 = (f32[128,4096]{1,0:T(8,128)}, f32[128,4096]{1,0:T(8,128)}, f32[512,1024]{1,0:T(8,128)}, f32[8,128]{1,0:T(8,128)}) custom-call(s32[1]{0:T(128)} %bitcast.refs_0_.refs_8_.refs_2_.refs_5_.refs_3_.refs_14_.refs_16_.refs_10_.rank_ref, bf16[128,3072]{1,0:T(8,128)(2,1)} %copy-done.3, bf16[128,3072]{1,0:T(8,128)(2,1)} %copy-done.8, ...), custom_call_target="tpu_custom_call" | custom-call | flops 2097152 | bytes 16777216 | tf_op jit(solution)/shard_map/spread_feed/pallas_call | solution.py:580
  (245 shorter events, 84.1 us)
Async XLA Ops:
  7.2 40.1 %all-gather.4.cloned.1.call-start = ((), (), s32[]{:S(2)}) async-start(), calls=%async_computation.8 | async-start | bytes 2654208 | tf_op jit(solution)/shard_map/all_gather | solution.py:1719
  11.2 124.6 %all-gather.6.cloned.1.call-start = ((), (), s32[]{:S(2)}) async-start(), calls=%async_computation.9 | async-start | bytes 4718592 | tf_op jit(solution)/shard_map/all_gather | solution.py:1720
  33.5 23.4 %all-to-all-start.1 = ((bf16[8,32,1152]{2,1,0:T(8,128)(2,1)}), bf16[8,32,1152]{2,1,0:T(8,128)(2,1)S(1)}, u32[]{:S(2)}, u32[]{:S(2)}) async-start(bf16[8,32,1152]{2,1,0:T(8,128)(2,1)} %bitcast.8), calls=%async_computation.1 | async-start | bytes 1179648 | tf_op jit(solution)/shard_map/all_to_all | solution.py:523
  38.5 106.6 %all-gather.8.cloned.1.call-start = ((), (), s32[]{:S(2)}) async-start(), calls=%async_computation.10 | async-start | bytes 2359296 | tf_op jit(solution)/shard_map/all_gather | solution.py:1721
  67.5 13.9 %collective-permute-start.3 = (bf16[256,1152]{1,0:T(8,128)(2,1)S(1)}, bf16[256,1152]{1,0:T(8,128)(2,1)S(1)}, u32[]{:S(2)}, u32[]{:S(2)}) collective-permute-start(bf16[256,1152]{1,0:T(8,128)(2,1)S(1)} %pad_maximum_fusion.2.refs_0_.refs_1_), channel_id=1, source_target_pairs={{0,16},{8,24},{16,0},{24,8},{1,17},{9,25},{17,1},{25,9},{2,18},{10... | collective-permute-start | bytes 1769480 | tf_op jit(solution)/shard_map/ppermute | solution.py:481
  68.7 13.7 %collective-permute-start.5 = (bf16[256,1152]{1,0:T(8,128)(2,1)S(1)}, bf16[256,1152]{1,0:T(8,128)(2,1)}, u32[]{:S(2)}, u32[]{:S(2)}) collective-permute-start(bf16[256,1152]{1,0:T(8,128)(2,1)S(1)} %pad_maximum_fusion.3.refs_2_.refs_3_), channel_id=1, source_target_pairs={{0,8},{8,0},{16,24},{24,16},{1,9},{9,1},{17,25},{25,17},{2,10},{10... | collective-permute-start | bytes 1769480 | tf_op jit(solution)/shard_map/ppermute | solution.py:481
  71.5 41.6 %all-to-all-start.2 = ((bf16[8,32,1024]{2,1,0:T(8,128)(2,1)}), bf16[8,32,1024]{2,1,0:T(8,128)(2,1)S(1)}, u32[]{:S(2)}, u32[]{:S(2)}) async-start(bf16[8,32,1024]{2,1,0:T(8,128)(2,1)} %slice.167), calls=%async_computation.2 | async-start | bytes 1048576 | tf_op jit(solution)/shard_map/all_to_all | solution.py:523
  76.2 188.7 %reduce-scatter.8.cloned.1.call-start = ((), (), s32[]{:S(2)}) async-start(), calls=%async_computation.13 | async-start | bytes 2359296 | tf_op jit(solution)/shard_map/reduce_scatter | solution.py:1766
  82.5 18.9 %collective-permute-start.7 = (bf16[1024,256]{1,0:T(8,128)(2,1)S(1)}, bf16[1024,256]{1,0:T(8,128)(2,1)S(1)}, u32[]{:S(2)}, u32[]{:S(2)}) collective-permute-start(bf16[1024,256]{1,0:T(8,128)(2,1)S(1)} %pad_maximum_fusion.5.refs_13_.refs_12_), channel_id=1, source_target_pairs={{0,8},{8,0},{16,24},{24,16},{1,9},{9,1},{17,25},{25,17},{2,10},{10... | collective-permute-start | bytes 1572872 | tf_op jit(solution)/shard_map/ppermute | solution.py:481
  83.6 17.8 %collective-permute-start.6 = (bf16[1024,256]{1,0:T(8,128)(2,1)S(1)}, bf16[1024,256]{1,0:T(8,128)(2,1)S(1)}, u32[]{:S(2)}, u32[]{:S(2)}) collective-permute-start(bf16[1024,256]{1,0:T(8,128)(2,1)S(1)} %pad_maximum_fusion.4.refs_11_.refs_10_), channel_id=1, source_target_pairs={{0,16},{8,24},{16,0},{24,8},{1,17},{9,25},{17,1},{25,9},{2,18},{10... | collective-permute-start | bytes 1572872 | tf_op jit(solution)/shard_map/ppermute | solution.py:481
  109.9 12.0 %collective-permute-start.10 = (bf16[512,512]{1,0:T(8,128)(2,1)S(1)}, bf16[512,512]{1,0:T(8,128)(2,1)S(1)}, u32[]{:S(2)}, u32[]{:S(2)}) collective-permute-start(bf16[512,512]{1,0:T(8,128)(2,1)S(1)} %pad_maximum_fusion.6), channel_id=1, source_target_pairs={{0,16},{8,24},{16,0},{24,8},{1,17},{9,25},{17,1},{25,9},{2,18},{10... | collective-permute-start | bytes 1572872 | tf_op jit(solution)/shard_map/ppermute | solution.py:481
  112.0 10.7 %collective-permute-start.11 = (bf16[512,512]{1,0:T(8,128)(2,1)S(1)}, bf16[512,512]{1,0:T(8,128)(2,1)S(1)}, u32[]{:S(2)}, u32[]{:S(2)}) collective-permute-start(bf16[512,512]{1,0:T(8,128)(2,1)S(1)} %pad_maximum_fusion.7), channel_id=1, source_target_pairs={{0,8},{8,0},{16,24},{24,16},{1,9},{9,1},{17,25},{25,17},{2,10},{10... | collective-permute-start | bytes 1572872 | tf_op jit(solution)/shard_map/ppermute | solution.py:481
  122.8 11.6 %collective-permute-start.13 = (bf16[128,1024]{1,0:T(8,128)(2,1)S(1)}, bf16[128,1024]{1,0:T(8,128)(2,1)S(1)}, u32[]{:S(2)}, u32[]{:S(2)}) collective-permute-start(bf16[128,1024]{1,0:T(8,128)(2,1)S(1)} %get-tuple-element.202), channel_id=1, source_target_pairs={{0,16},{8,24},{16,0},{24,8},{1,17},{9,25},{17,1},{25,9},{2,18},{10... | collective-permute-start | bytes 786440 | tf_op jit(solution)/shard_map/ppermute | solution.py:481
  124.4 9.9 %collective-permute-start.12 = (bf16[128,1024]{1,0:T(8,128)(2,1)S(1)}, bf16[128,1024]{1,0:T(8,128)(2,1)S(1)}, u32[]{:S(2)}, u32[]{:S(2)}) collective-permute-start(bf16[128,1024]{1,0:T(8,128)(2,1)S(1)} %get-tuple-element.203), channel_id=1, source_target_pairs={{0,8},{8,0},{16,24},{24,16},{1,9},{9,1},{17,25},{25,17},{2,10},{10... | collective-permute-start | bytes 786440 | tf_op jit(solution)/shard_map/ppermute | solution.py:481
  134.4 10.7 %collective-permute-start.15 = (bf16[256,1024]{1,0:T(8,128)(2,1)S(1)}, bf16[256,1024]{1,0:T(8,128)(2,1)S(1)}, u32[]{:S(2)}, u32[]{:S(2)}) collective-permute-start(bf16[256,1024]{1,0:T(8,128)(2,1)S(1)} %pad_maximum_fusion.9.refs_7_.refs_2_), channel_id=1, source_target_pairs={{0,8},{8,0},{16,24},{24,16},{1,9},{9,1},{17,25},{25,17},{2,10},{10... | collective-permute-start | bytes 1572872 | tf_op jit(solution)/shard_map/ppermute | solution.py:481
  157.4 107.5 %reduce-scatter.6.cloned.1.call-start = ((), (), s32[]{:S(2)}) async-start(), calls=%async_computation.12 | async-start | bytes 4718592 | tf_op jit(solution)/shard_map/reduce_scatter | solution.py:1771
  158.4 12.4 %collective-permute-start.16 = (bf16[256,1024]{1,0:T(8,128)(2,1)S(1)}, bf16[256,1024]{1,0:T(8,128)(2,1)S(1)}, u32[]{:S(2)}, u32[]{:S(2)}) collective-permute-start(bf16[256,1024]{1,0:T(8,128)(2,1)S(1)} %copy-done.35), channel_id=1, source_target_pairs={{0,16},{8,24},{16,0},{24,8},{1,17},{9,25},{17,1},{25,9},{2,18},{10... | collective-permute-start | bytes 1572872 | tf_op jit(solution)/shard_map/ppermute | solution.py:481
  170.8 12.4 %collective-permute-start.19 = (bf16[128,1024]{1,0:T(8,128)(2,1)S(1)}, bf16[128,1024]{1,0:T(8,128)(2,1)S(1)}, u32[]{:S(2)}, u32[]{:S(2)}) collective-permute-start(bf16[128,1024]{1,0:T(8,128)(2,1)S(1)} %slice_add_fusion), channel_id=1, source_target_pairs={{0,16},{8,24},{16,0},{24,8},{1,17},{9,25},{17,1},{25,9},{2,18},{10... | collective-permute-start | bytes 786440 | tf_op jit(solution)/shard_map/ppermute | solution.py:481
  172.1 11.2 %collective-permute-start.17 = (bf16[128,1024]{1,0:T(8,128)(2,1)S(1)}, bf16[128,1024]{1,0:T(8,128)(2,1)S(1)}, u32[]{:S(2)}, u32[]{:S(2)}) collective-permute-start(bf16[128,1024]{1,0:T(8,128)(2,1)S(1)} %slice_add_fusion.1), channel_id=1, source_target_pairs={{0,8},{8,0},{16,24},{24,16},{1,9},{9,1},{17,25},{25,17},{2,10},{10... | collective-permute-start | bytes 786440 | tf_op jit(solution)/shard_map/ppermute | solution.py:481
  183.2 104.7 %reduce-scatter.4.cloned.1.call-start = ((), (), s32[]{:S(2)}) async-start(), calls=%async_computation.11 | async-start | bytes 2654208 | tf_op jit(solution)/shard_map/reduce_scatter | solution.py:1803
  190.0 10.6 %collective-permute-start.21 = (bf16[256,512]{1,0:T(8,128)(2,1)}, bf16[256,512]{1,0:T(8,128)(2,1)S(1)}, u32[]{:S(2)}, u32[]{:S(2)}) collective-permute-start(bf16[256,512]{1,0:T(8,128)(2,1)} %get-tuple-element.135), channel_id=1, source_target_pairs={{0,16},{8,24},{16,0},{24,8},{1,17},{9,25},{17,1},{25,9},{2,18},{10... | collective-permute-start | bytes 786440 | tf_op jit(solution)/shard_map/ppermute | solution.py:481
  191.9 13.7 %collective-permute-start.22 = (bf16[256,512]{1,0:T(8,128)(2,1)}, bf16[256,512]{1,0:T(8,128)(2,1)S(1)}, u32[]{:S(2)}, u32[]{:S(2)}) collective-permute-start(bf16[256,512]{1,0:T(8,128)(2,1)} %get-tuple-element.136), channel_id=1, source_target_pairs={{0,24},{8,16},{16,8},{24,0},{1,25},{9,17},{17,9},{25,1},{2,26},{10... | collective-permute-start | bytes 786440 | tf_op jit(solution)/shard_map/ppermute | solution.py:481
  205.6 12.8 %collective-permute-start.23 = (bf16[256,1024]{1,0:T(8,128)(2,1)}, bf16[256,1024]{1,0:T(8,128)(2,1)S(1)}, u32[]{:S(2)}, u32[]{:S(2)}) collective-permute-start(bf16[256,1024]{1,0:T(8,128)(2,1)} %get-tuple-element.147), channel_id=1, source_target_pairs={{0,16},{8,24},{16,0},{24,8},{1,17},{9,25},{17,1},{25,9},{2,18},{10... | collective-permute-start | bytes 1572872 | tf_op jit(solution)/shard_map/ppermute | solution.py:481
  205.6 12.8 %collective-permute-start.24 = (bf16[256,1024]{1,0:T(8,128)(2,1)}, bf16[256,1024]{1,0:T(8,128)(2,1)S(1)}, u32[]{:S(2)}, u32[]{:S(2)}) collective-permute-start(bf16[256,1024]{1,0:T(8,128)(2,1)} %get-tuple-element.148), channel_id=1, source_target_pairs={{0,8},{8,0},{16,24},{24,16},{1,9},{9,1},{17,25},{25,17},{2,10},{10... | collective-permute-start | bytes 1572872 | tf_op jit(solution)/shard_map/ppermute | solution.py:481
  218.5 20.0 %collective-permute-start.26 = (bf16[128,1024]{1,0:T(8,128)(2,1)S(1)}, bf16[128,1024]{1,0:T(8,128)(2,1)S(1)}, u32[]{:S(2)}, u32[]{:S(2)}) collective-permute-start(bf16[128,1024]{1,0:T(8,128)(2,1)S(1)} %slice_add_fusion.4), channel_id=1, source_target_pairs={{0,16},{8,24},{16,0},{24,8},{1,17},{9,25},{17,1},{25,9},{2,18},{10... | collective-permute-start | bytes 786440 | tf_op jit(solution)/shard_map/ppermute | solution.py:481
  220.0 18.5 %collective-permute-start.25 = (bf16[128,1024]{1,0:T(8,128)(2,1)S(1)}, bf16[128,1024]{1,0:T(8,128)(2,1)S(1)}, u32[]{:S(2)}, u32[]{:S(2)}) collective-permute-start(bf16[128,1024]{1,0:T(8,128)(2,1)S(1)} %slice_add_fusion.5), channel_id=1, source_target_pairs={{0,8},{8,0},{16,24},{24,16},{1,9},{9,1},{17,25},{25,17},{2,10},{10... | collective-permute-start | bytes 786440 | tf_op jit(solution)/shard_map/ppermute | solution.py:481
  276.1 12.1 %collective-permute-start.32 = (bf16[128,3072]{1,0:T(8,128)(2,1)S(1)}, bf16[128,3072]{1,0:T(8,128)(2,1)S(1)}, u32[]{:S(2)}, u32[]{:S(2)}) collective-permute-start(bf16[128,3072]{1,0:T(8,128)(2,1)S(1)} %pad_maximum_fusion.lower), channel_id=1, source_target_pairs={{0,16},{8,24},{16,0},{24,8},{1,17},{9,25},{17,1},{25,9},{2,18},{10... | collective-permute-start | bytes 2359304 | tf_op jit(solution)/shard_map/ppermute | solution.py:481
  277.4 12.1 %collective-permute-start.34 = (bf16[128,3072]{1,0:T(8,128)(2,1)S(1)}, bf16[128,3072]{1,0:T(8,128)(2,1)S(1)}, u32[]{:S(2)}, u32[]{:S(2)}) collective-permute-start(bf16[128,3072]{1,0:T(8,128)(2,1)S(1)} %pad_maximum_fusion.1.upper), channel_id=1, source_target_pairs={{0,8},{8,0},{16,24},{24,16},{1,9},{9,1},{17,25},{25,17},{2,10},{10... | collective-permute-start | bytes 2359304 | tf_op jit(solution)/shard_map/ppermute | solution.py:481
  278.3 31.0 %all-to-all-start.3 = ((bf16[8,64,1024]{2,1,0:T(8,128)(2,1)}), bf16[8,64,1024]{2,1,0:T(8,128)(2,1)}, u32[]{:S(2)}, u32[]{:S(2)}) async-start(bf16[8,64,1024]{2,1,0:T(8,128)(2,1)} %own_last.1), calls=%async_computation.3 | async-start | bytes 2097152 | tf_op jit(solution)/shard_map/all_to_all | solution.py:1809
  297.2 12.2 %collective-permute-start.36 = (bf16[128,1152]{1,0:T(8,128)(2,1)S(1)}, bf16[128,1152]{1,0:T(8,128)(2,1)S(1)}, u32[]{:S(2)}, u32[]{:S(2)}) collective-permute-start(bf16[128,1152]{1,0:T(8,128)(2,1)S(1)} %pad_maximum_fusion.10.lower), channel_id=1, source_target_pairs={{0,16},{8,24},{16,0},{24,8},{1,17},{9,25},{17,1},{25,9},{2,18},{10... | collective-permute-start | bytes 884744 | tf_op jit(solution)/shard_map/ppermute | solution.py:481
  298.5 10.9 %collective-permute-start.38 = (bf16[128,1152]{1,0:T(8,128)(2,1)S(1)}, bf16[128,1152]{1,0:T(8,128)(2,1)S(1)}, u32[]{:S(2)}, u32[]{:S(2)}) collective-permute-start(bf16[128,1152]{1,0:T(8,128)(2,1)S(1)} %pad_maximum_fusion.11.upper), channel_id=1, source_target_pairs={{0,8},{8,0},{16,24},{24,16},{1,9},{9,1},{17,25},{25,17},{2,10},{10... | collective-permute-start | bytes 884744 | tf_op jit(solution)/shard_map/ppermute | solution.py:481
  310.1 17.4 %all-to-all-start.4 = ((bf16[4,2,64,1024]{3,2,1,0:T(8,128)(2,1)}), bf16[4,2,64,1024]{3,2,1,0:T(8,128)(2,1)S(1)}, u32[]{:S(2)}, u32[]{:S(2)}) async-start(bf16[4,2,64,1024]{3,2,1,0:T(8,128)(2,1)} %bitcast.16), calls=%async_computation.7 | async-start | bytes 2097152 | tf_op jit(solution)/shard_map/all_to_all | solution.py:1816
  (66 other events, 681.3 us)
Sparse Core Ops, SparseCore 0:
  11.3 35.9 all-gather.3
  49.5 60.6 all-gather.5
  111.8 27.6 all-gather.7
  157.5 36.7 reduce-scatter.7
  196.5 48.6 reduce-scatter.5
  251.6 36.2 reduce-scatter.3

commit v3 on v2

--- a/solution.py
+++ b/solution.py
@@ -1128,27 +1128,37 @@
 def feed_body(mixed, gate_up, both, hidden):
     count, _, per = hidden.ref.shape
     mixed.start(0)
-    gate_up.start()
+    gate_up.start(0, 2)
     mixed.start(1, 2, 3)
-
-    def one_chunk(index, carry):
-        mixed.wait_at(index)
-        gate_up_ref = gate_up.wait_first(index)
-        rows = mixed.ref[index]
-        for half in range(2):
-            here = slice(half * per // 2, (half + 1) * per // 2)
-            gate = dot_plain(rows, gate_up_ref[half])
-            up = dot_plain(rows, gate_up_ref[2 + half])
+    gate_up.start(1, 3)
+    for half in range(2):
+        here = slice(half * per // 2, (half + 1) * per // 2)
+        there = slice(per + half * per // 2, per + (half + 1) * per // 2)
+
+        def one_chunk(index, carry, half=half, here=here, there=there):
+            if half == 0:
+                mixed.wait_at(index)
+
+            @pl.when(index == 0)
+            def _():
+                for k in (half, 2 + half):
+                    gate_up.copies[k].wait()
+
+            rows = mixed.ref[index]
+            gate = dot_plain(rows, gate_up.ref[half])
+            up = dot_plain(rows, gate_up.ref[2 + half])
             sigmoid = 1.0 / (1.0 + jnp.exp(-gate))
             silu = gate * sigmoid
             both.ref[index, :, here] = (up * (sigmoid + silu * (1.0 - sigmoid))).astype(LOW)
-            both.ref[index, :, per + half * per // 2 : per + (half + 1) * per // 2] = silu.astype(LOW)
+            both.ref[index, :, there] = silu.astype(LOW)
             hidden.ref[index, :, here] = (silu * up).astype(LOW)
-        both.start_at(index)
-        hidden.start_at(index)
-        return carry
-
-    lax.fori_loop(0, count, one_chunk, 0)
+            if half == 1:
+                both.start_at(index)
+                hidden.start_at(index)
+            return carry
+
+        lax.fori_loop(0, count, one_chunk, 0)
+    gate_up.waited = True
 
 
 def feed(mixed, gate_up, token):
@@ -1277,18 +1287,11 @@
 
 
 def attend_back_body(
-    pair, parcels, q, k, v, wide, logs, cos, sin, query_sides, key_sides, weights_ref,
-    *rest,
+    parcels, turned, wide, logs, cos, sin, query_sides, key_sides, weights_ref, projections,
+    out, bias_ref, back, queries_ref, grads_ref, total_ref,
 ):
-    if pair == 1:
-        before, projections, out, bias_ref, back, *rest, joined_ref = rest
-    else:
-        out, bias_ref, *rest = rest
-    queries_ref, grads_ref, total_ref = rest
-    start_all(parcels, q, query_sides, logs, wide, k, v, key_sides, cos, sin)
-    if pair == 1:
-        start_all(before, projections)
-    length = q.ref.shape[0]
+    start_all(parcels, turned, query_sides, logs, wide, key_sides, cos, sin, projections)
+    length = turned.ref.shape[0]
     chunk = length // 4
     block = chunk // 2
     half_lane = lax.broadcasted_iota(jnp.int32, (chunk, 128), 1) // 64
@@ -1298,34 +1301,37 @@
         for place in range(4):
             to = slice((4 * half + place) * block, (4 * half + place + 1) * block)
             rows = slice(half * block, (half + 1) * block)
-            for head in range(2):
-                grads_ref[head, to, :128] = parcels_ref[order[place], rows, :]
-    q_ref, side_ref, log_ref, wide_ref = q.wait(), query_sides.wait(), logs.wait(), wide.wait()
+            for head in range(4):
+                at = 128 * (head // 2)
+                grads_ref[head, to, :128] = parcels_ref[order[place], rows, at : at + 128]
+    turned_ref, side_ref, log_ref, wide_ref = (
+        turned.wait(), query_sides.wait(), logs.wait(), wide.wait()
+    )
 
     def prepare(index, carry):
         rows = pl.ds(pl.multiple_of(index * chunk, chunk), chunk)
-        product = grads_ref[0, rows, :128].astype(WIDE) * wide_ref[rows, :]
-        scaled = q_ref[rows, :] * LOW(SCORE_SCALE)
-        for half in range(2):
-            head = 2 * pair + half
-            side = side_ref[rows, :] * weights_ref[head : head + 1, :]
-            for place, piece in enumerate(three_parts(-log_ref[rows, head : head + 1])):
-                side = jnp.where(lane == LSE_AT + place, piece, side)
-            queries_ref[half, rows, :128] = jnp.where(half_lane == half, scaled, LOW(0))
-            queries_ref[half, rows, 128:] = side
-            delta = jnp.sum(jnp.where(half_lane == half, product, 0.0), 1, keepdims=True)
-            extra = jnp.zeros((chunk, 128), LOW)
-            for place, piece in enumerate(three_parts(-delta)):
-                extra = jnp.where(lane == place, piece, extra)
-            grads_ref[half, rows, 128:] = extra
-        total_ref[rows, :] = jnp.zeros((chunk, 128), WIDE)
+        for pair in range(2):
+            at = 128 * pair
+            product = grads_ref[2 * pair, rows, :128].astype(WIDE) * wide_ref[rows, at : at + 128]
+            scaled = turned_ref[rows, at : at + 128] * LOW(SCORE_SCALE)
+            for half in range(2):
+                head = 2 * pair + half
+                side = side_ref[rows, :] * weights_ref[head : head + 1, :]
+                for place, piece in enumerate(three_parts(-log_ref[rows, head : head + 1])):
+                    side = jnp.where(lane == LSE_AT + place, piece, side)
+                queries_ref[head, rows, :128] = jnp.where(half_lane == half, scaled, LOW(0))
+                queries_ref[head, rows, 128:] = side
+                delta = jnp.sum(jnp.where(half_lane == half, product, 0.0), 1, keepdims=True)
+                extra = jnp.zeros((chunk, 128), LOW)
+                for place, piece in enumerate(three_parts(-delta)):
+                    extra = jnp.where(lane == place, piece, extra)
+                grads_ref[head, rows, 128:] = extra
+        total_ref[rows, :] = jnp.zeros((chunk, 256), WIDE)
         return carry
 
     lax.fori_loop(0, 4, prepare, 0)
     three_ones = jnp.where(lane < 3, 1.0, 0.0).astype(LOW)
-    k_ref, v_ref, key_ref, cos_ref, sin_ref = (
-        k.wait(), v.wait(), key_sides.wait(), cos.wait(), sin.wait()
-    )
+    key_ref, cos_ref, sin_ref = key_sides.wait(), cos.wait(), sin.wait()
 
     def one_block(index, carry):
         rows = pl.ds(pl.multiple_of(index * chunk, chunk), chunk)
@@ -1334,100 +1340,104 @@
         key_side = key_ref[rows, :]
         first_four = jnp.where(lane < 4, key_side.astype(WIDE), 0.0)
         sums = list(carry)
-        keys = k_ref[rows, :]
-        values = v_ref[rows, :]
-        keys_wide = jnp.concatenate([keys, key_side], 1)
-        grad_keys = jnp.zeros((chunk, 128), WIDE)
-        grad_values = jnp.zeros((chunk, 128), WIDE)
-        for half in range(2):
-            mine = half_lane == half
-            weights = jnp.exp(dot_rows(keys_wide, queries_ref[half]))
-            grad_weights = dot_rows(
-                jnp.concatenate([jnp.where(mine, values, LOW(0)), three_ones], 1), grads_ref[half]
-            )
-            grad_values = jnp.where(
-                mine, dot_plain(weights.astype(LOW), grads_ref[half, :, :128]), grad_values
-            )
-            grad_scores = (weights * grad_weights).astype(LOW)
-            both = dot_plain(
-                grad_scores,
-                jnp.concatenate([queries_ref[half, :, :128], side_ref[...]], 1),
-            )
-            grad_keys = grad_keys + both[:, :128]
-            counted = both[:, 128:]
-            same = jnp.sum(counted * first_four, 0, keepdims=True)
-            every = jnp.sum(jnp.where(lane < 4, counted, 0.0), 0, keepdims=True)
-            sums[half] = sums[half] + same
-            sums[2 + half] = sums[2 + half] + (every - same)
-            total_ref[...] += dot_first(grad_scores, jnp.where(mine, keys, LOW(0)))
-        out.ref[index, :, 128:256] = turn_pair(grad_keys, cosine, sine).astype(LOW)
-        out.ref[index, :, 256:] = grad_values.astype(LOW)
+        for pair in range(2):
+            at = 128 * pair
+            keys = turned_ref[rows, 256 + at : 384 + at]
+            values = turned_ref[rows, 512 + at : 640 + at]
+            keys_wide = jnp.concatenate([keys, key_side], 1)
+            grad_keys = jnp.zeros((chunk, 128), WIDE)
+            grad_values = jnp.zeros((chunk, 128), WIDE)
+            for half in range(2):
+                head = 2 * pair + half
+                mine = half_lane == half
+                weights = jnp.exp(dot_rows(keys_wide, queries_ref[head]))
+                grad_weights = dot_rows(
+                    jnp.concatenate([jnp.where(mine, values, LOW(0)), three_ones], 1),
+                    grads_ref[head],
+                )
+                grad_values = jnp.where(
+                    mine, dot_plain(weights.astype(LOW), grads_ref[head, :, :128]), grad_values
+                )
+                grad_scores = (weights * grad_weights).astype(LOW)
+                both = dot_plain(
+                    grad_scores,
+                    jnp.concatenate([queries_ref[head, :, :128], side_ref[...]], 1),
+                )
+                grad_keys = grad_keys + both[:, :128]
+                counted = both[:, 128:]
+                same = jnp.sum(counted * first_four, 0, keepdims=True)
+                every = jnp.sum(jnp.where(lane < 4, counted, 0.0), 0, keepdims=True)
+                sums[head] = sums[head] + same
+                sums[4 + head] = sums[4 + head] + (every - same)
+                total_ref[:, at : at + 128] += dot_first(
+                    grad_scores, jnp.where(mine, keys, LOW(0))
+                )
+            out.ref[index, :, 256 + at : 384 + at] = turn_pair(grad_keys, cosine, sine).astype(LOW)
+            out.ref[index, :, 512 + at : 640 + at] = grad_values.astype(LOW)
         return tuple(sums)
 
-    start = tuple(jnp.zeros((1, 128), WIDE) for _ in range(4))
+    start = tuple(jnp.zeros((1, 128), WIDE) for _ in range(8))
     sums = lax.fori_loop(0, 4, one_block, start)
-    bias_ref[...] = jnp.zeros_like(bias_ref)
-    for place in range(4):
+    for place in range(8):
         bias_ref[place : place + 1, :] = sums[place]
-    for place in range(4):
-        rows = slice(place * chunk, (place + 1) * chunk)
-        out.ref[place, :, :128] = turn_pair(
-            total_ref[rows, :] * SCORE_SCALE, cos_ref[rows, :], -sin_ref[rows, :]
-        ).astype(LOW)
-    if pair == 0:
-        return
-    out.start()
-    before_ref, projections_ref = before.wait(), projections.wait()
+    projections_ref = projections.wait()
 
     def one_chunk(index, carry):
-        for kind in range(3):
-            here = slice(128 * kind, 128 * (kind + 1))
-            joined_ref[:, 256 * kind : 256 * kind + 128] = before_ref[index, :, here]
-            joined_ref[:, 256 * kind + 128 : 256 * (kind + 1)] = out.ref[index, :, here]
-        back.ref[index] = dot_rows(joined_ref[...], projections_ref[...]).astype(LOW)
+        rows = pl.ds(pl.multiple_of(index * chunk, chunk), chunk)
+        for pair in range(2):
+            at = 128 * pair
+            out.ref[index, :, at : at + 128] = turn_pair(
+                total_ref[rows, at : at + 128] * SCORE_SCALE, cos_ref[rows, :], -sin_ref[rows, :]
+            ).astype(LOW)
+        out.start_at(index)
+        back.ref[index] = dot_rows(out.ref[index], projections_ref[...]).astype(LOW)
         back.start_at(index)
         return carry
 
     lax.fori_loop(0, 4, one_chunk, 0)
 
 
-def attend_back(pair, parcels, kept, weights, token, before=None, first_weights=None):
+def attend_back(parcels, kept, weights, first_weights, token):
     turned, attended, *others = kept
     length = turned.shape[0]
-    at = 128 * pair
     return run(
-        functools.partial(attend_back_body, pair),
+        attend_back_body,
         "attend_back",
-        40,
-        [group(parcels, at, 128)]
-        + [whole(turned, column + at, 128) for column in (0, 256, 512)]
-        + [whole(attended, at, 128)]
+        80,
+        [group(parcels, 0, 256), whole(turned), whole(attended)]
         + [whole(x) for x in others]
-        + [weights]
-        + ([rows_of(before), whole(first_weights, 0, 768)] if pair else []),
-        [out_rows((length, 384), LOW), ((8, 128), WIDE)]
-        + ([out_group((length // 4, D), LOW)] if pair else []),
+        + [weights, whole(first_weights, 0, 768)],
+        [out_rows((length, 768), LOW), ((8, 128), WIDE), out_group((length // 4, D), LOW)],
         [
-            pltpu.VMEM((2, length, 256), LOW),
-            pltpu.VMEM((2, length, 256), LOW),
-            pltpu.VMEM((length, 128), WIDE),
-        ]
-        + ([pltpu.VMEM((length // 4, 768), LOW)] if pair else []),
+            pltpu.VMEM((4, length, 256), LOW),
+            pltpu.VMEM((4, length, 256), LOW),
+            pltpu.VMEM((length, 256), WIDE),
+        ],
         token,
     )
 
 
 def gate_up_grads_body(mixed, near, far, out):
-    start_all(near, far, mixed)
+    mixed.start(0)
+    for k in range(2):
+        near.start(k)
+        far.start(k)
+    mixed.start(1, 2, 3)
+    near.waited = far.waited = True
     chunk = mixed.ref.shape[1] // 4
 
     def one_part(index, carry):
-        near_ref, far_ref = near.wait_first(index), far.wait_first(index)
         mixed.wait_at(index)
         total = None
         for k in range(4):
+            item = (near, far)[k % 2]
+
+            @pl.when(index == 0)
+            def _(item=item, k=k):
+                item.copies[k // 2].wait()
+
             more = dot_first(
-                mixed.ref[index, k * chunk : (k + 1) * chunk, :], (near_ref, far_ref)[k % 2][k // 2]
+                mixed.ref[index, k * chunk : (k + 1) * chunk, :], item.ref[k // 2]
             )
             total = more if total is None else total + more
         out.ref[index] = total.astype(LOW)
@@ -1450,12 +1460,15 @@
 
 def feed_out_body(hidden, down, out):
     start_all(down, hidden)
+    block = out.ref.shape[1]
 
     def one_chunk(index, carry):
         down_ref = down.wait_first(index)
         hidden.wait_at(index)
-        out.ref[index] = dot_plain(hidden.ref[index], down_ref[...]).astype(LOW)
-        out.start_at(index)
+        total = dot_plain(hidden.ref[index], down_ref[...]).astype(LOW)
+        for p in range(2):
+            q = jnp.where(index < 2, 2 * index + p, index - 2 + 2 * p)
+            out.ref[2 * q + index // 2] = total[p * block : (p + 1) * block]
         return carry
 
     lax.fori_loop(0, hidden.ref.shape[0], one_chunk, 0)
@@ -1463,26 +1476,31 @@
 
 def feed_out(hidden, down, token):
     length = hidden.shape[0]
+    block = length // 8
+
+    def pairs(refs, buffer):
+        return [
+            (buffer.at[2 * q + half], ref.at[pl.ds(half * block, block)])
+            for q, ref in enumerate(refs)
+            for half in range(2)
+        ]
+
     return run(
         feed_out_body,
         "feed_out",
         5,
         [rows_of(hidden), whole(down)],
-        [out_group((length // 4, D), LOW)],
+        [Plan([((2 * block, D), LOW)] * 4, (8, block, D), pairs, 8)],
         token=token,
     )
 
 
-def own_last_body(
-    n0, g0, l0, n1, g1, l1, m0, h0, k0, m1, h1, k1, x, base, middle_rows, gain_ref, out
-):
-    start_all(n0, g0, l0, x, base, m0, h0, k0, middle_rows, n1, g1, l1, m1, h1, k1)
+def own_last_body(n0, g0, l0, n1, g1, l1, forward, x, base, middle_rows, gain_ref, out):
+    start_all(n0, g0, l0, x, base, forward, middle_rows, n1, g1, l1)
     block = l0.ref.shape[0]
     piece = out.ref.shape[1] // 2
     each = block // piece
-    for half, (back, forward) in enumerate(
-        (((n0, g0, l0), (m0, h0, k0)), ((n1, g1, l1), (m1, h1, k1)))
-    ):
+    for half, back in enumerate(((n0, g0, l0), (n1, g1, l1))):
         rows = slice(half * block, (half + 1) * block)
         places = slice(half * each, (half + 1) * each)
         turned = sum_arrived(*back) * gain_ref[0:1, :]
@@ -1493,17 +1511,20 @@
             turned - normed * jnp.mean(turned * normed, -1, keepdims=True)
         )
         out.ref[places, :piece, :] = grad.astype(LOW).reshape(each, piece, D)
-        block_rows = sum_arrived(*forward) + middle_rows.wait()[rows, :]
+        block_rows = middle_rows.wait()[rows, :]
+        forward_ref = forward.wait()
+        for q in range(4):
+            block_rows = block_rows + forward_ref[q, rows, :].astype(WIDE)
         out.ref[places, piece:, :] = block_rows.astype(LOW).reshape(each, piece, D)
 
 
-def own_last(sums, out_sums, mine, base, middle_own, gain, n_seq, token):
+def own_last(sums, outs, mine, base, middle_own, gain, n_seq, token):
     quarter = base.shape[0]
     return run(
         own_last_body,
         "own_last",
         80,
-        [*arrivals(sums), *arrivals(out_sums), whole(mine), whole(base), whole(middle_own), gain],
+        [*arrivals(sums), group(outs), whole(mine), whole(base), whole(middle_own), gain],
         [out_whole((n_seq, 2 * quarter // n_seq, D), LOW)],
         token=token,
     )[0]
@@ -1528,48 +1549,39 @@
     )[0]
 
 
-def first_grads_body(rank_ref, mixed, proj0, proj1, heads, parcels, bias_ref, out, joined_ref):
+def first_grads_body(rank_ref, mixed, proj, heads, parcels, bias_ref, out, branch_ref):
     rank = rank_ref[0]
-    start_all(mixed, proj0, proj1, parcels, heads)
-    width = 256
+    start_all(mixed, proj, parcels, heads)
+    width = proj.ref.shape[1]
     block = parcels.ref.shape[1] // 2
-    for pair, proj in enumerate((proj0, proj1)):
-        ref = proj.wait()
-        for kind in range(3):
-            column = width * kind + 128 * pair
-            joined_ref[:, column : column + 128] = ref[:, 128 * kind : 128 * (kind + 1)]
     parcels_ref = parcels.wait()
     for half, order in enumerate((ORDER_A, ORDER_B)):
         for place in range(4):
             to = slice((4 * half + place) * block, (4 * half + place + 1) * block)
-            joined_ref[to, 3 * width :] = parcels_ref[
-                order[place], half * block : (half + 1) * block, :
-            ]
-    mixed_ref, heads_ref = mixed.wait(), heads.wait()
+            branch_ref[to, :] = parcels_ref[order[place], half * block : (half + 1) * block, :]
+    mixed_ref, proj_ref, heads_ref = mixed.wait(), proj.wait(), heads.wait()
 
     def one_part(index, carry):
-        out.ref[index, :, : 3 * width] = dot_first(
-            mixed_ref[index], joined_ref[:, : 3 * width]
+        out.ref[index, :, :width] = dot_first(mixed_ref[index], proj_ref[...]).astype(LOW)
+        out.ref[rank ^ index, :, width : width + 256] = dot_first(
+            heads_ref[index], branch_ref[...]
         ).astype(LOW)
-        out.ref[rank ^ index, :, 3 * width : 4 * width] = dot_first(
-            heads_ref[index], joined_ref[:, 3 * width :]
-        ).astype(LOW)
-        out.ref[index, :, 4 * width :] = bias_ref[...]
+        out.ref[index, :, width + 256 :] = bias_ref[...]
         return carry
 
     lax.fori_loop(0, 4, one_part, 0)
 
 
-def first_grads(rank, mixed, proj0, proj1, heads, parcels, bias_rows, token):
+def first_grads(rank, mixed, proj, heads, parcels, bias_rows, token):
     length = mixed.shape[0]
     return run(
         first_grads_body,
         "first_grads",
         8,
-        [rank, columns_of(mixed), whole(proj0), whole(proj1), columns_of(heads)]
+        [rank, columns_of(mixed), whole(proj), columns_of(heads)]
         + [group(parcels, 256, 256), bias_rows],
         [out_rows((D, 768 + 256 + 128), LOW)],
-        [pltpu.VMEM((length, 1024), LOW)],
+        [pltpu.VMEM((length, 256), LOW)],
         token,
     )[0]
 
@@ -1776,39 +1788,31 @@
         rank_row, sums, middle_own, cot_mine, gain, out_pieces,
         after(rank_row, gate_up_weight_grads),
     )
-    out_chunks = feed_out(hidden, down, after(rank_row, parcels[0]))
+    outs = feed_out(hidden, down, after(rank_row, parcels[0]))
     parcels = [parcels[0]] + [swap(parcels[r], r) for r in range(1, 4)]
 
-    far_chunks = lax.optimization_barrier(((out_chunks[1], out_chunks[3]), parcels))[0]
-    out_got = scatter_first((None, far_chunks[0], None, far_chunks[1]))
-    kept = (turned, attended, *kept)
-    proj0, bias0 = attend_back(
-        0, parcels, kept, weights, after(rank_row, far_chunks)
-    )
-    out_got = lax.optimization_barrier((out_got, bias0))[0]
-    out_sums = scatter_second(out_chunks, out_got)
-    proj1, bias1, *back = attend_back(
-        1, parcels, kept, weights, after(rank_row, out_got), proj0, first_weights
-    )
-    ready = lax.optimization_barrier((back[1], back[3], out_sums[2], out_sums[5]))
+    proj, bias, *back = attend_back(
+        parcels, (turned, attended, *kept), weights, first_weights, after(rank_row, outs[0])
+    )
+    outs = [outs[0]] + [swap(outs[q], q) for q in range(1, 4)]
+    ready = lax.optimization_barrier((back[1], back[3], *outs[1:]))
     got = scatter_first((None, ready[0], None, ready[1]))
-    bias_sums = jnp.sum(jnp.concatenate([bias0[:2], bias1[:2], bias0[2:4], bias1[2:4]], 0), 1)
+    bias_sums = jnp.sum(bias, 1)
     bias_parts = jnp.pad(jnp.concatenate(three_parts(bias_sums)), (0, 104))[None, :]
     slots = lax.broadcasted_iota(jnp.int32, (per, 1), 0) % shard == lax.axis_index("seq")
     bias_rows = jnp.where(slots, bias_parts, LOW(0))
     first_weight_grads = first_grads(
-        rank_row, mixed_first, proj0, proj1, heads, parcels, bias_rows, rank_row
+        rank_row, mixed_first, proj, heads, parcels, bias_rows, rank_row
     )
     got, first_weight_grads = lax.optimization_barrier((got, first_weight_grads))
     first_shard = lax.psum_scatter(first_weight_grads, "seq", scatter_dimension=0, tiled=True)
     sums = scatter_second(back, got)
+    feed_shard = join(gate_up_grad_shard, down_grad_shard, after(rank_row, first_weight_grads))
     last = own_last(
-        sums, out_sums, mine, grad_middle, middle_own, gain, n_seq,
-        after(rank_row, first_weight_grads),
+        sums, outs, mine, grad_middle, middle_own, gain, n_seq, after(rank_row, feed_shard)
     )
     moved = lax.all_to_all(last, "seq", 0, 0, tiled=True)
     quarter = tokens // 4
-    feed_shard = join(gate_up_grad_shard, down_grad_shard, after(rank_row, first_weight_grads))
     feed_pieces = gather_plane(after(feed_shard, last))
     first_pieces = gather_plane(after(first_shard, feed_pieces))
     moved, first_pieces = lax.optimization_barrier((moved, first_pieces))

time: 338 us -> 330 us (0.976)
  waiting for transfers between devices: 87.1 us -> 81.9 us
  Pallas kernels: 129 us -> 125 us
    all_to_all x1, waiting for transfers between devices: 9.61 us -> 4.41 us  [on_plane(): moved = lax.all_to_all(last, 'seq', 0, 0, tiled=True)]
    pallas_call x14 -> x13, Pallas kernels: 120 us -> 116 us  [run(): pl.pallas_call(kernel, out_shape=out_shapes, in_specs=in_specs, out_specs...]
    ppermute x39 -> x38, waiting for transfers between devices: 57.8 us -> 54.6 us  [swap(): return lax.ppermute(value, 'batch', [(i, i ^ bit) for i in range(4)])]
    ppermute x39 -> x38, starting transfers between devices: 42.1 us -> 42.4 us  [swap(): return lax.ppermute(value, 'batch', [(i, i ^ bit) for i in range(4)])]
  transfers between devices with their start and end apart: 49 -> 48, of which waited for: 27 -> 27; matrix products, arithmetic and copies ran while one was open for 5% -> 5% of each run, Pallas kernels for 34% -> 33%
where the time goes in v3:
time: 330 us; the launch traced here: 329 us
  Pallas kernels  125 us (38%)
  waiting for transfers between devices  81.9 us (25%)
  starting transfers between devices  63.3 us (19%)
  blocking collectives  20.7 us (6%)
  local copies, waits for them, and re-layouts  16.4 us (5%)
  between operations  14.8 us (4%)
  other arithmetic  7.26 us (2%)
    pallas_call x13, Pallas kernels, run(): pl.pallas_call(kernel, out_shape=out_shapes, in_specs=in_specs, out_specs...  116 us
    ppermute x38, waiting for transfers between devices, swap(): return lax.ppermute(value, 'batch', [(i, i ^ bit) for i in range(4)])  54.6 us
    ppermute x38, starting transfers between devices, swap(): return lax.ppermute(value, 'batch', [(i, i ^ bit) for i in range(4)])  42.4 us
    all_to_all x1, blocking collectives, on_plane(): packed = lax.all_to_all(packed, 'batch', 0, 0, tiled=True)  20.7 us
    all_to_all x2, starting transfers between devices, over_seq(): lax.all_to_all(pieces, 'seq', 0, 0, tiled=True)  9.71 us
    all_gather x1, waiting for transfers between devices, on_plane(): first_weights = lax.all_gather(first_shard, 'seq', axis=0, tiled=True)  8.76 us
    pallas_call x2, Pallas kernels, call(): pl.pallas_call(kernel, grid=(1,), out_shape=[jax.ShapeDtypeStruct(shape,...  8.63 us
    all_to_all x1, starting transfers between devices, on_plane(): moved = lax.all_to_all(last, 'seq', 0, 0, tiled=True)  7.28 us
  transfers between devices with their start and end apart: 48, of which 27 were waited for; matrix products, arithmetic and copies ran while one was open for 5% of the time, Pallas kernels for 33%

profile of v3, /device:TPU:0, one launch (start us, length us, event | category | flops | bytes accessed | tf_op | source)
XLA Modules:
  0.0 329.4 jit_solution(3356986107849590667)
XLA Ops:
  7.2 3.9 %pack.1 = (bf16[4,2,2,32,1152]{4,3,2,1,0:T(8,128)(2,1)}, bf16[128,1152]{1,0:T(8,128)(2,1)}, bf16[128,2048]{1,0:T(8,128)(2,1)}, bf16[128,1024]{1,0:T(8,128)(2,1)}) custom-call(s32[1]{0:T(128)} %bitcast.refs_0_.refs_8_.refs_2_.refs_5_.refs_3_.refs_14_.refs_13_.refs_9_.rank_ref, bf16[2,4,32,1024]{3,2,1,0:T(8,128)(2,1)} %bitcast.57, ...), custom_call_target="tpu_custom_call" | custom-call | flops 4600000000 | bytes 1048576 | tf_op jit(solution)/shard_map/pack/pallas_call | solution.py:768
  11.9 20.7 %all_to_all.25 = bf16[4,2,2,32,1152]{4,3,2,1,0:T(8,128)(2,1)S(1)} all-to-all(bf16[4,2,2,32,1152]{4,3,2,1,0:T(8,128)(2,1)} %get-tuple-element.95), channel_id=1, replica_groups=mesh['batch'=4,'seq'=8] {'batch'}, dimensions={0} | all-to-all | bytes 2359296 | tf_op jit(solution)/shard_map/all_to_all | solution.py:1734
  33.6 4.9 %all-to-all-start.1 = ((bf16[8,32,1152]{2,1,0:T(8,128)(2,1)}), bf16[8,32,1152]{2,1,0:T(8,128)(2,1)S(1)}, u32[]{:S(2)}, u32[]{:S(2)}) async-start(bf16[8,32,1152]{2,1,0:T(8,128)(2,1)} %bitcast.8), calls=%async_computation.1 | async-start | bytes 1179648 | tf_op jit(solution)/shard_map/all_to_all | solution.py:523
  38.6 8.8 %all-gather.4.cloned.1.call-done.refs_4_.refs_5_.refs_12_ = bf16[1024,1152]{1,0:T(8,128)(2,1)} async-done(((bf16[128,1152]{1,0:T(8,128)(2,1)}), bf16[1024,1152]{1,0:T(8,128)(2,1)}) %all-gather.4.cloned.1.call-update) | async-done | bytes 2359312 | tf_op jit(solution)/shard_map/all_gather | solution.py:1731
  53.5 3.5 %all-to-all-done.1 = bf16[8,32,1152]{2,1,0:T(8,128)(2,1)S(1)} async-done(((bf16[8,32,1152]{2,1,0:T(8,128)(2,1)}), bf16[8,32,1152]{2,1,0:T(8,128)(2,1)S(1)}, u32[]{:S(2)}, u32[]{:S(2)}) %all-to-all-start.1) | async-done | bytes 589856 | tf_op jit(solution)/shard_map/all_to_all | solution.py:523
  61.3 6.1 %collective-permute-done.2 = bf16[128,1152]{1,0:T(8,128)(2,1)S(1)} collective-permute-done((bf16[128,1152]{1,0:T(8,128)(2,1)S(1)}, bf16[128,1152]{1,0:T(8,128)(2,1)S(1)}, u32[]{:S(2)}, u32[]{:S(2)}) %collective-permute-start.2) | collective-permute-done | bytes 294944 | tf_op jit(solution)/shard_map/ppermute | solution.py:481
  71.5 4.8 %all-to-all-start.2 = ((bf16[8,32,1024]{2,1,0:T(8,128)(2,1)}), bf16[8,32,1024]{2,1,0:T(8,128)(2,1)S(1)}, u32[]{:S(2)}, u32[]{:S(2)}) async-start(bf16[8,32,1024]{2,1,0:T(8,128)(2,1)} %slice.135), calls=%async_computation.2 | async-start | bytes 1048576 | tf_op jit(solution)/shard_map/all_to_all | solution.py:523
  76.3 5.1 %collective-permute-done.3.refs_1_.refs_2_ = bf16[256,1152]{1,0:T(8,128)(2,1)S(1)} collective-permute-done((bf16[256,1152]{1,0:T(8,128)(2,1)S(1)}, bf16[256,1152]{1,0:T(8,128)(2,1)S(1)}, u32[]{:S(2)}, u32[]{:S(2)}) %collective-permute-start.3) | collective-permute-done | bytes 589856 | tf_op jit(solution)/shard_map/ppermute | solution.py:481
  84.7 16.7 %attend.1 = (f32[16,1024]{1,0:T(8,128)}, bf16[1024,1024]{1,0:T(8,128)(2,1)}, bf16[1024,768]{1,0:T(8,128)(2,1)}, f32[1024,256]{1,0:T(8,128)}, bf16[512,256]{1,0:T...) custom-call(bf16[256,1152]{1,0:T(8,128)(2,1)} %copy-done.11, ...), custom_call_target="tpu_custom_call" | custom-call | flops 17250000896 | bytes 1048576 | tf_op jit(solution)/shard_map/attend/pallas_call | solution.py:768
  104.2 4.6 %collective-permute-done.8.refs_7_ = bf16[512,256]{1,0:T(8,128)(2,1)S(1)} collective-permute-done((bf16[512,256]{1,0:T(8,128)(2,1)}, bf16[512,256]{1,0:T(8,128)(2,1)S(1)}, u32[]{:S(2)}, u32[]{:S(2)}) %collective-permute-start.8) | collective-permute-done | bytes 262176 | tf_op jit(solution)/shard_map/ppermute | solution.py:481
  113.2 8.8 %collective-permute-done.10.refs_9_ = bf16[512,512]{1,0:T(8,128)(2,1)S(1)} collective-permute-done((bf16[512,512]{1,0:T(8,128)(2,1)S(1)}, bf16[512,512]{1,0:T(8,128)(2,1)S(1)}, u32[]{:S(2)}, u32[]{:S(2)}) %collective-permute-start.10) | collective-permute-done | bytes 524320 | tf_op jit(solution)/shard_map/ppermute | solution.py:481
  125.8 8.6 %middle.1 = (bf16[1024,1024]{1,0:T(8,128)(2,1)}, f32[256,1024]{1,0:T(8,128)}, bf16[1024,1024]{1,0:T(8,128)(2,1)}) custom-call(s32[1]{0:T(128)} %bitcast.refs_0_.refs_8_.refs_2_.refs_5_.refs_3_.refs_14_.refs_13_.refs_9_.rank_ref, bf16[256,1152]{1,0:T(8,128)(2,1)} %copy-done.11, bf16[256,1152]{1,0:T(8,128)(2,1)} %copy-done.26, bf16[256,1152]{1,0:T(8,128)(2,1)} %copy-done.12, ...), custom_call_target="tpu_custom_call" | custom-call | flops 8049999872 | bytes 1048576 | tf_op jit(solution)/shard_map/middle/pallas_call | solution.py:768
  135.8 9.0 %feed.1 = (bf16[1024,2048]{1,0:T(8,128)(2,1)}, bf16[1024,1024]{1,0:T(8,128)(2,1)}) custom-call(bf16[1024,1024]{1,0:T(8,128)(2,1)} %get-tuple-element.107.refs_0_, bf16[1024,2048]{1,0:T(8,128)(2,1)} %all-gather.6.cloned.1.call-done.refs_1_.refs_3_, s32[1]{0:T(128)} %bitcast.refs_0_.refs_8_.refs_2_.refs_5_.refs_3_.refs_14_.refs_13_.refs_9_.rank_ref), custom_call_target="tpu_custom_call" | custom-call | flops 9200000000 | bytes 1048576 | tf_op jit(solution)/shard_map/feed/pallas_call | solution.py:768
  145.8 11.4 %feed_back.2 = (bf16[512,2048]{1,0:T(8,128)(2,1)}, bf16[256,1024]{1,0:T(8,128)(2,1)}, bf16[256,1024]{1,0:T(8,128)(2,1)}, bf16[1024,1024]{1,0:T(8,128)(2,1)}) custom-call(bf16[1024,2048]{1,0:T(8,128)(2,1)} %get-tuple-element.112.refs_0_, bf16[256,1024]{1,0:T(8,128)(2,1)} %copy-done.37, bf16[256,1024]{1,0:T(8,128)(2,1)} %copy-done.36, ...), custom_call_target="tpu_custom_call" | custom-call | flops 13799999488 | bytes 1048576 | tf_op jit(solution)/shard_map/feed_back/pallas_call | solution.py:768
  161.1 7.7 %feed_back.3 = (bf16[512,2048]{1,0:T(8,128)(2,1)}, bf16[256,1024]{1,0:T(8,128)(2,1)}, bf16[256,1024]{1,0:T(8,128)(2,1)}) custom-call(bf16[1024,2048]{1,0:T(8,128)(2,1)} %get-tuple-element.112.refs_0_, bf16[256,1024]{1,0:T(8,128)(2,1)} %copy-done.16, bf16[256,1024]{1,0:T(8,128)(2,1)} %copy-done.15, ...), custom_call_target="tpu_custom_call" | custom-call | flops 8049999872 | bytes 1048576 | tf_op jit(solution)/shard_map/feed_back/pallas_call | solution.py:768
  173.8 8.9 %gate_up_grads.1 = bf16[1024,2048]{1,0:T(8,128)(2,1)} custom-call(bf16[1024,1024]{1,0:T(8,128)(2,1)} %get-tuple-element.107.refs_0_, bf16[512,2048]{1,0:T(8,128)(2,1)} %get-tuple-element.123.refs_1_, bf16[512,2048]{1,0:T(8,128)(2,1)} %get-tuple-element.124.refs_2_, s32[1]{0:T(128)} %bitcast.refs_0_.refs_8_.refs_2_.refs_5_.refs_3_.refs_14_.refs_13_.refs_9_.rank_ref), custom_call_target="tpu_custom_call" | custom-call | flops 9200000000 | bytes 1048576 | tf_op jit(solution)/shard_map/gate_up_grads/pallas_call | solution.py:768
  183.6 5.8 %own_back.1 = (f32[256,1024]{1,0:T(8,128)}, bf16[256,512]{1,0:T(8,128)(2,1)}, bf16[256,512]{1,0:T(8,128)(2,1)}, bf16[256,512]{1,0:T(8,128)(2,1)}, bf16[256,512]{1,0:T(8,128)(2,1)}) custom-call(s32[1]{0:T(128)} %bitcast.refs_0_.refs_8_.refs_2_.refs_5_.refs_3_.refs_14_.refs_13_.refs_9_.rank_ref, bf16[256,1024]{1,0:T(8,128)(2,1)} %get-tuple-element.119.refs_1_, ...), custom_call_target="tpu_custom_call" | custom-call | flops 4600000000 | bytes 1048576 | tf_op jit(solution)/shard_map/own_back/pallas_call | solution.py:768
  192.9 6.5 %feed_out.1 = (bf16[256,1024]{1,0:T(8,128)(2,1)}, bf16[256,1024]{1,0:T(8,128)(2,1)}, bf16[256,1024]{1,0:T(8,128)(2,1)}, bf16[256,1024]{1,0:T(8,128)(2,1)}) custom-call(bf16[1024,1024]{1,0:T(8,128)(2,1)} %get-tuple-element.116.refs_5_.refs_0_, bf16[1024,1024]{1,0:T(8,128)(2,1)} %all-gather.8.cloned.1.call-done.refs_4_.refs_1_, ...), custom_call_target="tpu_custom_call" | custom-call | flops 5750000128 | bytes 1048576 | tf_op jit(solution)/shard_map/feed_out/pallas_call | solution.py:768
  203.0 2.4 collective-permute-done.22.refs_3_.refs_7_
  206.1 21.9 %attend_back.1 = (bf16[1024,768]{1,0:T(8,128)(2,1)}, f32[8,128]{1,0:T(8,128)}, bf16[256,1024]{1,0:T(8,128)(2,1)}, bf16[256,1024]{1,0:T(8,128)(2,1)}, bf16[256,10...) custom-call(bf16[256,512]{1,0:T(8,128)(2,1)} %get-tuple-element.127.refs_0_.refs_4_, bf16[256,512]{1,0:T(8,128)(2,1)} %copy-done.38, ...), custom_call_target="tpu_custom_call" | custom-call | flops 92000002048 | bytes 1048576 | tf_op jit(solution)/shard_map/attend_back/pallas_call | solution.py:768
  230.7 8.5 %first_grads.1 = bf16[1024,1152]{1,0:T(8,128)(2,1)} custom-call(s32[1]{0:T(128)} %bitcast.refs_0_.refs_8_.refs_2_.refs_5_.refs_3_.refs_14_.refs_13_.refs_9_.rank_ref, bf16[1024,1024]{1,0:T(8,128)(2,1)} %get-tuple-element.149.refs_1_, bf16[1024,768]{1,0:T(8,128)(2,1)} %get-tuple-element.150.refs_2_, bf16[1024,1024]{1,0:T(8,128)(2,1)} %get-tuple-element.151.refs_3_, ...), custom_call_target="tpu_custom_call" | custom-call | flops 9200000000 | bytes 1048576 | tf_op jit(solution)/shard_map/first_grads/pallas_call | solution.py:768
  250.1 5.6 %own_last.1 = bf16[8,64,1024]{2,1,0:T(8,128)(2,1)} custom-call(bf16[256,1024]{1,0:T(8,128)(2,1)} %get-tuple-element.141.refs_0_, bf16[256,1024]{1,0:T(8,128)(2,1)} %copy-done.22, bf16[128,1024]{1,0:T(8,128)(2,1)} %copy-done.44, bf16[256,1024]{1,0:T(8,128)(2,1)} %get-tuple-element.154.refs_3_, bf16[256,1024]{1,0:T(8,128)(2,1)} %copy-done.23, ...), custom_call_target="tpu_custom_call" | custom-call | flops 92000002048 | bytes 1048576 | tf_op jit(solution)/shard_map/own_last/pallas_call | solution.py:768
  257.0 7.8 %collective-permute-done.30 = bf16[64,3072]{1,0:T(8,128)(2,1)S(1)} collective-permute-done((bf16[64,3072]{1,0:T(8,128)(2,1)S(1)}, bf16[64,3072]{1,0:T(8,128)(2,1)S(1)}, u32[]{:S(2)}, u32[]{:S(2)}) %collective-permute-start.30) | collective-permute-done | bytes 393248 | tf_op jit(solution)/shard_map/ppermute | solution.py:481
  264.9 3.2 collective-permute-done.32
  268.9 7.3 %all-to-all-start.3 = ((bf16[8,64,1024]{2,1,0:T(8,128)(2,1)}), bf16[8,64,1024]{2,1,0:T(8,128)(2,1)}, u32[]{:S(2)}, u32[]{:S(2)}) async-start(bf16[8,64,1024]{2,1,0:T(8,128)(2,1)} %own_last.1), calls=%async_computation.5 | async-start | bytes 2097152 | tf_op jit(solution)/shard_map/all_to_all | solution.py:1814
  276.1 6.3 %reduce-scatter.8.cloned.1.call-done = bf16[128,1152]{1,0:T(8,128)(2,1)} async-done(((bf16[1024,1152]{1,0:T(8,128)(2,1)}), bf16[128,1152]{1,0:T(8,128)(2,1)}) %reduce-scatter.8.cloned.1.call-update) | async-done | bytes 294928 | tf_op jit(solution)/shard_map/reduce_scatter | solution.py:1808
  293.5 2.7 collective-permute-done.35.lower_far
  298.8 4.4 %all-to-all-done.3 = bf16[8,64,1024]{2,1,0:T(8,128)(2,1)} async-done(((bf16[8,64,1024]{2,1,0:T(8,128)(2,1)}), bf16[8,64,1024]{2,1,0:T(8,128)(2,1)}, u32[]{:S(2)}, u32[]{:S(2)}) %all-to-all-start.3) | async-done | bytes 1048608 | tf_op jit(solution)/shard_map/all_to_all | solution.py:1814
  303.3 3.5 %all-to-all-start.4 = ((bf16[4,2,64,1024]{3,2,1,0:T(8,128)(2,1)}), bf16[4,2,64,1024]{3,2,1,0:T(8,128)(2,1)S(1)}, u32[]{:S(2)}, u32[]{:S(2)}) async-start(bf16[4,2,64,1024]{3,2,1,0:T(8,128)(2,1)} %bitcast.16), calls=%async_computation.7 | async-start | bytes 2097152 | tf_op jit(solution)/shard_map/all_to_all | solution.py:1820
  306.8 5.8 %spread_feed.1 = (f32[128,4096]{1,0:T(8,128)}, f32[128,4096]{1,0:T(8,128)}, f32[512,1024]{1,0:T(8,128)}, f32[8,128]{1,0:T(8,128)}) custom-call(s32[1]{0:T(128)} %bitcast.refs_0_.refs_8_.refs_2_.refs_5_.refs_3_.refs_14_.refs_13_.refs_9_.rank_ref, bf16[128,3072]{1,0:T(8,128)(2,1)} %copy-done.3, bf16[128,3072]{1,0:T(8,128)(2,1)} %copy-done.9, ...), custom_call_target="tpu_custom_call" | custom-call | flops 2097152 | bytes 16777216 | tf_op jit(solution)/shard_map/spread_feed/pallas_call | solution.py:580
  312.6 2.9 spread_first.1
  318.1 2.4 all-to-all-done.4
  (230 shorter events, 84.2 us)
Async XLA Ops:
  7.2 40.1 %all-gather.4.cloned.1.call-start = ((), (), s32[]{:S(2)}) async-start(), calls=%async_computation.8 | async-start | bytes 2654208 | tf_op jit(solution)/shard_map/all_gather | solution.py:1731
  11.2 124.6 %all-gather.6.cloned.1.call-start = ((), (), s32[]{:S(2)}) async-start(), calls=%async_computation.9 | async-start | bytes 4718592 | tf_op jit(solution)/shard_map/all_gather | solution.py:1732
  33.6 23.4 %all-to-all-start.1 = ((bf16[8,32,1152]{2,1,0:T(8,128)(2,1)}), bf16[8,32,1152]{2,1,0:T(8,128)(2,1)S(1)}, u32[]{:S(2)}, u32[]{:S(2)}) async-start(bf16[8,32,1152]{2,1,0:T(8,128)(2,1)} %bitcast.8), calls=%async_computation.1 | async-start | bytes 1179648 | tf_op jit(solution)/shard_map/all_to_all | solution.py:523
  38.5 106.3 %all-gather.8.cloned.1.call-start = ((), (), s32[]{:S(2)}) async-start(), calls=%async_computation.10 | async-start | bytes 2359296 | tf_op jit(solution)/shard_map/all_gather | solution.py:1733
  67.5 13.9 %collective-permute-start.3 = (bf16[256,1152]{1,0:T(8,128)(2,1)S(1)}, bf16[256,1152]{1,0:T(8,128)(2,1)S(1)}, u32[]{:S(2)}, u32[]{:S(2)}) collective-permute-start(bf16[256,1152]{1,0:T(8,128)(2,1)S(1)} %pad_maximum_fusion.2.refs_0_.refs_1_), channel_id=1, source_target_pairs={{0,16},{8,24},{16,0},{24,8},{1,17},{9,25},{17,1},{25,9},{2,18},{10... | collective-permute-start | bytes 1769480 | tf_op jit(solution)/shard_map/ppermute | solution.py:481
  68.7 13.7 %collective-permute-start.5 = (bf16[256,1152]{1,0:T(8,128)(2,1)S(1)}, bf16[256,1152]{1,0:T(8,128)(2,1)}, u32[]{:S(2)}, u32[]{:S(2)}) collective-permute-start(bf16[256,1152]{1,0:T(8,128)(2,1)S(1)} %pad_maximum_fusion.3.refs_2_.refs_3_), channel_id=1, source_target_pairs={{0,8},{8,0},{16,24},{24,16},{1,9},{9,1},{17,25},{25,17},{2,10},{10... | collective-permute-start | bytes 1769480 | tf_op jit(solution)/shard_map/ppermute | solution.py:481
  71.5 41.6 %all-to-all-start.2 = ((bf16[8,32,1024]{2,1,0:T(8,128)(2,1)}), bf16[8,32,1024]{2,1,0:T(8,128)(2,1)S(1)}, u32[]{:S(2)}, u32[]{:S(2)}) async-start(bf16[8,32,1024]{2,1,0:T(8,128)(2,1)} %slice.135), calls=%async_computation.2 | async-start | bytes 1048576 | tf_op jit(solution)/shard_map/all_to_all | solution.py:523
  76.3 167.7 %reduce-scatter.6.cloned.1.call-start = ((), (), s32[]{:S(2)}) async-start(), calls=%async_computation.12 | async-start | bytes 2359296 | tf_op jit(solution)/shard_map/reduce_scatter | solution.py:1778
  82.5 18.9 %collective-permute-start.7 = (bf16[1024,256]{1,0:T(8,128)(2,1)S(1)}, bf16[1024,256]{1,0:T(8,128)(2,1)S(1)}, u32[]{:S(2)}, u32[]{:S(2)}) collective-permute-start(bf16[1024,256]{1,0:T(8,128)(2,1)S(1)} %pad_maximum_fusion.5.refs_13_.refs_12_), channel_id=1, source_target_pairs={{0,8},{8,0},{16,24},{24,16},{1,9},{9,1},{17,25},{25,17},{2,10},{10... | collective-permute-start | bytes 1572872 | tf_op jit(solution)/shard_map/ppermute | solution.py:481
  83.7 17.8 %collective-permute-start.6 = (bf16[1024,256]{1,0:T(8,128)(2,1)S(1)}, bf16[1024,256]{1,0:T(8,128)(2,1)S(1)}, u32[]{:S(2)}, u32[]{:S(2)}) collective-permute-start(bf16[1024,256]{1,0:T(8,128)(2,1)S(1)} %pad_maximum_fusion.4.refs_11_.refs_10_), channel_id=1, source_target_pairs={{0,16},{8,24},{16,0},{24,8},{1,17},{9,25},{17,1},{25,9},{2,18},{10... | collective-permute-start | bytes 1572872 | tf_op jit(solution)/shard_map/ppermute | solution.py:481
  109.9 12.0 %collective-permute-start.10 = (bf16[512,512]{1,0:T(8,128)(2,1)S(1)}, bf16[512,512]{1,0:T(8,128)(2,1)S(1)}, u32[]{:S(2)}, u32[]{:S(2)}) collective-permute-start(bf16[512,512]{1,0:T(8,128)(2,1)S(1)} %pad_maximum_fusion.6), channel_id=1, source_target_pairs={{0,16},{8,24},{16,0},{24,8},{1,17},{9,25},{17,1},{25,9},{2,18},{10... | collective-permute-start | bytes 1572872 | tf_op jit(solution)/shard_map/ppermute | solution.py:481
  112.1 10.7 %collective-permute-start.11 = (bf16[512,512]{1,0:T(8,128)(2,1)S(1)}, bf16[512,512]{1,0:T(8,128)(2,1)S(1)}, u32[]{:S(2)}, u32[]{:S(2)}) collective-permute-start(bf16[512,512]{1,0:T(8,128)(2,1)S(1)} %pad_maximum_fusion.7), channel_id=1, source_target_pairs={{0,8},{8,0},{16,24},{24,16},{1,9},{9,1},{17,25},{25,17},{2,10},{10... | collective-permute-start | bytes 1572872 | tf_op jit(solution)/shard_map/ppermute | solution.py:481
  122.8 11.6 %collective-permute-start.13 = (bf16[128,1024]{1,0:T(8,128)(2,1)S(1)}, bf16[128,1024]{1,0:T(8,128)(2,1)S(1)}, u32[]{:S(2)}, u32[]{:S(2)}) collective-permute-start(bf16[128,1024]{1,0:T(8,128)(2,1)S(1)} %get-tuple-element.190), channel_id=1, source_target_pairs={{0,16},{8,24},{16,0},{24,8},{1,17},{9,25},{17,1},{25,9},{2,18},{10... | collective-permute-start | bytes 786440 | tf_op jit(solution)/shard_map/ppermute | solution.py:481
  134.5 10.3 %collective-permute-start.15 = (bf16[256,1024]{1,0:T(8,128)(2,1)S(1)}, bf16[256,1024]{1,0:T(8,128)(2,1)S(1)}, u32[]{:S(2)}, u32[]{:S(2)}) collective-permute-start(bf16[256,1024]{1,0:T(8,128)(2,1)S(1)} %pad_maximum_fusion.9.refs_7_.refs_2_), channel_id=1, source_target_pairs={{0,8},{8,0},{16,24},{24,16},{1,9},{9,1},{17,25},{25,17},{2,10},{10... | collective-permute-start | bytes 1572872 | tf_op jit(solution)/shard_map/ppermute | solution.py:481
  157.2 87.9 %reduce-scatter.4.cloned.1.call-start = ((), (), s32[]{:S(2)}) async-start(), calls=%async_computation.11 | async-start | bytes 4718592 | tf_op jit(solution)/shard_map/reduce_scatter | solution.py:1783
  158.2 12.4 %collective-permute-start.16 = (bf16[256,1024]{1,0:T(8,128)(2,1)S(1)}, bf16[256,1024]{1,0:T(8,128)(2,1)S(1)}, u32[]{:S(2)}, u32[]{:S(2)}) collective-permute-start(bf16[256,1024]{1,0:T(8,128)(2,1)S(1)} %copy-done.33), channel_id=1, source_target_pairs={{0,16},{8,24},{16,0},{24,8},{1,17},{9,25},{17,1},{25,9},{2,18},{10... | collective-permute-start | bytes 1572872 | tf_op jit(solution)/shard_map/ppermute | solution.py:481
  170.5 12.3 %collective-permute-start.19 = (bf16[128,1024]{1,0:T(8,128)(2,1)S(1)}, bf16[128,1024]{1,0:T(8,128)(2,1)S(1)}, u32[]{:S(2)}, u32[]{:S(2)}) collective-permute-start(bf16[128,1024]{1,0:T(8,128)(2,1)S(1)} %slice_add_fusion), channel_id=1, source_target_pairs={{0,16},{8,24},{16,0},{24,8},{1,17},{9,25},{17,1},{25,9},{2,18},{10... | collective-permute-start | bytes 786440 | tf_op jit(solution)/shard_map/ppermute | solution.py:481
  171.8 11.0 %collective-permute-start.17 = (bf16[128,1024]{1,0:T(8,128)(2,1)S(1)}, bf16[128,1024]{1,0:T(8,128)(2,1)S(1)}, u32[]{:S(2)}, u32[]{:S(2)}) collective-permute-start(bf16[128,1024]{1,0:T(8,128)(2,1)S(1)} %slice_add_fusion.1), channel_id=1, source_target_pairs={{0,8},{8,0},{16,24},{24,16},{1,9},{9,1},{17,25},{25,17},{2,10},{10... | collective-permute-start | bytes 786440 | tf_op jit(solution)/shard_map/ppermute | solution.py:481
  182.8 99.6 %reduce-scatter.8.cloned.1.call-start = ((), (), s32[]{:S(2)}) async-start(), calls=%async_computation.13 | async-start | bytes 2654208 | tf_op jit(solution)/shard_map/reduce_scatter | solution.py:1808
  189.4 12.2 %collective-permute-start.20 = (bf16[256,512]{1,0:T(8,128)(2,1)}, bf16[256,512]{1,0:T(8,128)(2,1)S(1)}, u32[]{:S(2)}, u32[]{:S(2)}) collective-permute-start(bf16[256,512]{1,0:T(8,128)(2,1)} %get-tuple-element.128), channel_id=1, source_target_pairs={{0,8},{8,0},{16,24},{24,16},{1,9},{9,1},{17,25},{25,17},{2,10},{10... | collective-permute-start | bytes 786440 | tf_op jit(solution)/shard_map/ppermute | solution.py:481
  189.5 13.5 %collective-permute-start.21 = (bf16[256,512]{1,0:T(8,128)(2,1)}, bf16[256,512]{1,0:T(8,128)(2,1)S(1)}, u32[]{:S(2)}, u32[]{:S(2)}) collective-permute-start(bf16[256,512]{1,0:T(8,128)(2,1)} %get-tuple-element.129), channel_id=1, source_target_pairs={{0,16},{8,24},{16,0},{24,8},{1,17},{9,25},{17,1},{25,9},{2,18},{10... | collective-permute-start | bytes 786440 | tf_op jit(solution)/shard_map/ppermute | solution.py:481
  191.5 13.9 %collective-permute-start.22 = (bf16[256,512]{1,0:T(8,128)(2,1)}, bf16[256,512]{1,0:T(8,128)(2,1)S(1)}, u32[]{:S(2)}, u32[]{:S(2)}) collective-permute-start(bf16[256,512]{1,0:T(8,128)(2,1)} %get-tuple-element.130), channel_id=1, source_target_pairs={{0,24},{8,16},{16,8},{24,0},{1,25},{9,17},{17,9},{25,1},{2,26},{10... | collective-permute-start | bytes 786440 | tf_op jit(solution)/shard_map/ppermute | solution.py:481
  199.4 30.3 %collective-permute-start.23 = (bf16[256,1024]{1,0:T(8,128)(2,1)}, bf16[256,1024]{1,0:T(8,128)(2,1)S(1)}, u32[]{:S(2)}, u32[]{:S(2)}) collective-permute-start(bf16[256,1024]{1,0:T(8,128)(2,1)} %get-tuple-element.144), channel_id=1, source_target_pairs={{0,8},{8,0},{16,24},{24,16},{1,9},{9,1},{17,25},{25,17},{2,10},{10... | collective-permute-start | bytes 1572872 | tf_op jit(solution)/shard_map/ppermute | solution.py:481
  200.0 29.7 %collective-permute-start.24 = (bf16[256,1024]{1,0:T(8,128)(2,1)}, bf16[256,1024]{1,0:T(8,128)(2,1)S(1)}, u32[]{:S(2)}, u32[]{:S(2)}) collective-permute-start(bf16[256,1024]{1,0:T(8,128)(2,1)} %get-tuple-element.145), channel_id=1, source_target_pairs={{0,16},{8,24},{16,0},{24,8},{1,17},{9,25},{17,1},{25,9},{2,18},{10... | collective-permute-start | bytes 1572872 | tf_op jit(solution)/shard_map/ppermute | solution.py:481
  201.5 28.2 %collective-permute-start.25 = (bf16[256,1024]{1,0:T(8,128)(2,1)}, bf16[256,1024]{1,0:T(8,128)(2,1)S(1)}, u32[]{:S(2)}, u32[]{:S(2)}) collective-permute-start(bf16[256,1024]{1,0:T(8,128)(2,1)} %get-tuple-element.146), channel_id=1, source_target_pairs={{0,24},{8,16},{16,8},{24,0},{1,25},{9,17},{17,9},{25,1},{2,26},{10... | collective-permute-start | bytes 1572872 | tf_op jit(solution)/shard_map/ppermute | solution.py:481
  230.6 10.4 %collective-permute-start.26 = (bf16[256,1024]{1,0:T(8,128)(2,1)}, bf16[256,1024]{1,0:T(8,128)(2,1)S(1)}, u32[]{:S(2)}, u32[]{:S(2)}) collective-permute-start(bf16[256,1024]{1,0:T(8,128)(2,1)} %get-tuple-element.147), channel_id=1, source_target_pairs={{0,16},{8,24},{16,0},{24,8},{1,17},{9,25},{17,1},{25,9},{2,18},{10... | collective-permute-start | bytes 1572872 | tf_op jit(solution)/shard_map/ppermute | solution.py:481
  230.6 10.7 %collective-permute-start.27 = (bf16[256,1024]{1,0:T(8,128)(2,1)}, bf16[256,1024]{1,0:T(8,128)(2,1)S(1)}, u32[]{:S(2)}, u32[]{:S(2)}) collective-permute-start(bf16[256,1024]{1,0:T(8,128)(2,1)} %get-tuple-element.148), channel_id=1, source_target_pairs={{0,8},{8,0},{16,24},{24,16},{1,9},{9,1},{17,25},{25,17},{2,10},{10... | collective-permute-start | bytes 1572872 | tf_op jit(solution)/shard_map/ppermute | solution.py:481
  256.7 11.4 %collective-permute-start.32 = (bf16[64,3072]{1,0:T(8,128)(2,1)S(1)}, bf16[64,3072]{1,0:T(8,128)(2,1)S(1)}, u32[]{:S(2)}, u32[]{:S(2)}) collective-permute-start(bf16[64,3072]{1,0:T(8,128)(2,1)S(1)} %get-tuple-element.184), channel_id=1, source_target_pairs={{0,16},{8,24},{16,0},{24,8},{1,17},{9,25},{17,1},{25,9},{2,18},{10... | collective-permute-start | bytes 1179656 | tf_op jit(solution)/shard_map/ppermute | solution.py:481
  264.8 17.6 %collective-permute-start.31 = (bf16[128,3072]{1,0:T(8,128)(2,1)S(1)}, bf16[128,3072]{1,0:T(8,128)(2,1)S(1)}, u32[]{:S(2)}, u32[]{:S(2)}) collective-permute-start(bf16[128,3072]{1,0:T(8,128)(2,1)S(1)} %pad_maximum_fusion.lower), channel_id=1, source_target_pairs={{0,16},{8,24},{16,0},{24,8},{1,17},{9,25},{17,1},{25,9},{2,18},{10... | collective-permute-start | bytes 2359304 | tf_op jit(solution)/shard_map/ppermute | solution.py:481
  268.2 14.2 %collective-permute-start.33 = (bf16[128,3072]{1,0:T(8,128)(2,1)S(1)}, bf16[128,3072]{1,0:T(8,128)(2,1)S(1)}, u32[]{:S(2)}, u32[]{:S(2)}) collective-permute-start(bf16[128,3072]{1,0:T(8,128)(2,1)S(1)} %pad_maximum_fusion.1.upper), channel_id=1, source_target_pairs={{0,8},{8,0},{16,24},{24,16},{1,9},{9,1},{17,25},{25,17},{2,10},{10... | collective-permute-start | bytes 2359304 | tf_op jit(solution)/shard_map/ppermute | solution.py:481
  268.9 34.4 %all-to-all-start.3 = ((bf16[8,64,1024]{2,1,0:T(8,128)(2,1)}), bf16[8,64,1024]{2,1,0:T(8,128)(2,1)}, u32[]{:S(2)}, u32[]{:S(2)}) async-start(bf16[8,64,1024]{2,1,0:T(8,128)(2,1)} %own_last.1), calls=%async_computation.5 | async-start | bytes 2097152 | tf_op jit(solution)/shard_map/all_to_all | solution.py:1814
  303.3 17.2 %all-to-all-start.4 = ((bf16[4,2,64,1024]{3,2,1,0:T(8,128)(2,1)}), bf16[4,2,64,1024]{3,2,1,0:T(8,128)(2,1)S(1)}, u32[]{:S(2)}, u32[]{:S(2)}) async-start(bf16[4,2,64,1024]{3,2,1,0:T(8,128)(2,1)} %bitcast.16), calls=%async_computation.7 | async-start | bytes 2097152 | tf_op jit(solution)/shard_map/all_to_all | solution.py:1820
  (61 other events, 582.7 us)
Sparse Core Ops, SparseCore 0:
  11.3 35.9 all-gather.3
  49.5 60.6 all-gather.5
  111.8 27.6 all-gather.7
  157.3 36.8 reduce-scatter.5
  196.4 48.6 reduce-scatter.3
  247.2 35.1 reduce-scatter.7

commit v4 on v3

--- a/solution.py
+++ b/solution.py
@@ -1023,6 +1023,8 @@
                 upper.ref[here, at : at + 128] = low_rows
 
         logs.ref[index] = log_rows
+        logs.start_at(index)
+        wide.start_at(index)
         return carry
 
     lax.fori_loop(0, count, one_block, 0)
@@ -1265,12 +1267,14 @@
         grad.ref[rows, :] = cot.wait()[rows, :].astype(WIDE) + scale * (
             turned - normed * jnp.mean(turned * normed, -1, keepdims=True)
         )
+    grad.start()
     low_grad = grad.ref[...].astype(LOW)
     wo_ref = wo.wait()
     for q in range(4):
         place = pl.ds(pl.multiple_of((rank ^ q) * width, width), width)
         parcels.ref[q, :, :width] = dot_rows(low_grad, wo_ref[place, :]).astype(LOW)
         parcels.ref[q, :, width:] = grad.ref[:, place].astype(LOW)
+        parcels.start(q)
 
 
 def own_back(rank, sums, middle_own, cot_own, gain, out_pieces, token):
@@ -1469,6 +1473,7 @@
         for p in range(2):
             q = jnp.where(index < 2, 2 * index + p, index - 2 + 2 * p)
             out.ref[2 * q + index // 2] = total[p * block : (p + 1) * block]
+            out.start_at(2 * q + index // 2)
         return carry
 
     lax.fori_loop(0, hidden.ref.shape[0], one_chunk, 0)

time: 330 us -> 330 us (level)
  no operation moved by 1% of the time
where the time goes in v4:
time: 330 us; the launch traced here: 329 us
  Pallas kernels  124 us (38%)
  waiting for transfers between devices  81.5 us (25%)
  starting transfers between devices  64.1 us (19%)
  blocking collectives  20.7 us (6%)
  local copies, waits for them, and re-layouts  16.4 us (5%)
  between operations  14.8 us (4%)
  other arithmetic  7.26 us (2%)
    pallas_call x13, Pallas kernels, run(): pl.pallas_call(kernel, out_shape=out_shapes, in_specs=in_specs, out_specs...  115 us
    ppermute x38, waiting for transfers between devices, swap(): return lax.ppermute(value, 'batch', [(i, i ^ bit) for i in range(4)])  54.1 us
    ppermute x38, starting transfers between devices, swap(): return lax.ppermute(value, 'batch', [(i, i ^ bit) for i in range(4)])  42.6 us
    all_to_all x1, blocking collectives, on_plane(): packed = lax.all_to_all(packed, 'batch', 0, 0, tiled=True)  20.7 us
    all_to_all x2, starting transfers between devices, over_seq(): lax.all_to_all(pieces, 'seq', 0, 0, tiled=True)  9.71 us
    all_gather x1, waiting for transfers between devices, on_plane(): first_weights = lax.all_gather(first_shard, 'seq', axis=0, tiled=True)  8.76 us
    pallas_call x2, Pallas kernels, call(): pl.pallas_call(kernel, grid=(1,), out_shape=[jax.ShapeDtypeStruct(shape,...  8.63 us
    all_to_all x1, starting transfers between devices, on_plane(): moved = lax.all_to_all(last, 'seq', 0, 0, tiled=True)  7.84 us
  transfers between devices with their start and end apart: 48, of which 27 were waited for; matrix products, arithmetic and copies ran while one was open for 5% of the time, Pallas kernels for 33%

profile of v4, /device:TPU:0, one launch (start us, length us, event | category | flops | bytes accessed | tf_op | source)
XLA Modules:
  0.0 328.7 jit_solution(35084398648551056)
XLA Ops:
  7.2 3.9 %pack.1 = (bf16[4,2,2,32,1152]{4,3,2,1,0:T(8,128)(2,1)}, bf16[128,1152]{1,0:T(8,128)(2,1)}, bf16[128,2048]{1,0:T(8,128)(2,1)}, bf16[128,1024]{1,0:T(8,128)(2,1)}) custom-call(s32[1]{0:T(128)} %bitcast.refs_0_.refs_8_.refs_2_.refs_5_.refs_3_.refs_14_.refs_13_.refs_9_.rank_ref, bf16[2,4,32,1024]{3,2,1,0:T(8,128)(2,1)} %bitcast.57, ...), custom_call_target="tpu_custom_call" | custom-call | flops 4600000000 | bytes 1048576 | tf_op jit(solution)/shard_map/pack/pallas_call | solution.py:768
  11.9 20.7 %all_to_all.25 = bf16[4,2,2,32,1152]{4,3,2,1,0:T(8,128)(2,1)S(1)} all-to-all(bf16[4,2,2,32,1152]{4,3,2,1,0:T(8,128)(2,1)} %get-tuple-element.95), channel_id=1, replica_groups=mesh['batch'=4,'seq'=8] {'batch'}, dimensions={0} | all-to-all | bytes 2359296 | tf_op jit(solution)/shard_map/all_to_all | solution.py:1739
  33.6 4.9 %all-to-all-start.1 = ((bf16[8,32,1152]{2,1,0:T(8,128)(2,1)}), bf16[8,32,1152]{2,1,0:T(8,128)(2,1)S(1)}, u32[]{:S(2)}, u32[]{:S(2)}) async-start(bf16[8,32,1152]{2,1,0:T(8,128)(2,1)} %bitcast.8), calls=%async_computation.1 | async-start | bytes 1179648 | tf_op jit(solution)/shard_map/all_to_all | solution.py:523
  38.6 8.8 %all-gather.4.cloned.1.call-done.refs_4_.refs_5_.refs_12_ = bf16[1024,1152]{1,0:T(8,128)(2,1)} async-done(((bf16[128,1152]{1,0:T(8,128)(2,1)}), bf16[1024,1152]{1,0:T(8,128)(2,1)}) %all-gather.4.cloned.1.call-update) | async-done | bytes 2359312 | tf_op jit(solution)/shard_map/all_gather | solution.py:1736
  53.5 3.5 %all-to-all-done.1 = bf16[8,32,1152]{2,1,0:T(8,128)(2,1)S(1)} async-done(((bf16[8,32,1152]{2,1,0:T(8,128)(2,1)}), bf16[8,32,1152]{2,1,0:T(8,128)(2,1)S(1)}, u32[]{:S(2)}, u32[]{:S(2)}) %all-to-all-start.1) | async-done | bytes 589856 | tf_op jit(solution)/shard_map/all_to_all | solution.py:523
  61.3 6.1 %collective-permute-done.2 = bf16[128,1152]{1,0:T(8,128)(2,1)S(1)} collective-permute-done((bf16[128,1152]{1,0:T(8,128)(2,1)S(1)}, bf16[128,1152]{1,0:T(8,128)(2,1)S(1)}, u32[]{:S(2)}, u32[]{:S(2)}) %collective-permute-start.2) | collective-permute-done | bytes 294944 | tf_op jit(solution)/shard_map/ppermute | solution.py:481
  71.5 4.8 %all-to-all-start.2 = ((bf16[8,32,1024]{2,1,0:T(8,128)(2,1)}), bf16[8,32,1024]{2,1,0:T(8,128)(2,1)S(1)}, u32[]{:S(2)}, u32[]{:S(2)}) async-start(bf16[8,32,1024]{2,1,0:T(8,128)(2,1)} %slice.135), calls=%async_computation.2 | async-start | bytes 1048576 | tf_op jit(solution)/shard_map/all_to_all | solution.py:523
  76.3 5.1 %collective-permute-done.3.refs_1_.refs_2_ = bf16[256,1152]{1,0:T(8,128)(2,1)S(1)} collective-permute-done((bf16[256,1152]{1,0:T(8,128)(2,1)S(1)}, bf16[256,1152]{1,0:T(8,128)(2,1)S(1)}, u32[]{:S(2)}, u32[]{:S(2)}) %collective-permute-start.3) | collective-permute-done | bytes 589856 | tf_op jit(solution)/shard_map/ppermute | solution.py:481
  84.7 16.4 %attend.1 = (f32[16,1024]{1,0:T(8,128)}, bf16[1024,1024]{1,0:T(8,128)(2,1)}, bf16[1024,768]{1,0:T(8,128)(2,1)}, f32[1024,256]{1,0:T(8,128)}, bf16[512,256]{1,0:T...) custom-call(bf16[256,1152]{1,0:T(8,128)(2,1)} %copy-done.11, ...), custom_call_target="tpu_custom_call" | custom-call | flops 17250000896 | bytes 1048576 | tf_op jit(solution)/shard_map/attend/pallas_call | solution.py:768
  103.8 4.6 %collective-permute-done.8.refs_7_ = bf16[512,256]{1,0:T(8,128)(2,1)S(1)} collective-permute-done((bf16[512,256]{1,0:T(8,128)(2,1)}, bf16[512,256]{1,0:T(8,128)(2,1)S(1)}, u32[]{:S(2)}, u32[]{:S(2)}) %collective-permute-start.8) | collective-permute-done | bytes 262176 | tf_op jit(solution)/shard_map/ppermute | solution.py:481
  112.8 8.8 %collective-permute-done.10.refs_9_ = bf16[512,512]{1,0:T(8,128)(2,1)S(1)} collective-permute-done((bf16[512,512]{1,0:T(8,128)(2,1)S(1)}, bf16[512,512]{1,0:T(8,128)(2,1)S(1)}, u32[]{:S(2)}, u32[]{:S(2)}) %collective-permute-start.10) | collective-permute-done | bytes 524320 | tf_op jit(solution)/shard_map/ppermute | solution.py:481
  125.4 8.6 %middle.1 = (bf16[1024,1024]{1,0:T(8,128)(2,1)}, f32[256,1024]{1,0:T(8,128)}, bf16[1024,1024]{1,0:T(8,128)(2,1)}) custom-call(s32[1]{0:T(128)} %bitcast.refs_0_.refs_8_.refs_2_.refs_5_.refs_3_.refs_14_.refs_13_.refs_9_.rank_ref, bf16[256,1152]{1,0:T(8,128)(2,1)} %copy-done.11, bf16[256,1152]{1,0:T(8,128)(2,1)} %copy-done.26, bf16[256,1152]{1,0:T(8,128)(2,1)} %copy-done.12, ...), custom_call_target="tpu_custom_call" | custom-call | flops 8049999872 | bytes 1048576 | tf_op jit(solution)/shard_map/middle/pallas_call | solution.py:768
  135.4 9.0 %feed.1 = (bf16[1024,2048]{1,0:T(8,128)(2,1)}, bf16[1024,1024]{1,0:T(8,128)(2,1)}) custom-call(bf16[1024,1024]{1,0:T(8,128)(2,1)} %get-tuple-element.107.refs_0_, bf16[1024,2048]{1,0:T(8,128)(2,1)} %all-gather.6.cloned.1.call-done.refs_1_.refs_3_, s32[1]{0:T(128)} %bitcast.refs_0_.refs_8_.refs_2_.refs_5_.refs_3_.refs_14_.refs_13_.refs_9_.rank_ref), custom_call_target="tpu_custom_call" | custom-call | flops 9200000000 | bytes 1048576 | tf_op jit(solution)/shard_map/feed/pallas_call | solution.py:768
  145.4 11.4 %feed_back.2 = (bf16[512,2048]{1,0:T(8,128)(2,1)}, bf16[256,1024]{1,0:T(8,128)(2,1)}, bf16[256,1024]{1,0:T(8,128)(2,1)}, bf16[1024,1024]{1,0:T(8,128)(2,1)}) custom-call(bf16[1024,2048]{1,0:T(8,128)(2,1)} %get-tuple-element.112.refs_0_, bf16[256,1024]{1,0:T(8,128)(2,1)} %copy-done.37, bf16[256,1024]{1,0:T(8,128)(2,1)} %copy-done.36, ...), custom_call_target="tpu_custom_call" | custom-call | flops 13799999488 | bytes 1048576 | tf_op jit(solution)/shard_map/feed_back/pallas_call | solution.py:768
  160.7 7.7 %feed_back.3 = (bf16[512,2048]{1,0:T(8,128)(2,1)}, bf16[256,1024]{1,0:T(8,128)(2,1)}, bf16[256,1024]{1,0:T(8,128)(2,1)}) custom-call(bf16[1024,2048]{1,0:T(8,128)(2,1)} %get-tuple-element.112.refs_0_, bf16[256,1024]{1,0:T(8,128)(2,1)} %copy-done.16, bf16[256,1024]{1,0:T(8,128)(2,1)} %copy-done.15, ...), custom_call_target="tpu_custom_call" | custom-call | flops 8049999872 | bytes 1048576 | tf_op jit(solution)/shard_map/feed_back/pallas_call | solution.py:768
  172.8 8.9 %gate_up_grads.1 = bf16[1024,2048]{1,0:T(8,128)(2,1)} custom-call(bf16[1024,1024]{1,0:T(8,128)(2,1)} %get-tuple-element.107.refs_0_, bf16[512,2048]{1,0:T(8,128)(2,1)} %get-tuple-element.123.refs_1_, bf16[512,2048]{1,0:T(8,128)(2,1)} %get-tuple-element.124.refs_2_, s32[1]{0:T(128)} %bitcast.refs_0_.refs_8_.refs_2_.refs_5_.refs_3_.refs_14_.refs_13_.refs_9_.rank_ref), custom_call_target="tpu_custom_call" | custom-call | flops 9200000000 | bytes 1048576 | tf_op jit(solution)/shard_map/gate_up_grads/pallas_call | solution.py:768
  182.6 5.6 %own_back.1 = (f32[256,1024]{1,0:T(8,128)}, bf16[256,512]{1,0:T(8,128)(2,1)}, bf16[256,512]{1,0:T(8,128)(2,1)}, bf16[256,512]{1,0:T(8,128)(2,1)}, bf16[256,512]{1,0:T(8,128)(2,1)}) custom-call(s32[1]{0:T(128)} %bitcast.refs_0_.refs_8_.refs_2_.refs_5_.refs_3_.refs_14_.refs_13_.refs_9_.rank_ref, bf16[256,1024]{1,0:T(8,128)(2,1)} %get-tuple-element.119.refs_1_, ...), custom_call_target="tpu_custom_call" | custom-call | flops 4600000000 | bytes 1048576 | tf_op jit(solution)/shard_map/own_back/pallas_call | solution.py:768
  191.8 5.9 %feed_out.1 = (bf16[256,1024]{1,0:T(8,128)(2,1)}, bf16[256,1024]{1,0:T(8,128)(2,1)}, bf16[256,1024]{1,0:T(8,128)(2,1)}, bf16[256,1024]{1,0:T(8,128)(2,1)}) custom-call(bf16[1024,1024]{1,0:T(8,128)(2,1)} %get-tuple-element.116.refs_5_.refs_0_, bf16[1024,1024]{1,0:T(8,128)(2,1)} %all-gather.8.cloned.1.call-done.refs_4_.refs_1_, ...), custom_call_target="tpu_custom_call" | custom-call | flops 5750000128 | bytes 1048576 | tf_op jit(solution)/shard_map/feed_out/pallas_call | solution.py:768
  201.3 2.5 collective-permute-done.22.refs_3_.refs_7_
  204.5 21.9 %attend_back.1 = (bf16[1024,768]{1,0:T(8,128)(2,1)}, f32[8,128]{1,0:T(8,128)}, bf16[256,1024]{1,0:T(8,128)(2,1)}, bf16[256,1024]{1,0:T(8,128)(2,1)}, bf16[256,10...) custom-call(bf16[256,512]{1,0:T(8,128)(2,1)} %get-tuple-element.127.refs_0_.refs_4_, bf16[256,512]{1,0:T(8,128)(2,1)} %copy-done.38, ...), custom_call_target="tpu_custom_call" | custom-call | flops 92000002048 | bytes 1048576 | tf_op jit(solution)/shard_map/attend_back/pallas_call | solution.py:768
  229.1 8.5 %first_grads.1 = bf16[1024,1152]{1,0:T(8,128)(2,1)} custom-call(s32[1]{0:T(128)} %bitcast.refs_0_.refs_8_.refs_2_.refs_5_.refs_3_.refs_14_.refs_13_.refs_9_.rank_ref, bf16[1024,1024]{1,0:T(8,128)(2,1)} %get-tuple-element.149.refs_1_, bf16[1024,768]{1,0:T(8,128)(2,1)} %get-tuple-element.150.refs_2_, bf16[1024,1024]{1,0:T(8,128)(2,1)} %get-tuple-element.151.refs_3_, ...), custom_call_target="tpu_custom_call" | custom-call | flops 9200000000 | bytes 1048576 | tf_op jit(solution)/shard_map/first_grads/pallas_call | solution.py:768
  237.6 2.5 collective-permute-done.26.refs_1_
  249.3 5.6 %own_last.1 = bf16[8,64,1024]{2,1,0:T(8,128)(2,1)} custom-call(bf16[256,1024]{1,0:T(8,128)(2,1)} %get-tuple-element.141.refs_0_, bf16[256,1024]{1,0:T(8,128)(2,1)} %copy-done.22, bf16[128,1024]{1,0:T(8,128)(2,1)} %copy-done.44, bf16[256,1024]{1,0:T(8,128)(2,1)} %get-tuple-element.154.refs_3_, bf16[256,1024]{1,0:T(8,128)(2,1)} %copy-done.23, ...), custom_call_target="tpu_custom_call" | custom-call | flops 92000002048 | bytes 1048576 | tf_op jit(solution)/shard_map/own_last/pallas_call | solution.py:768
  256.2 7.0 %collective-permute-done.30 = bf16[64,3072]{1,0:T(8,128)(2,1)S(1)} collective-permute-done((bf16[64,3072]{1,0:T(8,128)(2,1)S(1)}, bf16[64,3072]{1,0:T(8,128)(2,1)S(1)}, u32[]{:S(2)}, u32[]{:S(2)}) %collective-permute-start.30) | collective-permute-done | bytes 393248 | tf_op jit(solution)/shard_map/ppermute | solution.py:481
  263.6 3.6 %collective-permute-done.32 = bf16[64,3072]{1,0:T(8,128)(2,1)S(1)} collective-permute-done((bf16[64,3072]{1,0:T(8,128)(2,1)S(1)}, bf16[64,3072]{1,0:T(8,128)(2,1)S(1)}, u32[]{:S(2)}, u32[]{:S(2)}) %collective-permute-start.32) | collective-permute-done | bytes 393248 | tf_op jit(solution)/shard_map/ppermute | solution.py:481
  267.3 7.8 %all-to-all-start.3 = ((bf16[8,64,1024]{2,1,0:T(8,128)(2,1)}), bf16[8,64,1024]{2,1,0:T(8,128)(2,1)}, u32[]{:S(2)}, u32[]{:S(2)}) async-start(bf16[8,64,1024]{2,1,0:T(8,128)(2,1)} %own_last.1), calls=%async_computation.5 | async-start | bytes 2097152 | tf_op jit(solution)/shard_map/all_to_all | solution.py:1819
  275.1 6.3 %reduce-scatter.8.cloned.1.call-done = bf16[128,1152]{1,0:T(8,128)(2,1)} async-done(((bf16[1024,1152]{1,0:T(8,128)(2,1)}), bf16[128,1152]{1,0:T(8,128)(2,1)}) %reduce-scatter.8.cloned.1.call-update) | async-done | bytes 294928 | tf_op jit(solution)/shard_map/reduce_scatter | solution.py:1813
  298.4 4.0 %all-to-all-done.3 = bf16[8,64,1024]{2,1,0:T(8,128)(2,1)} async-done(((bf16[8,64,1024]{2,1,0:T(8,128)(2,1)}), bf16[8,64,1024]{2,1,0:T(8,128)(2,1)}, u32[]{:S(2)}, u32[]{:S(2)}) %all-to-all-start.3) | async-done | bytes 1048608 | tf_op jit(solution)/shard_map/all_to_all | solution.py:1819
  302.4 3.5 %all-to-all-start.4 = ((bf16[4,2,64,1024]{3,2,1,0:T(8,128)(2,1)}), bf16[4,2,64,1024]{3,2,1,0:T(8,128)(2,1)S(1)}, u32[]{:S(2)}, u32[]{:S(2)}) async-start(bf16[4,2,64,1024]{3,2,1,0:T(8,128)(2,1)} %bitcast.16), calls=%async_computation.7 | async-start | bytes 2097152 | tf_op jit(solution)/shard_map/all_to_all | solution.py:1825
  306.0 5.8 %spread_feed.1 = (f32[128,4096]{1,0:T(8,128)}, f32[128,4096]{1,0:T(8,128)}, f32[512,1024]{1,0:T(8,128)}, f32[8,128]{1,0:T(8,128)}) custom-call(s32[1]{0:T(128)} %bitcast.refs_0_.refs_8_.refs_2_.refs_5_.refs_3_.refs_14_.refs_13_.refs_9_.rank_ref, bf16[128,3072]{1,0:T(8,128)(2,1)} %copy-done.3, bf16[128,3072]{1,0:T(8,128)(2,1)} %copy-done.9, ...), custom_call_target="tpu_custom_call" | custom-call | flops 2097152 | bytes 16777216 | tf_op jit(solution)/shard_map/spread_feed/pallas_call | solution.py:580
  311.7 2.9 spread_first.1
  317.2 2.6 all-to-all-done.4
  (230 shorter events, 84.7 us)
Async XLA Ops:
  7.2 40.1 %all-gather.4.cloned.1.call-start = ((), (), s32[]{:S(2)}) async-start(), calls=%async_computation.8 | async-start | bytes 2654208 | tf_op jit(solution)/shard_map/all_gather | solution.py:1736
  11.2 124.2 %all-gather.6.cloned.1.call-start = ((), (), s32[]{:S(2)}) async-start(), calls=%async_computation.9 | async-start | bytes 4718592 | tf_op jit(solution)/shard_map/all_gather | solution.py:1737
  33.6 23.4 %all-to-all-start.1 = ((bf16[8,32,1152]{2,1,0:T(8,128)(2,1)}), bf16[8,32,1152]{2,1,0:T(8,128)(2,1)S(1)}, u32[]{:S(2)}, u32[]{:S(2)}) async-start(bf16[8,32,1152]{2,1,0:T(8,128)(2,1)} %bitcast.8), calls=%async_computation.1 | async-start | bytes 1179648 | tf_op jit(solution)/shard_map/all_to_all | solution.py:523
  38.5 105.9 %all-gather.8.cloned.1.call-start = ((), (), s32[]{:S(2)}) async-start(), calls=%async_computation.10 | async-start | bytes 2359296 | tf_op jit(solution)/shard_map/all_gather | solution.py:1738
  67.5 13.9 %collective-permute-start.3 = (bf16[256,1152]{1,0:T(8,128)(2,1)S(1)}, bf16[256,1152]{1,0:T(8,128)(2,1)S(1)}, u32[]{:S(2)}, u32[]{:S(2)}) collective-permute-start(bf16[256,1152]{1,0:T(8,128)(2,1)S(1)} %pad_maximum_fusion.2.refs_0_.refs_1_), channel_id=1, source_target_pairs={{0,16},{8,24},{16,0},{24,8},{1,17},{9,25},{17,1},{25,9},{2,18},{10... | collective-permute-start | bytes 1769480 | tf_op jit(solution)/shard_map/ppermute | solution.py:481
  68.7 13.7 %collective-permute-start.5 = (bf16[256,1152]{1,0:T(8,128)(2,1)S(1)}, bf16[256,1152]{1,0:T(8,128)(2,1)}, u32[]{:S(2)}, u32[]{:S(2)}) collective-permute-start(bf16[256,1152]{1,0:T(8,128)(2,1)S(1)} %pad_maximum_fusion.3.refs_2_.refs_3_), channel_id=1, source_target_pairs={{0,8},{8,0},{16,24},{24,16},{1,9},{9,1},{17,25},{25,17},{2,10},{10... | collective-permute-start | bytes 1769480 | tf_op jit(solution)/shard_map/ppermute | solution.py:481
  71.5 41.3 %all-to-all-start.2 = ((bf16[8,32,1024]{2,1,0:T(8,128)(2,1)}), bf16[8,32,1024]{2,1,0:T(8,128)(2,1)S(1)}, u32[]{:S(2)}, u32[]{:S(2)}) async-start(bf16[8,32,1024]{2,1,0:T(8,128)(2,1)} %slice.135), calls=%async_computation.2 | async-start | bytes 1048576 | tf_op jit(solution)/shard_map/all_to_all | solution.py:523
  76.3 167.0 %reduce-scatter.6.cloned.1.call-start = ((), (), s32[]{:S(2)}) async-start(), calls=%async_computation.12 | async-start | bytes 2359296 | tf_op jit(solution)/shard_map/reduce_scatter | solution.py:1783
  82.5 18.6 %collective-permute-start.7 = (bf16[1024,256]{1,0:T(8,128)(2,1)S(1)}, bf16[1024,256]{1,0:T(8,128)(2,1)S(1)}, u32[]{:S(2)}, u32[]{:S(2)}) collective-permute-start(bf16[1024,256]{1,0:T(8,128)(2,1)S(1)} %pad_maximum_fusion.5.refs_13_.refs_12_), channel_id=1, source_target_pairs={{0,8},{8,0},{16,24},{24,16},{1,9},{9,1},{17,25},{25,17},{2,10},{10... | collective-permute-start | bytes 1572872 | tf_op jit(solution)/shard_map/ppermute | solution.py:481
  83.7 17.5 %collective-permute-start.6 = (bf16[1024,256]{1,0:T(8,128)(2,1)S(1)}, bf16[1024,256]{1,0:T(8,128)(2,1)S(1)}, u32[]{:S(2)}, u32[]{:S(2)}) collective-permute-start(bf16[1024,256]{1,0:T(8,128)(2,1)S(1)} %pad_maximum_fusion.4.refs_11_.refs_10_), channel_id=1, source_target_pairs={{0,16},{8,24},{16,0},{24,8},{1,17},{9,25},{17,1},{25,9},{2,18},{10... | collective-permute-start | bytes 1572872 | tf_op jit(solution)/shard_map/ppermute | solution.py:481
  109.6 12.0 %collective-permute-start.10 = (bf16[512,512]{1,0:T(8,128)(2,1)S(1)}, bf16[512,512]{1,0:T(8,128)(2,1)S(1)}, u32[]{:S(2)}, u32[]{:S(2)}) collective-permute-start(bf16[512,512]{1,0:T(8,128)(2,1)S(1)} %pad_maximum_fusion.6), channel_id=1, source_target_pairs={{0,16},{8,24},{16,0},{24,8},{1,17},{9,25},{17,1},{25,9},{2,18},{10... | collective-permute-start | bytes 1572872 | tf_op jit(solution)/shard_map/ppermute | solution.py:481
  111.7 10.7 %collective-permute-start.11 = (bf16[512,512]{1,0:T(8,128)(2,1)S(1)}, bf16[512,512]{1,0:T(8,128)(2,1)S(1)}, u32[]{:S(2)}, u32[]{:S(2)}) collective-permute-start(bf16[512,512]{1,0:T(8,128)(2,1)S(1)} %pad_maximum_fusion.7), channel_id=1, source_target_pairs={{0,8},{8,0},{16,24},{24,16},{1,9},{9,1},{17,25},{25,17},{2,10},{10... | collective-permute-start | bytes 1572872 | tf_op jit(solution)/shard_map/ppermute | solution.py:481
  122.4 11.6 %collective-permute-start.13 = (bf16[128,1024]{1,0:T(8,128)(2,1)S(1)}, bf16[128,1024]{1,0:T(8,128)(2,1)S(1)}, u32[]{:S(2)}, u32[]{:S(2)}) collective-permute-start(bf16[128,1024]{1,0:T(8,128)(2,1)S(1)} %get-tuple-element.190), channel_id=1, source_target_pairs={{0,16},{8,24},{16,0},{24,8},{1,17},{9,25},{17,1},{25,9},{2,18},{10... | collective-permute-start | bytes 786440 | tf_op jit(solution)/shard_map/ppermute | solution.py:481
  134.1 10.3 %collective-permute-start.15 = (bf16[256,1024]{1,0:T(8,128)(2,1)S(1)}, bf16[256,1024]{1,0:T(8,128)(2,1)S(1)}, u32[]{:S(2)}, u32[]{:S(2)}) collective-permute-start(bf16[256,1024]{1,0:T(8,128)(2,1)S(1)} %pad_maximum_fusion.9.refs_7_.refs_2_), channel_id=1, source_target_pairs={{0,8},{8,0},{16,24},{24,16},{1,9},{9,1},{17,25},{25,17},{2,10},{10... | collective-permute-start | bytes 1572872 | tf_op jit(solution)/shard_map/ppermute | solution.py:481
  156.8 87.9 %reduce-scatter.4.cloned.1.call-start = ((), (), s32[]{:S(2)}) async-start(), calls=%async_computation.11 | async-start | bytes 4718592 | tf_op jit(solution)/shard_map/reduce_scatter | solution.py:1788
  157.8 12.4 %collective-permute-start.16 = (bf16[256,1024]{1,0:T(8,128)(2,1)S(1)}, bf16[256,1024]{1,0:T(8,128)(2,1)S(1)}, u32[]{:S(2)}, u32[]{:S(2)}) collective-permute-start(bf16[256,1024]{1,0:T(8,128)(2,1)S(1)} %copy-done.33), channel_id=1, source_target_pairs={{0,16},{8,24},{16,0},{24,8},{1,17},{9,25},{17,1},{25,9},{2,18},{10... | collective-permute-start | bytes 1572872 | tf_op jit(solution)/shard_map/ppermute | solution.py:481
  169.8 12.1 %collective-permute-start.19 = (bf16[128,1024]{1,0:T(8,128)(2,1)S(1)}, bf16[128,1024]{1,0:T(8,128)(2,1)S(1)}, u32[]{:S(2)}, u32[]{:S(2)}) collective-permute-start(bf16[128,1024]{1,0:T(8,128)(2,1)S(1)} %slice_add_fusion), channel_id=1, source_target_pairs={{0,16},{8,24},{16,0},{24,8},{1,17},{9,25},{17,1},{25,9},{2,18},{10... | collective-permute-start | bytes 786440 | tf_op jit(solution)/shard_map/ppermute | solution.py:481
  171.4 10.5 %collective-permute-start.17 = (bf16[128,1024]{1,0:T(8,128)(2,1)S(1)}, bf16[128,1024]{1,0:T(8,128)(2,1)S(1)}, u32[]{:S(2)}, u32[]{:S(2)}) collective-permute-start(bf16[128,1024]{1,0:T(8,128)(2,1)S(1)} %slice_add_fusion.1), channel_id=1, source_target_pairs={{0,8},{8,0},{16,24},{24,16},{1,9},{9,1},{17,25},{25,17},{2,10},{10... | collective-permute-start | bytes 786440 | tf_op jit(solution)/shard_map/ppermute | solution.py:481
  181.8 99.7 %reduce-scatter.8.cloned.1.call-start = ((), (), s32[]{:S(2)}) async-start(), calls=%async_computation.13 | async-start | bytes 2654208 | tf_op jit(solution)/shard_map/reduce_scatter | solution.py:1813
  188.2 11.8 %collective-permute-start.20 = (bf16[256,512]{1,0:T(8,128)(2,1)}, bf16[256,512]{1,0:T(8,128)(2,1)S(1)}, u32[]{:S(2)}, u32[]{:S(2)}) collective-permute-start(bf16[256,512]{1,0:T(8,128)(2,1)} %get-tuple-element.128), channel_id=1, source_target_pairs={{0,8},{8,0},{16,24},{24,16},{1,9},{9,1},{17,25},{25,17},{2,10},{10... | collective-permute-start | bytes 786440 | tf_op jit(solution)/shard_map/ppermute | solution.py:481
  188.9 12.3 %collective-permute-start.21 = (bf16[256,512]{1,0:T(8,128)(2,1)}, bf16[256,512]{1,0:T(8,128)(2,1)S(1)}, u32[]{:S(2)}, u32[]{:S(2)}) collective-permute-start(bf16[256,512]{1,0:T(8,128)(2,1)} %get-tuple-element.129), channel_id=1, source_target_pairs={{0,16},{8,24},{16,0},{24,8},{1,17},{9,25},{17,1},{25,9},{2,18},{10... | collective-permute-start | bytes 786440 | tf_op jit(solution)/shard_map/ppermute | solution.py:481
  190.6 13.2 %collective-permute-start.22 = (bf16[256,512]{1,0:T(8,128)(2,1)}, bf16[256,512]{1,0:T(8,128)(2,1)S(1)}, u32[]{:S(2)}, u32[]{:S(2)}) collective-permute-start(bf16[256,512]{1,0:T(8,128)(2,1)} %get-tuple-element.130), channel_id=1, source_target_pairs={{0,24},{8,16},{16,8},{24,0},{1,25},{9,17},{17,9},{25,1},{2,26},{10... | collective-permute-start | bytes 786440 | tf_op jit(solution)/shard_map/ppermute | solution.py:481
  197.7 30.4 %collective-permute-start.23 = (bf16[256,1024]{1,0:T(8,128)(2,1)}, bf16[256,1024]{1,0:T(8,128)(2,1)S(1)}, u32[]{:S(2)}, u32[]{:S(2)}) collective-permute-start(bf16[256,1024]{1,0:T(8,128)(2,1)} %get-tuple-element.144), channel_id=1, source_target_pairs={{0,8},{8,0},{16,24},{24,16},{1,9},{9,1},{17,25},{25,17},{2,10},{10... | collective-permute-start | bytes 1572872 | tf_op jit(solution)/shard_map/ppermute | solution.py:481
  198.4 29.7 %collective-permute-start.24 = (bf16[256,1024]{1,0:T(8,128)(2,1)}, bf16[256,1024]{1,0:T(8,128)(2,1)S(1)}, u32[]{:S(2)}, u32[]{:S(2)}) collective-permute-start(bf16[256,1024]{1,0:T(8,128)(2,1)} %get-tuple-element.145), channel_id=1, source_target_pairs={{0,16},{8,24},{16,0},{24,8},{1,17},{9,25},{17,1},{25,9},{2,18},{10... | collective-permute-start | bytes 1572872 | tf_op jit(solution)/shard_map/ppermute | solution.py:481
  200.1 28.0 %collective-permute-start.25 = (bf16[256,1024]{1,0:T(8,128)(2,1)}, bf16[256,1024]{1,0:T(8,128)(2,1)S(1)}, u32[]{:S(2)}, u32[]{:S(2)}) collective-permute-start(bf16[256,1024]{1,0:T(8,128)(2,1)} %get-tuple-element.146), channel_id=1, source_target_pairs={{0,24},{8,16},{16,8},{24,0},{1,25},{9,17},{17,9},{25,1},{2,26},{10... | collective-permute-start | bytes 1572872 | tf_op jit(solution)/shard_map/ppermute | solution.py:481
  229.0 11.2 %collective-permute-start.26 = (bf16[256,1024]{1,0:T(8,128)(2,1)}, bf16[256,1024]{1,0:T(8,128)(2,1)S(1)}, u32[]{:S(2)}, u32[]{:S(2)}) collective-permute-start(bf16[256,1024]{1,0:T(8,128)(2,1)} %get-tuple-element.147), channel_id=1, source_target_pairs={{0,16},{8,24},{16,0},{24,8},{1,17},{9,25},{17,1},{25,9},{2,18},{10... | collective-permute-start | bytes 1572872 | tf_op jit(solution)/shard_map/ppermute | solution.py:481
  229.0 11.6 %collective-permute-start.27 = (bf16[256,1024]{1,0:T(8,128)(2,1)}, bf16[256,1024]{1,0:T(8,128)(2,1)S(1)}, u32[]{:S(2)}, u32[]{:S(2)}) collective-permute-start(bf16[256,1024]{1,0:T(8,128)(2,1)} %get-tuple-element.148), channel_id=1, source_target_pairs={{0,8},{8,0},{16,24},{24,16},{1,9},{9,1},{17,25},{25,17},{2,10},{10... | collective-permute-start | bytes 1572872 | tf_op jit(solution)/shard_map/ppermute | solution.py:481
  256.1 11.1 %collective-permute-start.32 = (bf16[64,3072]{1,0:T(8,128)(2,1)S(1)}, bf16[64,3072]{1,0:T(8,128)(2,1)S(1)}, u32[]{:S(2)}, u32[]{:S(2)}) collective-permute-start(bf16[64,3072]{1,0:T(8,128)(2,1)S(1)} %get-tuple-element.184), channel_id=1, source_target_pairs={{0,16},{8,24},{16,0},{24,8},{1,17},{9,25},{17,1},{25,9},{2,18},{10... | collective-permute-start | bytes 1179656 | tf_op jit(solution)/shard_map/ppermute | solution.py:481
  263.3 18.2 %collective-permute-start.31 = (bf16[128,3072]{1,0:T(8,128)(2,1)S(1)}, bf16[128,3072]{1,0:T(8,128)(2,1)S(1)}, u32[]{:S(2)}, u32[]{:S(2)}) collective-permute-start(bf16[128,3072]{1,0:T(8,128)(2,1)S(1)} %pad_maximum_fusion.lower), channel_id=1, source_target_pairs={{0,16},{8,24},{16,0},{24,8},{1,17},{9,25},{17,1},{25,9},{2,18},{10... | collective-permute-start | bytes 2359304 | tf_op jit(solution)/shard_map/ppermute | solution.py:481
  267.2 14.3 %collective-permute-start.33 = (bf16[128,3072]{1,0:T(8,128)(2,1)S(1)}, bf16[128,3072]{1,0:T(8,128)(2,1)S(1)}, u32[]{:S(2)}, u32[]{:S(2)}) collective-permute-start(bf16[128,3072]{1,0:T(8,128)(2,1)S(1)} %pad_maximum_fusion.1.upper), channel_id=1, source_target_pairs={{0,8},{8,0},{16,24},{24,16},{1,9},{9,1},{17,25},{25,17},{2,10},{10... | collective-permute-start | bytes 2359304 | tf_op jit(solution)/shard_map/ppermute | solution.py:481
  267.3 35.1 %all-to-all-start.3 = ((bf16[8,64,1024]{2,1,0:T(8,128)(2,1)}), bf16[8,64,1024]{2,1,0:T(8,128)(2,1)}, u32[]{:S(2)}, u32[]{:S(2)}) async-start(bf16[8,64,1024]{2,1,0:T(8,128)(2,1)} %own_last.1), calls=%async_computation.5 | async-start | bytes 2097152 | tf_op jit(solution)/shard_map/all_to_all | solution.py:1819
  302.4 17.4 %all-to-all-start.4 = ((bf16[4,2,64,1024]{3,2,1,0:T(8,128)(2,1)}), bf16[4,2,64,1024]{3,2,1,0:T(8,128)(2,1)S(1)}, u32[]{:S(2)}, u32[]{:S(2)}) async-start(bf16[4,2,64,1024]{3,2,1,0:T(8,128)(2,1)} %bitcast.16), calls=%async_computation.7 | async-start | bytes 2097152 | tf_op jit(solution)/shard_map/all_to_all | solution.py:1825
  (61 other events, 583.0 us)
Sparse Core Ops, SparseCore 0:
  11.3 35.9 all-gather.3
  49.5 60.6 all-gather.5
  111.8 27.7 all-gather.7
  156.9 36.9 reduce-scatter.5
  196.0 48.6 reduce-scatter.3
  246.9 34.5 reduce-scatter.7

commit v5 on v4

--- a/solution.py
+++ b/solution.py
@@ -1800,8 +1800,7 @@
         parcels, (turned, attended, *kept), weights, first_weights, after(rank_row, outs[0])
     )
     outs = [outs[0]] + [swap(outs[q], q) for q in range(1, 4)]
-    ready = lax.optimization_barrier((back[1], back[3], *outs[1:]))
-    got = scatter_first((None, ready[0], None, ready[1]))
+    got = scatter_first((None, back[1], None, back[3]))
     bias_sums = jnp.sum(bias, 1)
     bias_parts = jnp.pad(jnp.concatenate(three_parts(bias_sums)), (0, 104))[None, :]
     slots = lax.broadcasted_iota(jnp.int32, (per, 1), 0) % shard == lax.axis_index("seq")

time: 330 us -> 329 us (level)
  starting transfers between devices: 64.1 us -> 70.1 us
  waiting for transfers between devices: 81.5 us -> 75.7 us
    ppermute x38, waiting for transfers between devices: 54.1 us -> 47 us  [swap(): return lax.ppermute(value, 'batch', [(i, i ^ bit) for i in range(4)])]
    ppermute x38, starting transfers between devices: 42.6 us -> 47.9 us  [swap(): return lax.ppermute(value, 'batch', [(i, i ^ bit) for i in range(4)])]
    all_to_all x1, waiting for transfers between devices: 4.02 us -> 0.44 us  [on_plane(): moved = lax.all_to_all(last, 'seq', 0, 0, tiled=True)]
  transfers between devices with their start and end apart: 48 -> 48, of which waited for: 27 -> 25; matrix products, arithmetic and copies ran while one was open for 5% -> 5% of each run, Pallas kernels for 33% -> 33%
where the time goes in v5:
time: 329 us; the launch traced here: 328 us
  Pallas kernels  124 us (38%)
  waiting for transfers between devices  75.7 us (23%)
  starting transfers between devices  70.1 us (21%)
  blocking collectives  20.7 us (6%)
  local copies, waits for them, and re-layouts  15.5 us (5%)
  between operations  14.8 us (4%)
  other arithmetic  7.26 us (2%)
    pallas_call x13, Pallas kernels, run(): pl.pallas_call(kernel, out_shape=out_shapes, in_specs=in_specs, out_specs...  115 us
    ppermute x38, starting transfers between devices, swap(): return lax.ppermute(value, 'batch', [(i, i ^ bit) for i in range(4)])  47.9 us
    ppermute x38, waiting for transfers between devices, swap(): return lax.ppermute(value, 'batch', [(i, i ^ bit) for i in range(4)])  47 us
    all_to_all x1, blocking collectives, on_plane(): packed = lax.all_to_all(packed, 'batch', 0, 0, tiled=True)  20.7 us
    all_to_all x2, starting transfers between devices, over_seq(): lax.all_to_all(pieces, 'seq', 0, 0, tiled=True)  9.71 us
    all_gather x1, waiting for transfers between devices, on_plane(): first_weights = lax.all_gather(first_shard, 'seq', axis=0, tiled=True)  8.76 us
    reduce_scatter x1, waiting for transfers between devices, on_plane(): lax.psum_scatter(first_weight_grads, 'seq', scatter_dimension=0, tiled=True)  8.7 us
    pallas_call x2, Pallas kernels, call(): pl.pallas_call(kernel, grid=(1,), out_shape=[jax.ShapeDtypeStruct(shape,...  8.63 us
  transfers between devices with their start and end apart: 48, of which 25 were waited for; matrix products, arithmetic and copies ran while one was open for 5% of the time, Pallas kernels for 33%

profile of v5, /device:TPU:0, one launch (start us, length us, event | category | flops | bytes accessed | tf_op | source)
XLA Modules:
  0.0 328.0 jit_solution(5046200100981969672)
XLA Ops:
  7.2 3.9 %pack.1 = (bf16[4,2,2,32,1152]{4,3,2,1,0:T(8,128)(2,1)}, bf16[128,1152]{1,0:T(8,128)(2,1)}, bf16[128,2048]{1,0:T(8,128)(2,1)}, bf16[128,1024]{1,0:T(8,128)(2,1)}) custom-call(s32[1]{0:T(128)} %bitcast.refs_0_.refs_8_.refs_2_.refs_5_.refs_3_.refs_14_.refs_13_.refs_9_.rank_ref, bf16[2,4,32,1024]{3,2,1,0:T(8,128)(2,1)} %bitcast.57, ...), custom_call_target="tpu_custom_call" | custom-call | flops 4600000000 | bytes 1048576 | tf_op jit(solution)/shard_map/pack/pallas_call | solution.py:768
  11.9 20.7 %all_to_all.25 = bf16[4,2,2,32,1152]{4,3,2,1,0:T(8,128)(2,1)S(1)} all-to-all(bf16[4,2,2,32,1152]{4,3,2,1,0:T(8,128)(2,1)} %get-tuple-element.93), channel_id=1, replica_groups=mesh['batch'=4,'seq'=8] {'batch'}, dimensions={0} | all-to-all | bytes 2359296 | tf_op jit(solution)/shard_map/all_to_all | solution.py:1739
  33.6 4.9 %all-to-all-start.1 = ((bf16[8,32,1152]{2,1,0:T(8,128)(2,1)}), bf16[8,32,1152]{2,1,0:T(8,128)(2,1)S(1)}, u32[]{:S(2)}, u32[]{:S(2)}) async-start(bf16[8,32,1152]{2,1,0:T(8,128)(2,1)} %bitcast.8), calls=%async_computation.1 | async-start | bytes 1179648 | tf_op jit(solution)/shard_map/all_to_all | solution.py:523
  38.5 8.8 %all-gather.4.cloned.1.call-done.refs_4_.refs_5_.refs_12_ = bf16[1024,1152]{1,0:T(8,128)(2,1)} async-done(((bf16[128,1152]{1,0:T(8,128)(2,1)}), bf16[1024,1152]{1,0:T(8,128)(2,1)}) %all-gather.4.cloned.1.call-update) | async-done | bytes 2359312 | tf_op jit(solution)/shard_map/all_gather | solution.py:1736
  53.5 3.5 %all-to-all-done.1 = bf16[8,32,1152]{2,1,0:T(8,128)(2,1)S(1)} async-done(((bf16[8,32,1152]{2,1,0:T(8,128)(2,1)}), bf16[8,32,1152]{2,1,0:T(8,128)(2,1)S(1)}, u32[]{:S(2)}, u32[]{:S(2)}) %all-to-all-start.1) | async-done | bytes 589856 | tf_op jit(solution)/shard_map/all_to_all | solution.py:523
  61.3 6.1 %collective-permute-done.2 = bf16[128,1152]{1,0:T(8,128)(2,1)S(1)} collective-permute-done((bf16[128,1152]{1,0:T(8,128)(2,1)S(1)}, bf16[128,1152]{1,0:T(8,128)(2,1)S(1)}, u32[]{:S(2)}, u32[]{:S(2)}) %collective-permute-start.2) | collective-permute-done | bytes 294944 | tf_op jit(solution)/shard_map/ppermute | solution.py:481
  71.5 4.8 %all-to-all-start.2 = ((bf16[8,32,1024]{2,1,0:T(8,128)(2,1)}), bf16[8,32,1024]{2,1,0:T(8,128)(2,1)S(1)}, u32[]{:S(2)}, u32[]{:S(2)}) async-start(bf16[8,32,1024]{2,1,0:T(8,128)(2,1)} %slice.135), calls=%async_computation.2 | async-start | bytes 1048576 | tf_op jit(solution)/shard_map/all_to_all | solution.py:523
  76.3 5.1 %collective-permute-done.3.refs_1_.refs_2_ = bf16[256,1152]{1,0:T(8,128)(2,1)S(1)} collective-permute-done((bf16[256,1152]{1,0:T(8,128)(2,1)S(1)}, bf16[256,1152]{1,0:T(8,128)(2,1)S(1)}, u32[]{:S(2)}, u32[]{:S(2)}) %collective-permute-start.3) | collective-permute-done | bytes 589856 | tf_op jit(solution)/shard_map/ppermute | solution.py:481
  84.7 16.4 %attend.1 = (f32[16,1024]{1,0:T(8,128)}, bf16[1024,1024]{1,0:T(8,128)(2,1)}, bf16[1024,768]{1,0:T(8,128)(2,1)}, f32[1024,256]{1,0:T(8,128)}, bf16[512,256]{1,0:T...) custom-call(bf16[256,1152]{1,0:T(8,128)(2,1)} %copy-done.11, ...), custom_call_target="tpu_custom_call" | custom-call | flops 17250000896 | bytes 1048576 | tf_op jit(solution)/shard_map/attend/pallas_call | solution.py:768
  103.8 4.6 %collective-permute-done.8.refs_7_ = bf16[512,256]{1,0:T(8,128)(2,1)S(1)} collective-permute-done((bf16[512,256]{1,0:T(8,128)(2,1)}, bf16[512,256]{1,0:T(8,128)(2,1)S(1)}, u32[]{:S(2)}, u32[]{:S(2)}) %collective-permute-start.8) | collective-permute-done | bytes 262176 | tf_op jit(solution)/shard_map/ppermute | solution.py:481
  112.8 8.8 %collective-permute-done.10.refs_9_ = bf16[512,512]{1,0:T(8,128)(2,1)S(1)} collective-permute-done((bf16[512,512]{1,0:T(8,128)(2,1)S(1)}, bf16[512,512]{1,0:T(8,128)(2,1)S(1)}, u32[]{:S(2)}, u32[]{:S(2)}) %collective-permute-start.10) | collective-permute-done | bytes 524320 | tf_op jit(solution)/shard_map/ppermute | solution.py:481
  125.4 8.6 %middle.1 = (bf16[1024,1024]{1,0:T(8,128)(2,1)}, f32[256,1024]{1,0:T(8,128)}, bf16[1024,1024]{1,0:T(8,128)(2,1)}) custom-call(s32[1]{0:T(128)} %bitcast.refs_0_.refs_8_.refs_2_.refs_5_.refs_3_.refs_14_.refs_13_.refs_9_.rank_ref, bf16[256,1152]{1,0:T(8,128)(2,1)} %copy-done.11, bf16[256,1152]{1,0:T(8,128)(2,1)} %copy-done.26, bf16[256,1152]{1,0:T(8,128)(2,1)} %copy-done.12, ...), custom_call_target="tpu_custom_call" | custom-call | flops 8049999872 | bytes 1048576 | tf_op jit(solution)/shard_map/middle/pallas_call | solution.py:768
  135.4 8.9 %feed.1 = (bf16[1024,2048]{1,0:T(8,128)(2,1)}, bf16[1024,1024]{1,0:T(8,128)(2,1)}) custom-call(bf16[1024,1024]{1,0:T(8,128)(2,1)} %get-tuple-element.105.refs_0_, bf16[1024,2048]{1,0:T(8,128)(2,1)} %all-gather.6.cloned.1.call-done.refs_1_.refs_3_, s32[1]{0:T(128)} %bitcast.refs_0_.refs_8_.refs_2_.refs_5_.refs_3_.refs_14_.refs_13_.refs_9_.rank_ref), custom_call_target="tpu_custom_call" | custom-call | flops 9200000000 | bytes 1048576 | tf_op jit(solution)/shard_map/feed/pallas_call | solution.py:768
  145.3 11.3 %feed_back.2 = (bf16[512,2048]{1,0:T(8,128)(2,1)}, bf16[256,1024]{1,0:T(8,128)(2,1)}, bf16[256,1024]{1,0:T(8,128)(2,1)}, bf16[1024,1024]{1,0:T(8,128)(2,1)}) custom-call(bf16[1024,2048]{1,0:T(8,128)(2,1)} %get-tuple-element.110.refs_0_, bf16[256,1024]{1,0:T(8,128)(2,1)} %copy-done.35, bf16[256,1024]{1,0:T(8,128)(2,1)} %copy-done.34, ...), custom_call_target="tpu_custom_call" | custom-call | flops 13799999488 | bytes 1048576 | tf_op jit(solution)/shard_map/feed_back/pallas_call | solution.py:768
  160.7 7.7 %feed_back.3 = (bf16[512,2048]{1,0:T(8,128)(2,1)}, bf16[256,1024]{1,0:T(8,128)(2,1)}, bf16[256,1024]{1,0:T(8,128)(2,1)}) custom-call(bf16[1024,2048]{1,0:T(8,128)(2,1)} %get-tuple-element.110.refs_0_, bf16[256,1024]{1,0:T(8,128)(2,1)} %copy-done.16, bf16[256,1024]{1,0:T(8,128)(2,1)} %copy-done.15, ...), custom_call_target="tpu_custom_call" | custom-call | flops 8049999872 | bytes 1048576 | tf_op jit(solution)/shard_map/feed_back/pallas_call | solution.py:768
  172.7 8.9 %gate_up_grads.1 = bf16[1024,2048]{1,0:T(8,128)(2,1)} custom-call(bf16[1024,1024]{1,0:T(8,128)(2,1)} %get-tuple-element.105.refs_0_, bf16[512,2048]{1,0:T(8,128)(2,1)} %get-tuple-element.121.refs_1_, bf16[512,2048]{1,0:T(8,128)(2,1)} %get-tuple-element.122.refs_2_, s32[1]{0:T(128)} %bitcast.refs_0_.refs_8_.refs_2_.refs_5_.refs_3_.refs_14_.refs_13_.refs_9_.rank_ref), custom_call_target="tpu_custom_call" | custom-call | flops 9200000000 | bytes 1048576 | tf_op jit(solution)/shard_map/gate_up_grads/pallas_call | solution.py:768
  182.5 5.6 %own_back.1 = (f32[256,1024]{1,0:T(8,128)}, bf16[256,512]{1,0:T(8,128)(2,1)}, bf16[256,512]{1,0:T(8,128)(2,1)}, bf16[256,512]{1,0:T(8,128)(2,1)}, bf16[256,512]{1,0:T(8,128)(2,1)}) custom-call(s32[1]{0:T(128)} %bitcast.refs_0_.refs_8_.refs_2_.refs_5_.refs_3_.refs_14_.refs_13_.refs_9_.rank_ref, bf16[256,1024]{1,0:T(8,128)(2,1)} %get-tuple-element.117.refs_1_, ...), custom_call_target="tpu_custom_call" | custom-call | flops 4600000000 | bytes 1048576 | tf_op jit(solution)/shard_map/own_back/pallas_call | solution.py:768
  191.7 5.9 %feed_out.1 = (bf16[256,1024]{1,0:T(8,128)(2,1)}, bf16[256,1024]{1,0:T(8,128)(2,1)}, bf16[256,1024]{1,0:T(8,128)(2,1)}, bf16[256,1024]{1,0:T(8,128)(2,1)}) custom-call(bf16[1024,1024]{1,0:T(8,128)(2,1)} %get-tuple-element.114.refs_5_.refs_0_, bf16[1024,1024]{1,0:T(8,128)(2,1)} %all-gather.8.cloned.1.call-done.refs_4_.refs_1_, ...), custom_call_target="tpu_custom_call" | custom-call | flops 5750000128 | bytes 1048576 | tf_op jit(solution)/shard_map/feed_out/pallas_call | solution.py:768
  204.3 21.9 %attend_back.1 = (bf16[1024,768]{1,0:T(8,128)(2,1)}, f32[8,128]{1,0:T(8,128)}, bf16[256,1024]{1,0:T(8,128)(2,1)}, bf16[256,1024]{1,0:T(8,128)(2,1)}, bf16[256,10...) custom-call(bf16[256,512]{1,0:T(8,128)(2,1)} %get-tuple-element.125.refs_0_.refs_4_, bf16[256,512]{1,0:T(8,128)(2,1)} %copy-done.36, ...), custom_call_target="tpu_custom_call" | custom-call | flops 92000002048 | bytes 1048576 | tf_op jit(solution)/shard_map/attend_back/pallas_call | solution.py:768
  228.2 8.4 %first_grads.1 = bf16[1024,1152]{1,0:T(8,128)(2,1)} custom-call(s32[1]{0:T(128)} %bitcast.refs_0_.refs_8_.refs_2_.refs_5_.refs_3_.refs_14_.refs_13_.refs_9_.rank_ref, bf16[1024,1024]{1,0:T(8,128)(2,1)} %get-tuple-element.142.refs_1_, bf16[1024,768]{1,0:T(8,128)(2,1)} %get-tuple-element.143.refs_2_, bf16[1024,1024]{1,0:T(8,128)(2,1)} %get-tuple-element.144.refs_3_, ...), custom_call_target="tpu_custom_call" | custom-call | flops 9200000000 | bytes 1048576 | tf_op jit(solution)/shard_map/first_grads/pallas_call | solution.py:768
  240.8 3.8 %reduce-scatter.4.cloned.1.call-done.refs_0_ = bf16[128,2048]{1,0:T(8,128)(2,1)} async-done(((bf16[1024,2048]{1,0:T(8,128)(2,1)}), bf16[128,2048]{1,0:T(8,128)(2,1)}) %reduce-scatter.4.cloned.1.call-update) | async-done | bytes 524304 | tf_op jit(solution)/shard_map/reduce_scatter | solution.py:1788
  247.8 5.6 %own_last.1 = bf16[8,64,1024]{2,1,0:T(8,128)(2,1)} custom-call(bf16[256,1024]{1,0:T(8,128)(2,1)} %get-tuple-element.139.refs_0_, bf16[256,1024]{1,0:T(8,128)(2,1)} %copy-done.22, bf16[128,1024]{1,0:T(8,128)(2,1)} %copy-done.40, bf16[256,1024]{1,0:T(8,128)(2,1)} %get-tuple-element.147.refs_3_, bf16[256,1024]{1,0:T(8,128)(2,1)} %copy-done.23, ...), custom_call_target="tpu_custom_call" | custom-call | flops 92000002048 | bytes 1048576 | tf_op jit(solution)/shard_map/own_last/pallas_call | solution.py:768
  256.1 5.8 %collective-permute-done.30 = bf16[64,3072]{1,0:T(8,128)(2,1)S(1)} collective-permute-done((bf16[64,3072]{1,0:T(8,128)(2,1)S(1)}, bf16[64,3072]{1,0:T(8,128)(2,1)S(1)}, u32[]{:S(2)}, u32[]{:S(2)}) %collective-permute-start.30) | collective-permute-done | bytes 393248 | tf_op jit(solution)/shard_map/ppermute | solution.py:481
  265.1 8.5 %all-to-all-start.3 = ((bf16[8,64,1024]{2,1,0:T(8,128)(2,1)}), bf16[8,64,1024]{2,1,0:T(8,128)(2,1)}, u32[]{:S(2)}, u32[]{:S(2)}) async-start(bf16[8,64,1024]{2,1,0:T(8,128)(2,1)} %own_last.1), calls=%async_computation.5 | async-start | bytes 2097152 | tf_op jit(solution)/shard_map/all_to_all | solution.py:1818
  273.6 8.7 %reduce-scatter.8.cloned.1.call-done = bf16[128,1152]{1,0:T(8,128)(2,1)} async-done(((bf16[1024,1152]{1,0:T(8,128)(2,1)}), bf16[128,1152]{1,0:T(8,128)(2,1)}) %reduce-scatter.8.cloned.1.call-update) | async-done | bytes 294928 | tf_op jit(solution)/shard_map/reduce_scatter | solution.py:1812
  284.9 3.3 %collective-permute-start.36 = (bf16[64,1152]{1,0:T(8,128)(2,1)S(1)}, bf16[64,1152]{1,0:T(8,128)(2,1)S(1)}, u32[]{:S(2)}, u32[]{:S(2)}) collective-permute-start(bf16[64,1152]{1,0:T(8,128)(2,1)S(1)} %get-tuple-element.188), channel_id=1, source_target_pairs={{0,16},{8,24},{16,0},{24,8},{1,17},{9,25},{17,1},{25,9},{2,18},{10... | collective-permute-start | bytes 442376 | tf_op jit(solution)/shard_map/ppermute | solution.py:481
  288.9 5.3 %collective-permute-start.35 = (bf16[128,1152]{1,0:T(8,128)(2,1)S(1)}, bf16[128,1152]{1,0:T(8,128)(2,1)S(1)}, u32[]{:S(2)}, u32[]{:S(2)}) collective-permute-start(bf16[128,1152]{1,0:T(8,128)(2,1)S(1)} %pad_maximum_fusion.10.lower), channel_id=1, source_target_pairs={{0,16},{8,24},{16,0},{24,8},{1,17},{9,25},{17,1},{25,9},{2,18},{10... | collective-permute-start | bytes 884744 | tf_op jit(solution)/shard_map/ppermute | solution.py:481
  295.1 3.8 %collective-permute-done.35.lower_far = bf16[128,1152]{1,0:T(8,128)(2,1)S(1)} collective-permute-done((bf16[128,1152]{1,0:T(8,128)(2,1)S(1)}, bf16[128,1152]{1,0:T(8,128)(2,1)S(1)}, u32[]{:S(2)}, u32[]{:S(2)}) %collective-permute-start.35) | collective-permute-done | bytes 294944 | tf_op jit(solution)/shard_map/ppermute | solution.py:481
  301.5 3.5 %all-to-all-start.4 = ((bf16[4,2,64,1024]{3,2,1,0:T(8,128)(2,1)}), bf16[4,2,64,1024]{3,2,1,0:T(8,128)(2,1)S(1)}, u32[]{:S(2)}, u32[]{:S(2)}) async-start(bf16[4,2,64,1024]{3,2,1,0:T(8,128)(2,1)} %bitcast.16), calls=%async_computation.7 | async-start | bytes 2097152 | tf_op jit(solution)/shard_map/all_to_all | solution.py:1824
  305.1 5.8 %spread_feed.1 = (f32[128,4096]{1,0:T(8,128)}, f32[128,4096]{1,0:T(8,128)}, f32[512,1024]{1,0:T(8,128)}, f32[8,128]{1,0:T(8,128)}) custom-call(s32[1]{0:T(128)} %bitcast.refs_0_.refs_8_.refs_2_.refs_5_.refs_3_.refs_14_.refs_13_.refs_9_.rank_ref, bf16[128,3072]{1,0:T(8,128)(2,1)} %copy-done.3, bf16[128,3072]{1,0:T(8,128)(2,1)} %copy-done.9, ...), custom_call_target="tpu_custom_call" | custom-call | flops 2097152 | bytes 16777216 | tf_op jit(solution)/shard_map/spread_feed/pallas_call | solution.py:580
  310.9 2.9 spread_first.1
  316.4 2.8 all-to-all-done.4
  (226 shorter events, 78.6 us)
Async XLA Ops:
  7.2 40.1 %all-gather.4.cloned.1.call-start = ((), (), s32[]{:S(2)}) async-start(), calls=%async_computation.8 | async-start | bytes 2654208 | tf_op jit(solution)/shard_map/all_gather | solution.py:1736
  11.2 124.2 %all-gather.6.cloned.1.call-start = ((), (), s32[]{:S(2)}) async-start(), calls=%async_computation.9 | async-start | bytes 4718592 | tf_op jit(solution)/shard_map/all_gather | solution.py:1737
  33.6 23.4 %all-to-all-start.1 = ((bf16[8,32,1152]{2,1,0:T(8,128)(2,1)}), bf16[8,32,1152]{2,1,0:T(8,128)(2,1)S(1)}, u32[]{:S(2)}, u32[]{:S(2)}) async-start(bf16[8,32,1152]{2,1,0:T(8,128)(2,1)} %bitcast.8), calls=%async_computation.1 | async-start | bytes 1179648 | tf_op jit(solution)/shard_map/all_to_all | solution.py:523
  38.5 105.9 %all-gather.8.cloned.1.call-start = ((), (), s32[]{:S(2)}) async-start(), calls=%async_computation.10 | async-start | bytes 2359296 | tf_op jit(solution)/shard_map/all_gather | solution.py:1738
  67.5 13.9 %collective-permute-start.3 = (bf16[256,1152]{1,0:T(8,128)(2,1)S(1)}, bf16[256,1152]{1,0:T(8,128)(2,1)S(1)}, u32[]{:S(2)}, u32[]{:S(2)}) collective-permute-start(bf16[256,1152]{1,0:T(8,128)(2,1)S(1)} %pad_maximum_fusion.2.refs_0_.refs_1_), channel_id=1, source_target_pairs={{0,16},{8,24},{16,0},{24,8},{1,17},{9,25},{17,1},{25,9},{2,18},{10... | collective-permute-start | bytes 1769480 | tf_op jit(solution)/shard_map/ppermute | solution.py:481
  68.7 13.7 %collective-permute-start.5 = (bf16[256,1152]{1,0:T(8,128)(2,1)S(1)}, bf16[256,1152]{1,0:T(8,128)(2,1)}, u32[]{:S(2)}, u32[]{:S(2)}) collective-permute-start(bf16[256,1152]{1,0:T(8,128)(2,1)S(1)} %pad_maximum_fusion.3.refs_2_.refs_3_), channel_id=1, source_target_pairs={{0,8},{8,0},{16,24},{24,16},{1,9},{9,1},{17,25},{25,17},{2,10},{10... | collective-permute-start | bytes 1769480 | tf_op jit(solution)/shard_map/ppermute | solution.py:481
  71.5 41.2 %all-to-all-start.2 = ((bf16[8,32,1024]{2,1,0:T(8,128)(2,1)}), bf16[8,32,1024]{2,1,0:T(8,128)(2,1)S(1)}, u32[]{:S(2)}, u32[]{:S(2)}) async-start(bf16[8,32,1024]{2,1,0:T(8,128)(2,1)} %slice.135), calls=%async_computation.2 | async-start | bytes 1048576 | tf_op jit(solution)/shard_map/all_to_all | solution.py:523
  76.3 164.5 %reduce-scatter.6.cloned.1.call-start = ((), (), s32[]{:S(2)}) async-start(), calls=%async_computation.12 | async-start | bytes 2359296 | tf_op jit(solution)/shard_map/reduce_scatter | solution.py:1783
  82.5 18.6 %collective-permute-start.7 = (bf16[1024,256]{1,0:T(8,128)(2,1)S(1)}, bf16[1024,256]{1,0:T(8,128)(2,1)S(1)}, u32[]{:S(2)}, u32[]{:S(2)}) collective-permute-start(bf16[1024,256]{1,0:T(8,128)(2,1)S(1)} %pad_maximum_fusion.5.refs_13_.refs_12_), channel_id=1, source_target_pairs={{0,8},{8,0},{16,24},{24,16},{1,9},{9,1},{17,25},{25,17},{2,10},{10... | collective-permute-start | bytes 1572872 | tf_op jit(solution)/shard_map/ppermute | solution.py:481
  83.6 17.5 %collective-permute-start.6 = (bf16[1024,256]{1,0:T(8,128)(2,1)S(1)}, bf16[1024,256]{1,0:T(8,128)(2,1)S(1)}, u32[]{:S(2)}, u32[]{:S(2)}) collective-permute-start(bf16[1024,256]{1,0:T(8,128)(2,1)S(1)} %pad_maximum_fusion.4.refs_11_.refs_10_), channel_id=1, source_target_pairs={{0,16},{8,24},{16,0},{24,8},{1,17},{9,25},{17,1},{25,9},{2,18},{10... | collective-permute-start | bytes 1572872 | tf_op jit(solution)/shard_map/ppermute | solution.py:481
  109.6 12.0 %collective-permute-start.10 = (bf16[512,512]{1,0:T(8,128)(2,1)S(1)}, bf16[512,512]{1,0:T(8,128)(2,1)S(1)}, u32[]{:S(2)}, u32[]{:S(2)}) collective-permute-start(bf16[512,512]{1,0:T(8,128)(2,1)S(1)} %pad_maximum_fusion.6), channel_id=1, source_target_pairs={{0,16},{8,24},{16,0},{24,8},{1,17},{9,25},{17,1},{25,9},{2,18},{10... | collective-permute-start | bytes 1572872 | tf_op jit(solution)/shard_map/ppermute | solution.py:481
  111.7 10.7 %collective-permute-start.11 = (bf16[512,512]{1,0:T(8,128)(2,1)S(1)}, bf16[512,512]{1,0:T(8,128)(2,1)S(1)}, u32[]{:S(2)}, u32[]{:S(2)}) collective-permute-start(bf16[512,512]{1,0:T(8,128)(2,1)S(1)} %pad_maximum_fusion.7), channel_id=1, source_target_pairs={{0,8},{8,0},{16,24},{24,16},{1,9},{9,1},{17,25},{25,17},{2,10},{10... | collective-permute-start | bytes 1572872 | tf_op jit(solution)/shard_map/ppermute | solution.py:481
  122.4 11.6 %collective-permute-start.13 = (bf16[128,1024]{1,0:T(8,128)(2,1)S(1)}, bf16[128,1024]{1,0:T(8,128)(2,1)S(1)}, u32[]{:S(2)}, u32[]{:S(2)}) collective-permute-start(bf16[128,1024]{1,0:T(8,128)(2,1)S(1)} %get-tuple-element.186), channel_id=1, source_target_pairs={{0,16},{8,24},{16,0},{24,8},{1,17},{9,25},{17,1},{25,9},{2,18},{10... | collective-permute-start | bytes 786440 | tf_op jit(solution)/shard_map/ppermute | solution.py:481
  134.1 10.3 %collective-permute-start.15 = (bf16[256,1024]{1,0:T(8,128)(2,1)S(1)}, bf16[256,1024]{1,0:T(8,128)(2,1)S(1)}, u32[]{:S(2)}, u32[]{:S(2)}) collective-permute-start(bf16[256,1024]{1,0:T(8,128)(2,1)S(1)} %pad_maximum_fusion.9.refs_7_.refs_2_), channel_id=1, source_target_pairs={{0,8},{8,0},{16,24},{24,16},{1,9},{9,1},{17,25},{25,17},{2,10},{10... | collective-permute-start | bytes 1572872 | tf_op jit(solution)/shard_map/ppermute | solution.py:481
  156.7 87.8 %reduce-scatter.4.cloned.1.call-start = ((), (), s32[]{:S(2)}) async-start(), calls=%async_computation.11 | async-start | bytes 4718592 | tf_op jit(solution)/shard_map/reduce_scatter | solution.py:1788
  157.7 12.4 %collective-permute-start.16 = (bf16[256,1024]{1,0:T(8,128)(2,1)S(1)}, bf16[256,1024]{1,0:T(8,128)(2,1)S(1)}, u32[]{:S(2)}, u32[]{:S(2)}) collective-permute-start(bf16[256,1024]{1,0:T(8,128)(2,1)S(1)} %copy-done.31), channel_id=1, source_target_pairs={{0,16},{8,24},{16,0},{24,8},{1,17},{9,25},{17,1},{25,9},{2,18},{10... | collective-permute-start | bytes 1572872 | tf_op jit(solution)/shard_map/ppermute | solution.py:481
  169.7 12.0 %collective-permute-start.19 = (bf16[128,1024]{1,0:T(8,128)(2,1)S(1)}, bf16[128,1024]{1,0:T(8,128)(2,1)S(1)}, u32[]{:S(2)}, u32[]{:S(2)}) collective-permute-start(bf16[128,1024]{1,0:T(8,128)(2,1)S(1)} %slice_add_fusion), channel_id=1, source_target_pairs={{0,16},{8,24},{16,0},{24,8},{1,17},{9,25},{17,1},{25,9},{2,18},{10... | collective-permute-start | bytes 786440 | tf_op jit(solution)/shard_map/ppermute | solution.py:481
  171.3 10.4 %collective-permute-start.17 = (bf16[128,1024]{1,0:T(8,128)(2,1)S(1)}, bf16[128,1024]{1,0:T(8,128)(2,1)S(1)}, u32[]{:S(2)}, u32[]{:S(2)}) collective-permute-start(bf16[128,1024]{1,0:T(8,128)(2,1)S(1)} %slice_add_fusion.1), channel_id=1, source_target_pairs={{0,8},{8,0},{16,24},{24,16},{1,9},{9,1},{17,25},{25,17},{2,10},{10... | collective-permute-start | bytes 786440 | tf_op jit(solution)/shard_map/ppermute | solution.py:481
  181.7 100.6 %reduce-scatter.8.cloned.1.call-start = ((), (), s32[]{:S(2)}) async-start(), calls=%async_computation.13 | async-start | bytes 2654208 | tf_op jit(solution)/shard_map/reduce_scatter | solution.py:1812
  188.1 11.9 %collective-permute-start.20 = (bf16[256,512]{1,0:T(8,128)(2,1)}, bf16[256,512]{1,0:T(8,128)(2,1)S(1)}, u32[]{:S(2)}, u32[]{:S(2)}) collective-permute-start(bf16[256,512]{1,0:T(8,128)(2,1)} %get-tuple-element.126), channel_id=1, source_target_pairs={{0,8},{8,0},{16,24},{24,16},{1,9},{9,1},{17,25},{25,17},{2,10},{10... | collective-permute-start | bytes 786440 | tf_op jit(solution)/shard_map/ppermute | solution.py:481
  188.9 12.3 %collective-permute-start.21 = (bf16[256,512]{1,0:T(8,128)(2,1)}, bf16[256,512]{1,0:T(8,128)(2,1)S(1)}, u32[]{:S(2)}, u32[]{:S(2)}) collective-permute-start(bf16[256,512]{1,0:T(8,128)(2,1)} %get-tuple-element.127), channel_id=1, source_target_pairs={{0,16},{8,24},{16,0},{24,8},{1,17},{9,25},{17,1},{25,9},{2,18},{10... | collective-permute-start | bytes 786440 | tf_op jit(solution)/shard_map/ppermute | solution.py:481
  190.5 13.1 %collective-permute-start.22 = (bf16[256,512]{1,0:T(8,128)(2,1)}, bf16[256,512]{1,0:T(8,128)(2,1)S(1)}, u32[]{:S(2)}, u32[]{:S(2)}) collective-permute-start(bf16[256,512]{1,0:T(8,128)(2,1)} %get-tuple-element.128), channel_id=1, source_target_pairs={{0,24},{8,16},{16,8},{24,0},{1,25},{9,17},{17,9},{25,1},{2,26},{10... | collective-permute-start | bytes 786440 | tf_op jit(solution)/shard_map/ppermute | solution.py:481
  197.6 49.0 %collective-permute-start.27 = (bf16[256,1024]{1,0:T(8,128)(2,1)}, bf16[256,1024]{1,0:T(8,128)(2,1)S(1)}, u32[]{:S(2)}, u32[]{:S(2)}) collective-permute-start(bf16[256,1024]{1,0:T(8,128)(2,1)} %get-tuple-element.149), channel_id=1, source_target_pairs={{0,8},{8,0},{16,24},{24,16},{1,9},{9,1},{17,25},{25,17},{2,10},{10... | collective-permute-start | bytes 1572872 | tf_op jit(solution)/shard_map/ppermute | solution.py:481
  198.4 48.3 %collective-permute-start.28 = (bf16[256,1024]{1,0:T(8,128)(2,1)}, bf16[256,1024]{1,0:T(8,128)(2,1)}, u32[]{:S(2)}, u32[]{:S(2)}) collective-permute-start(bf16[256,1024]{1,0:T(8,128)(2,1)} %get-tuple-element.150), channel_id=1, source_target_pairs={{0,16},{8,24},{16,0},{24,8},{1,17},{9,25},{17,1},{25,9},{2,18},{10... | collective-permute-start | bytes 1572872 | tf_op jit(solution)/shard_map/ppermute | solution.py:481
  200.0 46.6 %collective-permute-start.29 = (bf16[256,1024]{1,0:T(8,128)(2,1)}, bf16[256,1024]{1,0:T(8,128)(2,1)}, u32[]{:S(2)}, u32[]{:S(2)}) collective-permute-start(bf16[256,1024]{1,0:T(8,128)(2,1)} %get-tuple-element.151), channel_id=1, source_target_pairs={{0,24},{8,16},{16,8},{24,0},{1,25},{9,17},{17,9},{25,1},{2,26},{10... | collective-permute-start | bytes 1572872 | tf_op jit(solution)/shard_map/ppermute | solution.py:481
  226.2 12.3 %collective-permute-start.23 = (bf16[256,1024]{1,0:T(8,128)(2,1)}, bf16[256,1024]{1,0:T(8,128)(2,1)S(1)}, u32[]{:S(2)}, u32[]{:S(2)}) collective-permute-start(bf16[256,1024]{1,0:T(8,128)(2,1)} %get-tuple-element.140), channel_id=1, source_target_pairs={{0,16},{8,24},{16,0},{24,8},{1,17},{9,25},{17,1},{25,9},{2,18},{10... | collective-permute-start | bytes 1572872 | tf_op jit(solution)/shard_map/ppermute | solution.py:481
  226.3 12.3 %collective-permute-start.24 = (bf16[256,1024]{1,0:T(8,128)(2,1)}, bf16[256,1024]{1,0:T(8,128)(2,1)S(1)}, u32[]{:S(2)}, u32[]{:S(2)}) collective-permute-start(bf16[256,1024]{1,0:T(8,128)(2,1)} %get-tuple-element.141), channel_id=1, source_target_pairs={{0,8},{8,0},{16,24},{24,16},{1,9},{9,1},{17,25},{25,17},{2,10},{10... | collective-permute-start | bytes 1572872 | tf_op jit(solution)/shard_map/ppermute | solution.py:481
  254.6 10.2 %collective-permute-start.32 = (bf16[64,3072]{1,0:T(8,128)(2,1)S(1)}, bf16[64,3072]{1,0:T(8,128)(2,1)S(1)}, u32[]{:S(2)}, u32[]{:S(2)}) collective-permute-start(bf16[64,3072]{1,0:T(8,128)(2,1)S(1)} %get-tuple-element.180), channel_id=1, source_target_pairs={{0,16},{8,24},{16,0},{24,8},{1,17},{9,25},{17,1},{25,9},{2,18},{10... | collective-permute-start | bytes 1179656 | tf_op jit(solution)/shard_map/ppermute | solution.py:481
  262.0 20.3 %collective-permute-start.31 = (bf16[128,3072]{1,0:T(8,128)(2,1)S(1)}, bf16[128,3072]{1,0:T(8,128)(2,1)S(1)}, u32[]{:S(2)}, u32[]{:S(2)}) collective-permute-start(bf16[128,3072]{1,0:T(8,128)(2,1)S(1)} %pad_maximum_fusion.lower), channel_id=1, source_target_pairs={{0,16},{8,24},{16,0},{24,8},{1,17},{9,25},{17,1},{25,9},{2,18},{10... | collective-permute-start | bytes 2359304 | tf_op jit(solution)/shard_map/ppermute | solution.py:481
  264.9 17.3 %collective-permute-start.33 = (bf16[128,3072]{1,0:T(8,128)(2,1)S(1)}, bf16[128,3072]{1,0:T(8,128)(2,1)S(1)}, u32[]{:S(2)}, u32[]{:S(2)}) collective-permute-start(bf16[128,3072]{1,0:T(8,128)(2,1)S(1)} %pad_maximum_fusion.1.upper), channel_id=1, source_target_pairs={{0,8},{8,0},{16,24},{24,16},{1,9},{9,1},{17,25},{25,17},{2,10},{10... | collective-permute-start | bytes 2359304 | tf_op jit(solution)/shard_map/ppermute | solution.py:481
  265.1 36.4 %all-to-all-start.3 = ((bf16[8,64,1024]{2,1,0:T(8,128)(2,1)}), bf16[8,64,1024]{2,1,0:T(8,128)(2,1)}, u32[]{:S(2)}, u32[]{:S(2)}) async-start(bf16[8,64,1024]{2,1,0:T(8,128)(2,1)} %own_last.1), calls=%async_computation.5 | async-start | bytes 2097152 | tf_op jit(solution)/shard_map/all_to_all | solution.py:1818
  301.5 17.6 %all-to-all-start.4 = ((bf16[4,2,64,1024]{3,2,1,0:T(8,128)(2,1)}), bf16[4,2,64,1024]{3,2,1,0:T(8,128)(2,1)S(1)}, u32[]{:S(2)}, u32[]{:S(2)}) async-start(bf16[4,2,64,1024]{3,2,1,0:T(8,128)(2,1)} %bitcast.16), calls=%async_computation.7 | async-start | bytes 2097152 | tf_op jit(solution)/shard_map/all_to_all | solution.py:1824
  (59 other events, 575.2 us)
Sparse Core Ops, SparseCore 0:
  11.3 35.9 all-gather.3
  49.5 60.6 all-gather.5
  111.8 27.6 all-gather.7
  156.8 36.9 reduce-scatter.5
  195.9 48.5 reduce-scatter.3
  246.7 35.4 reduce-scatter.7
